TPU v7x, 512 devices: a whole 4x8x8 slice. The times are simulated.
512 devices in a mesh: tm: 64 (over z, y), band: 8 (over x, core).
Axes of the slice: x: 4, y: 8, z: 8, core: 2. Of those that a mesh axis runs over, the one named last changes fastest.
Arguments:
- audio_clips: float32 [8, 2, 112896], P(None, None, 'tm'), may hold values from -6 to 6
- band_widths: int32 [64], replicated, may hold values from 1 to 128, 1024 in all
- band_gain: float32 [64, 512], P('band'), may hold values from 0.25 to 1.75
- band_weight: bfloat16 [64, 512, 384], P('band', 'tm'), may hold values from -0.5 to 0.5
- norm_gain: float32 [384], replicated, may hold values from 0.25 to 1.75
- qkv_weight: bfloat16 [384, 1536], replicated
- out_weight: bfloat16 [512, 384], replicated, may hold values from -0.25 to 0.25
- cotangent: bfloat16 [64, 8, 256, 384], P('band', None, 'tm'), may hold values from -6 to 6
Outputs:
- attended: bfloat16 [64, 8, 256, 384], P('band', None, 'tm')
- grad_qkv: float32 [384, 1536], replicated
- grad_out: float32 [512, 384], replicated
Inputs may be any that keep to these rules, and one draw needn't show every extreme that they name: `band_widths`: the bands are consecutive and cover all 1024 bins; the widest has exactly 128 bins.
All inputs are finite; a program needn't handle non-finite values.
Results may differ from a plain program's by a relative error of at most 0.0095.
Values may be sent and summed in bfloat16 or wider, within the bound.
No kernel may reach another device: no remote copies, remote signals or barrier semaphores. Data moves between devices by JAX's collectives and lax.ppermute only.
A program may use at most 64 MiB of HBM per device.

v0:
```python
import math

import jax
import jax.numpy as jnp
from jax import lax
from jax.sharding import PartitionSpec as P

D = 384
HEADS = 8
HDIM = 64
WIN = 2048
HOP = 441
BANDS = 64
MAXW = 128
CLIPS = 8
INNER = 512
FEAT = 512


def shifted(value, axis, steps):
    count = lax.axis_size(axis)
    first, last = (max(0, -steps), min(count, count - steps))
    return lax.ppermute(value, axis, [(source, source + steps) for source in range(first, last)])


def dft_table(window_len, first_bin, bin_count):
    sample_at = lax.iota(jnp.int32, window_len)
    bin_at = first_bin + lax.iota(jnp.int32, bin_count)
    phase = sample_at[:, None] * bin_at[None, :] % window_len
    angle = phase.astype(jnp.float32) * (2.0 * math.pi / window_len)
    taper = 0.5 - 0.5 * jnp.cos(sample_at.astype(jnp.float32) * (2.0 * math.pi / window_len))
    column = (taper / math.sqrt(window_len))[:, None]
    return jnp.stack([jnp.cos(angle) * column, -jnp.sin(angle) * column], axis=1)


def cut_frames(samples, frame_total, hop_len, window_len):
    position = (
        lax.iota(jnp.int32, frame_total)[:, None] * hop_len
        + lax.iota(jnp.int32, window_len)[None, :]
    )
    return jnp.take(samples, position, axis=2)


def band_normed(raw, band_width, gain_row):
    keep_bins = (lax.iota(jnp.int32, MAXW) < band_width).astype(jnp.float32)
    masked = raw * keep_bins
    mean_sq = jnp.sum(masked * masked, axis=(1, 3, 4)) / (4 * band_width).astype(jnp.float32)
    inverse = lax.rsqrt(jnp.maximum(mean_sq, 0.25))
    scaled = masked * inverse[:, None, :, None, None]
    arranged = jnp.transpose(scaled, (0, 2, 4, 1, 3)).reshape(-1, FEAT)
    return (arranged * gain_row[None, :]).astype(jnp.bfloat16)


def rotary_tables(frame_total):
    position = lax.iota(jnp.int32, frame_total).astype(jnp.float32)
    freq = jnp.exp(
        lax.iota(jnp.int32, HDIM // 2).astype(jnp.float32) * (-2.0 * math.log(10000.0) / HDIM)
    )
    angle = position[:, None] * freq[None, :]
    return (jnp.cos(angle)[:, None, :], jnp.sin(angle)[:, None, :])


def rotate(values, cosine, sine_part, sign):
    first_half = values[..., : HDIM // 2]
    second_half = values[..., HDIM // 2 :]
    return jnp.concatenate(
        [
            first_half * cosine - sign * second_half * sine_part,
            second_half * cosine + sign * first_half * sine_part,
        ],
        axis=-1,
    )


def device_product(pattern, left, right):
    return jnp.einsum(pattern, left, right, preferred_element_type=jnp.float32)


def layer(x_seq, g_seq, norm_gain, qkv_weight, out_weight, product):
    frame_total = x_seq.shape[0]
    x_full = x_seq.astype(jnp.float32)
    normed_x = (
        x_full * lax.rsqrt(jnp.mean(x_full * x_full, axis=-1, keepdims=True) + 1e-06) * norm_gain
    ).astype(jnp.bfloat16)
    projected = product("fd,de->fe", normed_x, qkv_weight)
    query = projected[:, :INNER].reshape(frame_total, HEADS, HDIM)
    key_part = projected[:, INNER : 2 * INNER].reshape(frame_total, HEADS, HDIM)
    value_part = projected[:, 2 * INNER :].reshape(frame_total, HEADS, HDIM)
    cosine, sine_part = rotary_tables(frame_total)
    factor = 1.0 / math.sqrt(HDIM)
    query_b = (rotate(query, cosine, sine_part, 1.0) * factor).astype(jnp.bfloat16)
    key_b = rotate(key_part, cosine, sine_part, 1.0).astype(jnp.bfloat16)
    value_b = value_part.astype(jnp.bfloat16)
    grad_mixed = (
        product("fd,id->fi", g_seq, out_weight)
        .astype(jnp.bfloat16)
        .reshape(frame_total, HEADS, HDIM)
    )

    def head_pass(operands):
        head_q, head_k, head_v, head_g = operands
        scores = product("fd,gd->fg", head_q, head_k)
        peak = jnp.max(scores, axis=-1, keepdims=True)
        expo = jnp.exp(scores - peak)
        probs = expo / jnp.sum(expo, axis=-1, keepdims=True)
        probs_b = probs.astype(jnp.bfloat16)
        mixed = product("fg,gd->fd", probs_b, head_v)
        grad_p = product("fd,gd->fg", head_g, head_v)
        grad_v = product("fg,fd->gd", probs_b, head_g)
        row_dot = jnp.sum(probs * grad_p, axis=-1, keepdims=True)
        grad_s = (probs * (grad_p - row_dot)).astype(jnp.bfloat16)
        grad_q = product("fg,gd->fd", grad_s, head_k)
        grad_k = product("fg,fd->gd", grad_s, head_q)
        return (mixed, grad_q, grad_k, grad_v)

    def heads_first(values):
        return jnp.transpose(values, (1, 0, 2))

    mixed, grad_q, grad_k, grad_v = lax.map(
        head_pass,
        (heads_first(query_b), heads_first(key_b), heads_first(value_b), heads_first(grad_mixed)),
    )
    mixed_b = heads_first(mixed).reshape(frame_total, INNER).astype(jnp.bfloat16)
    attended = (x_full + product("fi,id->fd", mixed_b, out_weight)).astype(jnp.bfloat16)
    grad_out = product("fi,fd->id", mixed_b, g_seq)
    grad_query = rotate(heads_first(grad_q) * factor, cosine, sine_part, -1.0).reshape(
        frame_total, INNER
    )
    grad_key = rotate(heads_first(grad_k), cosine, sine_part, -1.0).reshape(frame_total, INNER)
    grad_value = heads_first(grad_v).reshape(frame_total, INNER)
    grad_proj = jnp.concatenate([grad_query, grad_key, grad_value], axis=-1).astype(jnp.bfloat16)
    grad_qkv = product("fd,fe->de", normed_x, grad_proj)
    return (attended, grad_qkv, grad_out)


def body(
    audio_clips, band_widths, band_gain, band_weight, norm_gain, qkv_weight, out_weight, cotangent
):
    own_bands = BANDS // lax.axis_size("band")
    frame_block = audio_clips.shape[2] // HOP
    rim = shifted(audio_clips[:, :, : WIN - HOP], "tm", -1)
    extended = jnp.concatenate([audio_clips, rim], axis=2)
    frames = cut_frames(extended, frame_block, HOP, WIN)
    band_place = lax.axis_index("band")
    starts = jnp.cumsum(band_widths, dtype=jnp.int32) - band_widths
    first_band = band_place * own_bands
    widths_own = lax.dynamic_slice_in_dim(band_widths, first_band, own_bands)
    starts_own = lax.dynamic_slice_in_dim(starts, first_band, own_bands)

    def one_band(inputs_now):
        band_width, row_start, gain_row = inputs_now
        raw = jnp.einsum(
            "cafn,nrk->cafrk",
            frames,
            dft_table(WIN, row_start, MAXW),
            precision=lax.Precision.HIGHEST,
        )
        return band_normed(raw, band_width, gain_row)

    normed = lax.map(one_band, (widths_own, starts_own, band_gain))
    tokens = jnp.einsum(
        "btf,bfd->btd",
        normed,
        lax.all_gather(band_weight, "tm", axis=1, tiled=True),
        preferred_element_type=jnp.float32,
    ).astype(jnp.bfloat16)
    local_tokens = tokens.reshape(own_bands * CLIPS, frame_block, D)
    local_grads = cotangent.reshape(own_bands * CLIPS, frame_block, D)
    sequences, cotangents = (
        lax.all_to_all(local_tokens, "tm", split_axis=0, concat_axis=1, tiled=True),
        lax.all_to_all(local_grads, "tm", split_axis=0, concat_axis=1, tiled=True),
    )

    def advance(totals, seq_pair):
        attended, grad_qkv, grad_out = layer(
            seq_pair[0], seq_pair[1], norm_gain, qkv_weight, out_weight, device_product
        )
        return ((totals[0] + grad_qkv, totals[1] + grad_out), attended)

    start_totals = (jnp.zeros((D, 3 * INNER), jnp.float32), jnp.zeros((INNER, D), jnp.float32))
    totals, attended = lax.scan(advance, start_totals, (sequences, cotangents))
    returned = lax.all_to_all(attended, "tm", split_axis=1, concat_axis=0, tiled=True)
    attended_out = returned.reshape(own_bands, CLIPS, frame_block, D)
    factor_all = 1.0 / math.sqrt(BANDS * CLIPS * frame_block * lax.axis_size("tm"))
    local_q = totals[0] * factor_all
    local_o = totals[1] * factor_all
    grad_qkv, grad_out = lax.psum((local_q, local_o), ("tm", "band"))
    return (attended_out, grad_qkv, grad_out)


def solution(mesh):
    return jax.shard_map(
        body,
        mesh=mesh,
        in_specs=(
            P(None, None, "tm"),
            P(),
            P("band", None),
            P("band", "tm", None),
            P(),
            P(),
            P(),
            P("band", None, "tm", None),
        ),
        out_specs=(P("band", None, "tm", None), P(), P()),
        check_vma=False,
    )
```

profile of v0, /device:TPU:1, one launch (start us, length us, event | category | flops | bytes accessed | tf_op | source)
XLA Modules:
  0.0 595.3 jit_solution(10036554316416144996)
XLA Ops:
  7.2 1.0 slice.48
  8.2 1.3 collective-permute-start
  9.6 18.3 %all-to-all-start.1 = ((bf16[64,4,384]{2,1,0:T(4,128)(2,1)}), bf16[64,4,384]{2,1,0:T(4,128)(2,1)}, u32[]{:S(2)}, u32[]{:S(2)}) async-start(bf16[64,4,384]{2,1,0:T(4,128)(2,1)} %bitcast.178), calls=%async_computation.1 | async-start | bytes 393216 | tf_op jit(solution)/shard_map/all_to_all | solution.py:171
  27.9 2.7 copy.72
  31.3 2.2 copy.73
  33.5 9.0 %pad_maximum_fusion = f32[8,2,3371]{0,1,2:T(2,128)} fusion(f32[8,2,1607]{0,1,2:T(2,128)} %copy.73, f32[8,2,1764]{0,1,2:T(2,128)S(1)} %copy.72), kind=kLoop, calls=%fused_computation.67 | loop fusion | flops 53936 | bytes 431488 | tf_op jit(solution)/shard_map/concatenate | solution.py:142
  42.5 58.1 %gather_fusion = f32[8192,8,2]{1,2,0:T(2,128)} fusion(f32[8,2,3371]{0,1,2:T(2,128)} %pad_maximum_fusion, s32[8192]{0:T(1024)S(1)} %broadcast_clamp_fusion), kind=kCustom, calls=%fused_computation | custom fusion | bytes 1081344 | tf_op jit(solution)/shard_map/jit(_take)/gather | solution.py:41
  100.6 10.2 %copy.88 = f32[4,2048,8,2]{1,0,2,3:T(4,128)S(1)} copy(f32[4,2048,8,2]{2,3,1,0:T(2,128)} %bitcast.165) | data formatting | bytes 1048576 | tf_op jit(solution)/shard_map/jit(_take)/gather | solution.py:41
  111.0 1.1 copy.75
  112.1 111.5 %while.40 = (s32[]{:T(128)}, bf16[8,32,512]{1,2,0:T(8,128)(2,1)}, s32[8]{0:T(128)S(1)}, f32[8,2,4,2048]{3,0,2,1:T(8,128)}, s32[8]{0:T(128)S(1)}, /*index=5*/f32[8,512]{1,0:T(8,128)}, s32[]{:T(128)}, s32[]{:T(128)}) while((s32[]{:T(128)}, bf16[8,32,512]{1,2,0:T(8,128)(2,1)}, s32[8]{0:T(128)S(1)}, f32[8,2,4,2048]{3,0,2,1:T(8,128)}, ...), condition=%wide.region_3.4_spmd, body=%wide.region_1.3_spmd.sunk | while | flops 407742880 | bytes 5399697 | solution.py:160
  113.4 4.2 cosine_multiply_fusion.2
  118.8 2.5 multiply_reduce_fusion.5
  122.1 1.9 copy.99
  127.3 4.2 cosine_multiply_fusion.2
  132.8 2.5 multiply_reduce_fusion.5
  136.0 1.9 copy.99
  141.3 4.2 cosine_multiply_fusion.2
  146.7 2.5 multiply_reduce_fusion.5
  149.9 1.9 copy.99
  155.2 4.2 cosine_multiply_fusion.2
  160.7 2.5 multiply_reduce_fusion.5
  163.9 1.9 copy.99
  169.1 4.2 cosine_multiply_fusion.2
  174.6 2.5 multiply_reduce_fusion.5
  177.8 1.9 copy.99
  183.1 4.2 cosine_multiply_fusion.2
  188.5 2.5 multiply_reduce_fusion.5
  191.8 1.9 copy.99
  197.0 4.2 cosine_multiply_fusion.2
  202.5 2.5 multiply_reduce_fusion.5
  205.7 1.9 copy.99
  211.0 4.2 cosine_multiply_fusion.2
  216.4 2.5 multiply_reduce_fusion.5
  219.7 1.9 copy.99
  223.6 2.8 convolution_convert_fusion.1
  227.2 12.3 %all-to-all-start = ((bf16[64,4,384]{2,1,0:T(4,128)(2,1)}), bf16[64,4,384]{2,1,0:T(4,128)(2,1)S(1)}, u32[]{:S(2)}, u32[]{:S(2)}) async-start(bf16[64,4,384]{2,1,0:T(4,128)(2,1)} %reshape.443), calls=%async_computation | async-start | bytes 393216 | tf_op jit(solution)/shard_map/all_to_all | solution.py:170
  239.7 1.0 squeeze.35
  241.9 9.6 %all-to-all-done = bf16[64,4,384]{2,1,0:T(4,128)(2,1)S(1)} async-done(((bf16[64,4,384]{2,1,0:T(4,128)(2,1)}), bf16[64,4,384]{2,1,0:T(4,128)(2,1)S(1)}, u32[]{:S(2)}, u32[]{:S(2)}) %all-to-all-start) | async-done | bytes 196640 | tf_op jit(solution)/shard_map/all_to_all | solution.py:170
  253.7 1.8 copy.79
  255.8 44.2 %while.41 = (s32[]{:T(128)}, bf16[8,256,64]{1,2,0:T(8,128)(2,1)S(1)}, f32[8,256,64]{1,2,0:T(8,128)}, f32[8,256,64]{1,2,0:T(8,128)}, bf16[8,256,64]{1,2,0:T(8,128...) while((s32[]{:T(128)}, ...), condition=%wide.region_9.10_spmd, body=%wide.region_5.9_spmd.sunk | while | flops 51510528 | bytes 3034213 | solution.py:119
  256.1 1.0 multiply_reduce_fusion.6
  258.9 1.6 fusion.104
  261.7 1.0 multiply_reduce_fusion.6
  264.4 1.6 fusion.104
  267.2 1.0 multiply_reduce_fusion.6
  269.9 1.6 fusion.104
  272.7 1.0 multiply_reduce_fusion.6
  275.4 1.6 fusion.104
  278.2 1.0 multiply_reduce_fusion.6
  281.0 1.6 fusion.104
  283.8 1.0 multiply_reduce_fusion.6
  286.5 1.6 fusion.104
  289.3 1.0 multiply_reduce_fusion.6
  292.0 1.6 fusion.104
  294.8 1.0 multiply_reduce_fusion.6
  297.5 1.6 fusion.104
  300.0 1.1 multiply_bitcast_fusion.1
  301.2 1.2 convolution_multiply_fusion.1
  302.6 2.0 convolution_multiply_fusion
  306.7 1.8 reduce.8
  308.7 16.3 %all_to_all.12 = bf16[64,2,768]{2,1,0:T(2,128)(2,1)S(1)} all-to-all(bf16[64,2,768]{2,1,0:T(2,128)(2,1)S(1)} %reshape.466), channel_id=1, replica_groups=mesh['tm'=64,'band'=8] {'tm'}, dimensions={0} | all-to-all | bytes 393216 | tf_op jit(solution)/shard_map/all_to_all | solution.py:182
  325.1 1.1 bitcast_reduce_fusion
  327.0 257.3 %all-reduce.3.cloned.1.call-done = (f32[384,1536]{1,0:T(8,128)}, f32[512,384]{1,0:T(8,128)}) async-done(((f32[384,1536]{1,0:T(8,128)}, f32[512,384]{1,0:T(8,128)}), (f32[384,1536]{1,0:T(8,128)}, f32[512,384]{1,0:T(8,128)})) %all-reduce.3.cloned.1.call-update) | async-done | bytes 3145744 | tf_op jit(solution)/shard_map/psum | solution.py:187
  584.3 3.3 copy.130
  (198 shorter events, 70.4 us)
Async XLA Ops:
  7.2 244.7 %copy-start = (bf16[384,1536]{1,0:T(8,128)(2,1)S(1)}, bf16[384,1536]{1,0:T(8,128)(2,1)}, u32[]{:S(2)}) copy-start(bf16[384,1536]{1,0:T(8,128)(2,1)} %param.17) | copy-start | bytes 3538948
  7.2 23.6 %copy-start.8 = (s32[64]{0:T(128)S(1)}, s32[64]{0:T(128)}, u32[]{:S(2)}) copy-start(s32[64]{0:T(128)} %param.13) | copy-start | bytes 772
  7.2 216.4 %all-gather.2.cloned.1.call-start = ((), (), s32[]{:S(2)}) async-start(), calls=%async_computation.3 | async-start | bytes 3194880 | tf_op jit(solution)/shard_map/all_gather | solution.py:164
  8.2 23.1 %collective-permute-start = (f32[8,2,1607]{2,0,1:T(8,128)S(1)}, f32[8,2,1607]{2,0,1:T(8,128)S(1)}, u32[]{:S(2)}, u32[]{:S(2)}) collective-permute-start(f32[8,2,1607]{2,0,1:T(8,128)S(1)} %copy.94), channel_id=1, source_target_pairs={{8,0},{16,8},{24,16},{32,24},{40,32},{48,40},{56,48},{64,56},{72,6... | collective-permute-start | bytes 308552 | tf_op jit(solution)/shard_map/ppermute | solution.py:23
  9.6 217.6 %all-to-all-start.1 = ((bf16[64,4,384]{2,1,0:T(4,128)(2,1)}), bf16[64,4,384]{2,1,0:T(4,128)(2,1)}, u32[]{:S(2)}, u32[]{:S(2)}) async-start(bf16[64,4,384]{2,1,0:T(4,128)(2,1)} %bitcast.178), calls=%async_computation.1 | async-start | bytes 393216 | tf_op jit(solution)/shard_map/all_to_all | solution.py:171
  223.6 17.1 %copy-start.1 = (bf16[512,384]{1,0:T(8,128)(2,1)S(1)}, bf16[512,384]{1,0:T(8,128)(2,1)}, u32[]{:S(2)}) copy-start(bf16[512,384]{1,0:T(8,128)(2,1)} %param.18) | copy-start | bytes 1179652
  226.5 25.4 %copy-start.7 = (f32[384]{0:T(512)S(1)}, f32[384]{0:T(512)}, u32[]{:S(2)}) copy-start(f32[384]{0:T(512)} %param.16) | copy-start | bytes 4612
  227.2 24.3 %all-to-all-start = ((bf16[64,4,384]{2,1,0:T(4,128)(2,1)}), bf16[64,4,384]{2,1,0:T(4,128)(2,1)S(1)}, u32[]{:S(2)}, u32[]{:S(2)}) async-start(bf16[64,4,384]{2,1,0:T(4,128)(2,1)} %reshape.443), calls=%async_computation | async-start | bytes 393216 | tf_op jit(solution)/shard_map/all_to_all | solution.py:170
  239.5 344.8 %all-reduce.3.cloned.1.call-start = ((), (), s32[]{:S(2)}) async-start(), calls=%async_computation.4 | async-start | bytes 6291456 | tf_op jit(solution)/shard_map/psum | solution.py:187
  253.7 2.1 copy-start.3
  300.0 2.3 copy-start.5
  301.2 1.4 copy-start.6
  304.6 1.0 copy-start.2
  584.3 3.3 copy-start.4
Sparse Core Ops, SparseCore 0:
  11.0 88.2 all-gather.1
  304.7 279.5 all-reduce.2
where the time goes:
time: 599 us; the launch traced here: 595 us
  waiting for transfers between devices  267 us (45%)
  local copies, waits for them, and re-layouts  124 us (21%)
  matrix products  70 us (12%)
  other arithmetic  65.9 us (11%)
  starting transfers between devices  31.9 us (5%)
  blocking collectives  16.3 us (3%)
  between operations  14.4 us (2%)
    psum x1, waiting for transfers between devices, body(): grad_qkv, grad_out = lax.psum((local_q, local_o), ('tm', 'band'))  257 us
    gather x2, local copies, waits for them, and re-layouts, cut_frames(): return jnp.take(samples, position, axis=2)  68.3 us
    dot_general x53, matrix products, device_product(): return jnp.einsum(pattern, left, right, preferred_element_type=jnp.float32)  47.4 us
    mul x8, other arithmetic, dft_table(): jnp.cos(angle) * column  33.7 us
    dot_general x8, matrix products, one_band(): jnp.einsum('cafn,nrk->cafrk', frames, dft_table(WIN, row_start, MAXW), pr...  19.8 us
    all_to_all x1, starting transfers between devices, body(): lax.all_to_all(local_grads, 'tm', split_axis=0, concat_axis=1, tiled=True)  18.3 us
    all_to_all x1, blocking collectives, body(): lax.all_to_all(attended, 'tm', split_axis=1, concat_axis=0, tiled=True)  16.3 us
    dynamic_slice x24, local copies, waits for them, and re-layouts, body(): normed = lax.map(one_band, (widths_own, starts_own, band_gain))  15.2 us
  transfers between devices with their start and end apart: 5, of which 2 were waited for; matrix products, arithmetic and copies ran while one was open for 34% of the time, Pallas kernels for 0%

commit v1 on v0

v1 whole, which is shorter than its diff:
```python
import math

import jax
import jax.numpy as jnp
import numpy as np
from jax import lax
from jax.experimental import pallas as pl
from jax.experimental.pallas import tpu as pltpu
from jax.sharding import Mesh, PartitionSpec as P

D = 384
HEADS = 8
HDIM = 64
WIN = 2048
HOP = 441
BANDS = 64
MAXW = 128
CLIPS = 8
INNER = 512
BINS = 1024
FEAT = 512
FRAMES = 256

OUTER = 8
SPAN = WIN // OUTER
HIGH = BINS // OUTER


def window_table():
    sample_at = np.arange(WIN, dtype=np.float64)
    taper = (0.5 - 0.5 * np.cos(sample_at * (2.0 * np.pi / WIN))) / np.sqrt(WIN)
    return taper.reshape(1, WIN).astype(np.float32)


def twiddle_table():
    phase = np.outer(np.arange(OUTER), np.arange(SPAN)) % WIN
    angle = phase * (2.0 * np.pi / WIN)
    return np.concatenate([np.cos(angle), np.sin(angle)], axis=0).astype(np.float32)


def inner_table():
    phase = np.outer(np.arange(SPAN), np.arange(HIGH)) % SPAN
    angle = phase * (2.0 * np.pi / SPAN)
    real, imag = np.cos(angle), np.sin(angle)
    return np.concatenate(
        [np.concatenate([real, -imag], axis=1), np.concatenate([imag, real], axis=1)], axis=0
    ).astype(np.float32)


def rotary_table(frame_order):
    freq = np.exp(np.arange(HDIM // 2, dtype=np.float32) * np.float32(-2.0 * math.log(10000.0) / HDIM))
    angle = (frame_order.astype(np.float32)[:, None] * freq.astype(np.float32)[None, :]).astype(np.float64)
    cosine, sine = np.cos(angle), np.sin(angle)
    return (
        np.concatenate([cosine] * 4, axis=1).astype(np.float32),
        np.concatenate([-sine, sine, -sine, sine], axis=1).astype(np.float32),
    )


def spectrum_kernel(
    frames_here,
    widths_ref,
    starts_ref,
    audio_ref,
    rim_ref,
    gain_ref,
    place_ref,
    taper_ref,
    twiddle_ref,
    inner_ref,
    out_ref,
    lead,
    tail,
    framed,
    stage,
    bins,
    pick,
):
    own = audio_ref.shape[1]
    rows = audio_ref.shape[0]
    total = rows * frames_here
    lead[:, :own] = audio_ref[...]
    tail[:, : WIN - HOP] = rim_ref[...]
    lane = lax.broadcasted_iota(jnp.int32, (rows, WIN), 1)
    for f in range(frames_here):
        here = own - HOP * f
        head = lead[...] if f == 0 else pltpu.roll(lead[...], WIN - HOP * f, 1)
        rest = pltpu.roll(tail[...], here % WIN, 1)
        frame = jnp.where(lane < here, head, rest) * taper_ref[...]
        for block in range(WIN // 128):
            framed[block, pl.ds(f, rows, stride=frames_here), :] = frame[
                :, block * 128 : (block + 1) * 128
            ]
    root = math.sqrt(0.5)
    for half in range(SPAN // 128):
        x = [framed[2 * n + half] for n in range(OUTER)]
        e0, e1, e2, e3 = x[0] + x[4], x[1] + x[5], x[2] + x[6], x[3] + x[7]
        d0, d1, d2, d3 = x[0] - x[4], x[1] - x[5], x[2] - x[6], x[3] - x[7]
        s02, s13 = e0 + e2, e1 + e3
        p = (d1 - d3) * root
        q = (d1 + d3) * root
        real = [s02 + s13, d0 + p, e0 - e2, d0 - p, s02 - s13]
        imag = [None, -(q + d2), e3 - e1, d2 - q, None]
        lanes = slice(half * 128, (half + 1) * 128)
        for low in range(OUTER):
            if low <= 4:
                re, im = real[low], imag[low]
            else:
                re, im = real[8 - low], -imag[8 - low]
            at = slice(low * total, (low + 1) * total)
            if low == 0:
                stage[at, half * 128 : (half + 1) * 128] = re
                stage[at, SPAN + half * 128 : SPAN + (half + 1) * 128] = jnp.zeros_like(re)
                continue
            c = twiddle_ref[low : low + 1, lanes]
            s = twiddle_ref[OUTER + low : OUTER + low + 1, lanes]
            if im is None:
                zr, zi = re * c, -(re * s)
            else:
                zr, zi = re * c + im * s, im * c - re * s
            stage[at, half * 128 : (half + 1) * 128] = zr
            stage[at, SPAN + half * 128 : SPAN + (half + 1) * 128] = zi
    made = jnp.dot(
        stage[...],
        inner_ref[...],
        preferred_element_type=jnp.float32,
        precision=lax.Precision.HIGHEST,
    )
    for low in range(OUTER):
        for part in range(2):
            piece = made[low * total : (low + 1) * total, part * HIGH : (part + 1) * HIGH]
            cols = slice(low * HIGH, (low + 1) * HIGH)
            for split in range(3):
                at = (split * 2 + part) * total
                kept = piece.astype(jnp.bfloat16)
                bins[at : at + total, cols] = kept
                piece = piece - kept.astype(jnp.float32)
    target = place_ref[...]
    for low in range(OUTER):
        bin_at = low + OUTER * lax.broadcasted_iota(jnp.int32, (HIGH, target.shape[1]), 0)
        pick[low * HIGH : (low + 1) * HIGH, :] = jnp.where(bin_at == target, 1.0, 0.0).astype(
            jnp.bfloat16
        )
    own_bands = target.shape[1] // MAXW
    half_rows = total // 2
    chosen = jnp.dot(bins[...], pick[...], preferred_element_type=jnp.float32)
    exact = chosen[: 2 * total] + chosen[2 * total : 4 * total] + chosen[4 * total :]
    for band in range(own_bands):
        cols = slice(band * MAXW, (band + 1) * MAXW)
        re = exact[:total, cols]
        im = exact[total:, cols]
        power = jnp.sum(re * re + im * im, axis=1, keepdims=True)
        power = power[:half_rows] + power[half_rows:]
        count = (4 * widths_ref[0, band]).astype(jnp.float32)
        inverse = lax.rsqrt(jnp.maximum(power / count, 0.25))
        for a in range(2):
            for r in range(2):
                value = (re, im)[r][a * half_rows : (a + 1) * half_rows]
                which = 2 * a + r
                out_ref[
                    band * half_rows : (band + 1) * half_rows,
                    which * MAXW : (which + 1) * MAXW,
                ] = (value * inverse * gain_ref[band, which : which + 1, :]).astype(jnp.bfloat16)


def swap_halves(values):
    width = values.shape[1]
    lane = lax.broadcasted_iota(jnp.int32, values.shape, 1)
    forward = pltpu.roll(values, width - HDIM // 2, 1)
    backward = pltpu.roll(values, HDIM // 2, 1)
    return jnp.where(lane % HDIM < HDIM // 2, forward, backward)


def dot(left, right, dims=((1,), (0,))):
    return lax.dot_general(left, right, (dims, ((), ())), preferred_element_type=jnp.float32)


def layer_kernel(
    feats_ref,
    weight_ref,
    grads_ref,
    gain_ref,
    qkv_ref,
    outw_ref,
    cos_ref,
    sin_ref,
    attended_ref,
    grad_qkv_ref,
    grad_out_ref,
    query_s,
    key_s,
    mixed_s,
    gproj_s,
    *,
    factor_all,
):
    natural = lax.broadcasted_iota(jnp.int32, (FEAT, FEAT), 1)
    wanted = lax.broadcasted_iota(jnp.int32, (FEAT, FEAT), 0)
    wanted = (wanted % MAXW) * 4 + wanted // MAXW
    order = jnp.where(natural == wanted, 1.0, 0.0).astype(jnp.bfloat16)
    weight = dot(order, weight_ref[...]).astype(jnp.bfloat16)
    x = dot(feats_ref[...], weight).astype(jnp.bfloat16).astype(jnp.float32)
    scale = lax.rsqrt(jnp.mean(x * x, axis=1, keepdims=True) + 1e-06)
    normed_x = (x * scale * gain_ref[...]).astype(jnp.bfloat16)
    factor = 1.0 / math.sqrt(HDIM)
    cosine = cos_ref[...]
    sine = sin_ref[...]
    qk = dot(normed_x, qkv_ref[:, : 2 * INNER])
    for block in range(INNER // 128):
        cols = slice(block * 128, (block + 1) * 128)
        q = qk[:, cols]
        k = qk[:, INNER + block * 128 : INNER + (block + 1) * 128]
        query_s[:, cols] = ((q * cosine + swap_halves(q) * sine) * factor).astype(jnp.bfloat16)
        key_s[:, cols] = (k * cosine + swap_halves(k) * sine).astype(jnp.bfloat16)
    value_b = dot(normed_x, qkv_ref[:, 2 * INNER :]).astype(jnp.bfloat16)
    grad_mixed = dot(grads_ref[...], outw_ref[...], ((1,), (1,))).astype(jnp.bfloat16)
    for pair in range(HEADS // 2):
        cols = slice(pair * 128, (pair + 1) * 128)
        results = []
        for side in range(2):
            head = slice(side * HDIM, (side + 1) * HDIM)
            head_q = query_s[:, cols][:, head]
            head_k = key_s[:, cols][:, head]
            head_v = value_b[:, cols][:, head]
            head_g = grad_mixed[:, cols][:, head]
            scores = dot(head_q, head_k, ((1,), (1,)))
            peak = jnp.max(scores, axis=1, keepdims=True)
            expo = jnp.exp(scores - peak)
            probs = expo / jnp.sum(expo, axis=1, keepdims=True)
            probs_b = probs.astype(jnp.bfloat16)
            mixed = dot(probs_b, head_v)
            grad_p = dot(head_g, head_v, ((1,), (1,)))
            grad_v = dot(probs_b, head_g, ((0,), (0,)))
            row_dot = jnp.sum(probs * grad_p, axis=1, keepdims=True)
            grad_s = (probs * (grad_p - row_dot)).astype(jnp.bfloat16)
            grad_q = dot(grad_s, head_k)
            grad_k = dot(grad_s, head_q, ((0,), (0,)))
            results.append((mixed, grad_q, grad_k, grad_v))
        mixed, grad_q, grad_k, grad_v = (
            jnp.concatenate([low, high], axis=1) for low, high in zip(*results)
        )
        mixed_s[:, cols] = mixed.astype(jnp.bfloat16)
        grad_q = grad_q * factor
        gproj_s[:, cols] = (grad_q * cosine - swap_halves(grad_q) * sine).astype(jnp.bfloat16)
        gproj_s[:, INNER + pair * 128 : INNER + (pair + 1) * 128] = (
            grad_k * cosine - swap_halves(grad_k) * sine
        ).astype(jnp.bfloat16)
        gproj_s[:, 2 * INNER + pair * 128 : 2 * INNER + (pair + 1) * 128] = grad_v.astype(
            jnp.bfloat16
        )
    mixed_b = mixed_s[...]
    attended_ref[...] = (x + dot(mixed_b, outw_ref[...])).astype(jnp.bfloat16)
    grad_out_ref[...] = (dot(mixed_b, grads_ref[...], ((0,), (0,))) * factor_all).astype(
        grad_out_ref.dtype
    )
    grad_qkv_ref[...] = (dot(normed_x, gproj_s[...], ((0,), (0,))) * factor_all).astype(
        grad_qkv_ref.dtype
    )


def whole(memory_space=pltpu.VMEM):
    return pl.BlockSpec(memory_space=memory_space)


def spectrum(frames_here, widths_own, starts_own, audio, rim, gain, place):
    rows, own = audio.shape
    total = rows * frames_here
    own_bands = place.shape[1] // MAXW
    return pl.pallas_call(
        lambda *refs: spectrum_kernel(frames_here, *refs),
        out_shape=jax.ShapeDtypeStruct((own_bands * total // 2, FEAT), jnp.bfloat16),
        in_specs=[whole(pltpu.SMEM)] * 2 + [whole()] * 7,
        out_specs=whole(),
        scratch_shapes=[
            pltpu.VMEM((rows, WIN), jnp.float32),
            pltpu.VMEM((rows, WIN), jnp.float32),
            pltpu.VMEM((WIN // 128, total, 128), jnp.float32),
            pltpu.VMEM((OUTER * total, 2 * SPAN), jnp.float32),
            pltpu.VMEM((6 * total, BINS), jnp.bfloat16),
            pltpu.VMEM((BINS, own_bands * MAXW), jnp.bfloat16),
        ],
        name="spectrum",
    )(
        widths_own,
        starts_own,
        audio,
        rim,
        gain,
        place,
        jnp.asarray(window_table()),
        jnp.asarray(twiddle_table()),
        jnp.asarray(inner_table()),
    )


def layer(feats, weight, grads, norm_gain, qkv_weight, out_weight, factor_all, grad_type):
    cosine, sine = rotary_table(np.arange(FRAMES))
    return pl.pallas_call(
        lambda *refs: layer_kernel(*refs, factor_all=factor_all),
        out_shape=(
            jax.ShapeDtypeStruct((FRAMES, D), jnp.bfloat16),
            jax.ShapeDtypeStruct((D, 3 * INNER), grad_type),
            jax.ShapeDtypeStruct((INNER, D), grad_type),
        ),
        in_specs=[whole()] * 8,
        out_specs=(whole(),) * 3,
        scratch_shapes=[
            pltpu.VMEM((FRAMES, INNER), jnp.bfloat16),
            pltpu.VMEM((FRAMES, INNER), jnp.bfloat16),
            pltpu.VMEM((FRAMES, INNER), jnp.bfloat16),
            pltpu.VMEM((FRAMES, 3 * INNER), jnp.bfloat16),
        ],
        name="layer",
    )(
        feats,
        weight,
        grads,
        norm_gain.reshape(1, D),
        qkv_weight,
        out_weight,
        jnp.asarray(cosine),
        jnp.asarray(sine),
    )


def body(
    audio_clips, band_widths, band_gain, band_weight, norm_gain, qkv_weight, out_weight, cotangent
):
    tm = lax.axis_size("tm")
    own_bands = BANDS // lax.axis_size("band")
    frame_block = audio_clips.shape[2] // HOP
    audio = jnp.transpose(audio_clips, (1, 0, 2)).reshape(2 * CLIPS, -1)
    rim = lax.ppermute(
        audio[:, : WIN - HOP], "tm", [(source, source - 1) for source in range(1, tm)]
    )
    starts = jnp.cumsum(band_widths, dtype=jnp.int32) - band_widths
    first_band = lax.axis_index("band") * own_bands
    widths_own = lax.dynamic_slice_in_dim(band_widths, first_band, own_bands)
    starts_own = lax.dynamic_slice_in_dim(starts, first_band, own_bands)
    within = lax.iota(jnp.int32, MAXW)[None, :]
    place = jnp.where(within < widths_own[:, None], starts_own[:, None] + within, -1)
    gain = jnp.transpose(band_gain.reshape(own_bands, MAXW, 4), (0, 2, 1))
    normed = spectrum(
        frame_block,
        widths_own.reshape(1, own_bands),
        starts_own.reshape(1, own_bands),
        audio,
        rim,
        gain,
        place.reshape(1, own_bands * MAXW),
    )
    sequences = own_bands * CLIPS
    early = jnp.concatenate(
        [
            cotangent.reshape(sequences, frame_block, D),
            jnp.broadcast_to(
                band_weight[:, None], (own_bands, CLIPS, FEAT // tm, D)
            ).reshape(sequences, FEAT // tm, D),
        ],
        axis=1,
    )
    early = lax.all_to_all(early, "tm", split_axis=0, concat_axis=0, tiled=True)
    grads = early[:, :frame_block].reshape(FRAMES, D)
    weight = early[:, frame_block:].reshape(FEAT, D)
    feats = lax.all_to_all(
        normed.reshape(sequences, frame_block, FEAT), "tm", split_axis=0, concat_axis=0, tiled=True
    ).reshape(FRAMES, FEAT)
    factor_all = 1.0 / math.sqrt(BANDS * CLIPS * FRAMES)
    attended, grad_qkv, grad_out = layer(
        feats, weight, grads, norm_gain, qkv_weight, out_weight, factor_all, jnp.float32
    )
    returned = lax.all_to_all(
        attended.reshape(tm, frame_block, D), "tm", split_axis=0, concat_axis=0, tiled=True
    )
    attended_out = returned.reshape(own_bands, CLIPS, frame_block, D)
    grad_qkv, grad_out = lax.psum((grad_qkv, grad_out), ("tm", "band"))
    return (attended_out, grad_qkv, grad_out)


def solution(mesh):
    return jax.shard_map(
        body,
        mesh=mesh,
        in_specs=(
            P(None, None, "tm"),
            P(),
            P("band", None),
            P("band", "tm", None),
            P(),
            P(),
            P(),
            P("band", None, "tm", None),
        ),
        out_specs=(P("band", None, "tm", None), P(), P()),
        check_vma=False,
    )
```

time: 599 us -> 391 us (0.65)
  local copies, waits for them, and re-layouts: 124 us -> 17.1 us
  matrix products: 70 us -> 0 us
  other arithmetic: 65.9 us -> 2.7 us
  waiting for transfers between devices: 267 us -> 293 us
  Pallas kernels: 0 us -> 17.9 us
  starting transfers between devices: 31.9 us -> 25.3 us
    dot_general x62 -> x0, matrix products: 70 us -> none  [the longest x53 47.4 us: device_product(): return jnp.einsum(pattern, left, right, preferred_element_type=jnp.float32)]
    gather x2 -> x0, local copies, waits for them, and re-layouts: 68.3 us -> none  [cut_frames(): return jnp.take(samples, position, axis=2)]
    mul x19 -> x0, other arithmetic: 35.6 us -> none  [the longest x8 33.7 us: dft_table(): jnp.cos(angle) * column]
    all_to_all x2, waiting for transfers between devices: 9.62 us -> 30.8 us  [the longest x1 19.4 us: body(): early = lax.all_to_all(early, 'tm', split_axis=0, concat_axis=0, tiled=True)]
    pallas_call x0 -> x2, Pallas kernels: none -> 17.9 us  [the longest x1 12.2 us: layer(): pl.pallas_call(lambda *refs: layer_kernel(*refs, factor_all=factor_all),...]
    dynamic_slice x24 -> x0, local copies, waits for them, and re-layouts: 15.2 us -> none  [body(): normed = lax.map(one_band, (widths_own, starts_own, band_gain))]
    mul x8 -> x0, local copies, waits for them, and re-layouts: 15 us -> none  [band_normed(): scaled = masked * inverse[:, None, :, None, None]]
    concatenate x2 -> x1, other arithmetic: 9.04 us -> 1.17 us  [body(): jnp.concatenate([cotangent.reshape(sequences, frame_block, D), jnp.broadc...]
  transfers between devices with their start and end apart: 5 -> 4, of which waited for: 2 -> 3; matrix products, arithmetic and copies ran while one was open for 34% -> 2% of each run, Pallas kernels for 0% -> 0%
where the time goes in v1:
time: 391 us; the launch traced here: 390 us
  waiting for transfers between devices  293 us (75%)
  starting transfers between devices  25.3 us (6%)
  blocking collectives  19.8 us (5%)
  Pallas kernels  17.9 us (5%)
  local copies, waits for them, and re-layouts  17.1 us (4%)
  between operations  14.1 us (4%)
    psum x1, waiting for transfers between devices, body(): grad_qkv, grad_out = lax.psum((grad_qkv, grad_out), ('tm', 'band'))  262 us
    all_to_all x1, blocking collectives, body(): lax.all_to_all(attended.reshape(tm, frame_block, D), 'tm', split_axis=0,...  19.8 us
    all_to_all x1, waiting for transfers between devices, body(): early = lax.all_to_all(early, 'tm', split_axis=0, concat_axis=0, tiled=True)  19.4 us
    all_to_all x1, starting transfers between devices, body(): lax.all_to_all(normed.reshape(sequences, frame_block, FEAT), 'tm', split_...  18 us
    pallas_call x1, Pallas kernels, layer(): pl.pallas_call(lambda *refs: layer_kernel(*refs, factor_all=factor_all),...  12.2 us
    all_to_all x1, waiting for transfers between devices, body(): lax.all_to_all(normed.reshape(sequences, frame_block, FEAT), 'tm', split_...  11.4 us
  transfers between devices with their start and end apart: 4, of which 3 were waited for; matrix products, arithmetic and copies ran while one was open for 2% of the time, Pallas kernels for 0%

profile of v1, /device:TPU:1, one launch (start us, length us, event | category | flops | bytes accessed | tf_op | source)
XLA Modules:
  0.0 389.7 jit_solution(6734651795128554275)
XLA Ops:
  7.2 0.9 copy.23
  8.1 0.0 copy-start
  8.1 0.0 copy-start.5
  8.1 1.4 collective-permute-start
  9.5 1.3 dynamic-slice_bitcast_fusion.1.refs_0_
  10.8 0.7 dynamic_slice.6
  11.6 0.7 copy.18
  12.3 0.1 reduce-window.9
  12.4 0.0 copy-start.3
  12.4 0.1 reduce
  12.5 0.7 sub.3
  13.2 0.1 dynamic_slice.7
  13.3 0.8 copy.20
  14.1 0.7 copy.21
  14.8 0.7 add_select_fusion
  15.5 0.6 dynamic-slice_bitcast_fusion.refs_1_
  16.1 0.0 collective-permute-done.refs_3_
  16.1 0.0 copy-start.4
  16.1 0.0 copy-done
  16.1 0.6 copy-done.4
  16.7 5.7 %spectrum.1 = bf16[256,512]{1,0:T(8,128)(2,1)} custom-call(s32[1,8]{1,0:T(1,128)} %dynamic-slice_bitcast_fusion.1.refs_0_, s32[1,8]{1,0:T(1,128)} %dynamic-slice_bitcast_fusion.refs_1_, f32[16,1764]{1,0:T(8,128)} %bitcast.20, f32[16,1607]{1,0:T(8,128)} %copy-done.4, f32[8,4,128]{2,1,0:T(4,128)} %bitcast.24, s32[1,1024]{1,0:T(1,128)} %bitcast.25, ...), custom_call_target="tpu_custom_call" | custom-call | tf_op jit(solution)/shard_map/spectrum/pallas_call | solution.py:269
  22.5 1.7 reshape.130
  24.2 18.0 %all-to-all-start = ((bf16[64,4,512]{2,1,0:T(4,128)(2,1)}), bf16[64,4,512]{2,1,0:T(4,128)(2,1)S(1)}, u32[]{:S(2)}, u32[]{:S(2)}) async-start(bf16[64,4,512]{2,1,0:T(4,128)(2,1)} %reshape.130), calls=%async_computation | async-start | bytes 524288 | tf_op jit(solution)/shard_map/all_to_all | solution.py:365
  42.2 0.0 copy-done.5
  42.3 0.0 copy-start.6
  42.3 0.0 copy-done.3
  42.3 1.2 pad_maximum_fusion
  43.5 11.4 %all-to-all-done = bf16[64,4,512]{2,1,0:T(4,128)(2,1)S(1)} async-done(((bf16[64,4,512]{2,1,0:T(4,128)(2,1)}), bf16[64,4,512]{2,1,0:T(4,128)(2,1)S(1)}, u32[]{:S(2)}, u32[]{:S(2)}) %all-to-all-start) | async-done | bytes 262176 | tf_op jit(solution)/shard_map/all_to_all | solution.py:365
  54.9 5.6 %all-to-all-start.1 = ((bf16[64,12,384]{2,1,0:T(8,128)(2,1)}), bf16[64,12,384]{2,1,0:T(8,128)(2,1)S(1)}, u32[]{:S(2)}, u32[]{:S(2)}) async-start(bf16[64,12,384]{2,1,0:T(8,128)(2,1)} %pad_maximum_fusion), calls=%async_computation.1 | async-start | bytes 1572864 | tf_op jit(solution)/shard_map/all_to_all | solution.py:362
  60.6 0.2 all-reduce.3.cloned.1.call-start
  60.8 0.0 copy-done.6
  60.8 0.6 reshape.136.refs_3_
  61.4 0.8 reshape.131.refs_0_
  62.1 19.4 %all-to-all-done.1 = bf16[64,12,384]{2,1,0:T(8,128)(2,1)S(1)} async-done(((bf16[64,12,384]{2,1,0:T(8,128)(2,1)}), bf16[64,12,384]{2,1,0:T(8,128)(2,1)S(1)}, u32[]{:S(2)}, u32[]{:S(2)}) %all-to-all-start.1) | async-done | bytes 589856 | tf_op jit(solution)/shard_map/all_to_all | solution.py:362
  81.5 0.1 slice.14
  81.6 0.7 reshape.135.refs_2_
  82.3 0.9 slice_bitcast_fusion.refs_1_
  83.2 12.2 %layer.1 = (bf16[256,384]{1,0:T(8,128)(2,1)}, f32[384,1536]{1,0:T(8,128)}, f32[512,384]{1,0:T(8,128)}) custom-call(bf16[256,512]{1,0:T(8,128)(2,1)} %reshape.131.refs_0_, bf16[512,384]{1,0:T(8,128)(2,1)} %slice_bitcast_fusion.refs_1_, bf16[256,384]{1,0:T(8,128)(2,1)} %reshape.135.refs_2_, f32[1,384]{1,0:T(1,128)} %reshape.136.refs_3_, ...), custom_call_target="tpu_custom_call" | custom-call | tf_op jit(solution)/shard_map/layer/pallas_call | solution.py:298
  95.3 0.0 copy-start.2
  95.3 0.0 all-reduce.3.cloned.1.call-update
  95.4 0.9 copy-done.2
  96.3 0.1 reshape.137
  96.3 19.8 %all_to_all.15 = bf16[64,4,384]{2,1,0:T(4,128)(2,1)S(1)} all-to-all(bf16[64,4,384]{2,1,0:T(4,128)(2,1)S(1)} %reshape.137), channel_id=1, replica_groups=mesh['tm'=64,'band'=8] {'tm'}, dimensions={0} | all-to-all | bytes 393216 | tf_op jit(solution)/shard_map/all_to_all | solution.py:372
  116.1 261.9 %all-reduce.3.cloned.1.call-done = (f32[384,1536]{1,0:T(8,128)}, f32[512,384]{1,0:T(8,128)}) async-done(((f32[384,1536]{1,0:T(8,128)}, f32[512,384]{1,0:T(8,128)}), (f32[384,1536]{1,0:T(8,128)}, f32[512,384]{1,0:T(8,128)})) %all-reduce.3.cloned.1.call-update) | async-done | bytes 3145744 | tf_op jit(solution)/shard_map/psum | solution.py:376
  378.0 0.7 copy.27
  378.6 0.0 copy-start.1
  378.6 3.3 copy.28
  381.9 0.0 copy-done.1
  381.9 0.9 copy.29
  (2 shorter events, 0.0 us)
Async XLA Ops:
  8.1 8.0 %copy-start = (f32[2,8,1764]{2,1,0:T(8,128)}, f32[2,8,1764]{2,1,0:T(8,128)S(1)}, u32[]{:S(2)}) copy-start(f32[2,8,1764]{2,1,0:T(8,128)S(1)} %copy.23) | copy-start | bytes 338692
  8.1 34.1 %copy-start.5 = (bf16[8,8,384]{2,1,0:T(8,128)(2,1)S(1)}, bf16[8,8,384]{2,1,0:T(8,128)(2,1)}, u32[]{:S(2)}) copy-start(bf16[8,8,384]{2,1,0:T(8,128)(2,1)} %param.16) | copy-start | bytes 147460
  8.1 8.0 %collective-permute-start = (f32[16,1607]{1,0:T(8,128)S(1)}, f32[16,1607]{1,0:T(8,128)S(1)}, u32[]{:S(2)}, u32[]{:S(2)}) collective-permute-start(f32[16,1607]{1,0:T(8,128)S(1)} %slice.12), channel_id=1, source_target_pairs={{8,0},{16,8},{24,16},{32,24},{40,32},{48,40},{56,48},{64,56},{72,6... | collective-permute-start | bytes 308552 | tf_op jit(solution)/shard_map/ppermute | solution.py:333
  12.4 29.9 %copy-start.3 = (bf16[8,8,4,384]{3,2,1,0:T(4,128)(2,1)S(1)}, bf16[8,8,4,384]{3,2,1,0:T(4,128)(2,1)}, u32[]{:S(2)}) copy-start(bf16[8,8,4,384]{3,2,1,0:T(4,128)(2,1)} %param.20) | copy-start | bytes 589828
  16.1 0.6 copy-start.4
  24.2 30.7 %all-to-all-start = ((bf16[64,4,512]{2,1,0:T(4,128)(2,1)}), bf16[64,4,512]{2,1,0:T(4,128)(2,1)S(1)}, u32[]{:S(2)}, u32[]{:S(2)}) async-start(bf16[64,4,512]{2,1,0:T(4,128)(2,1)} %reshape.130), calls=%async_computation | async-start | bytes 524288 | tf_op jit(solution)/shard_map/all_to_all | solution.py:365
  42.3 18.5 %copy-start.6 = (f32[384]{0:T(512)S(1)}, f32[384]{0:T(512)}, u32[]{:S(2)}) copy-start(f32[384]{0:T(512)} %param.17) | copy-start | bytes 4612
  54.9 26.6 %all-to-all-start.1 = ((bf16[64,12,384]{2,1,0:T(8,128)(2,1)}), bf16[64,12,384]{2,1,0:T(8,128)(2,1)S(1)}, u32[]{:S(2)}, u32[]{:S(2)}) async-start(bf16[64,12,384]{2,1,0:T(8,128)(2,1)} %pad_maximum_fusion), calls=%async_computation.1 | async-start | bytes 1572864 | tf_op jit(solution)/shard_map/all_to_all | solution.py:362
  60.6 317.4 %all-reduce.3.cloned.1.call-start = ((), (), s32[]{:S(2)}) async-start(), calls=%async_computation.3 | async-start | bytes 6291456 | tf_op jit(solution)/shard_map/psum | solution.py:376
  95.3 0.9 copy-start.2
  378.6 3.3 copy-start.1
Sparse Core Ops, SparseCore 0:
  95.5 282.4 all-reduce.2

commit v2 on v1

--- a/solution.py
+++ b/solution.py
@@ -185,8 +185,7 @@
     cos_ref,
     sin_ref,
     attended_ref,
-    grad_qkv_ref,
-    grad_out_ref,
+    partial_ref,
     query_s,
     key_s,
     mixed_s,
@@ -250,12 +249,19 @@
         )
     mixed_b = mixed_s[...]
     attended_ref[...] = (x + dot(mixed_b, outw_ref[...])).astype(jnp.bfloat16)
-    grad_out_ref[...] = (dot(mixed_b, grads_ref[...], ((0,), (0,))) * factor_all).astype(
-        grad_out_ref.dtype
-    )
-    grad_qkv_ref[...] = (dot(normed_x, gproj_s[...], ((0,), (0,))) * factor_all).astype(
-        grad_qkv_ref.dtype
-    )
+    for block in range(3 * INNER // D):
+        part = dot(normed_x, gproj_s[:, block * D : (block + 1) * D], ((0,), (0,)))
+        partial_ref[block * D : (block + 1) * D, :] = (part * factor_all).astype(jnp.bfloat16)
+    part = dot(mixed_b, grads_ref[...], ((0,), (0,)))
+    partial_ref[3 * INNER :, :] = (part * factor_all).astype(jnp.bfloat16)
+
+
+def unpack_kernel(gathered_ref, grad_qkv_ref, grad_out_ref):
+    for block in range(3 * INNER // D):
+        grad_qkv_ref[:, block * D : (block + 1) * D] = gathered_ref[
+            block * D : (block + 1) * D, :
+        ].astype(jnp.float32)
+    grad_out_ref[...] = gathered_ref[3 * INNER :, :].astype(jnp.float32)
 
 
 def whole(memory_space=pltpu.VMEM):
@@ -293,17 +299,16 @@
     )
 
 
-def layer(feats, weight, grads, norm_gain, qkv_weight, out_weight, factor_all, grad_type):
+def layer(feats, weight, grads, norm_gain, qkv_weight, out_weight, factor_all):
     cosine, sine = rotary_table(np.arange(FRAMES))
     return pl.pallas_call(
         lambda *refs: layer_kernel(*refs, factor_all=factor_all),
         out_shape=(
             jax.ShapeDtypeStruct((FRAMES, D), jnp.bfloat16),
-            jax.ShapeDtypeStruct((D, 3 * INNER), grad_type),
-            jax.ShapeDtypeStruct((INNER, D), grad_type),
+            jax.ShapeDtypeStruct((4 * INNER, D), jnp.bfloat16),
         ),
         in_specs=[whole()] * 8,
-        out_specs=(whole(),) * 3,
+        out_specs=(whole(),) * 2,
         scratch_shapes=[
             pltpu.VMEM((FRAMES, INNER), jnp.bfloat16),
             pltpu.VMEM((FRAMES, INNER), jnp.bfloat16),
@@ -323,18 +328,66 @@
     )
 
 
+def unpack(gathered):
+    return pl.pallas_call(
+        unpack_kernel,
+        out_shape=(
+            jax.ShapeDtypeStruct((D, 3 * INNER), jnp.float32),
+            jax.ShapeDtypeStruct((INNER, D), jnp.float32),
+        ),
+        in_specs=[whole()],
+        out_specs=(whole(),) * 2,
+        name="unpack",
+    )(gathered)
+
+
+def exchange(blocks, axis):
+    return lax.all_to_all(blocks, axis, split_axis=0, concat_axis=0, tiled=True)
+
+
+def reduced(blocks):
+    return jnp.sum(blocks.astype(jnp.float32), axis=0).astype(jnp.bfloat16)
+
+
+def scatter_sum(values, axis):
+    count = lax.axis_size(axis)
+    blocks = values.reshape(count, values.shape[0] // count, values.shape[1])
+    return reduced(exchange(blocks, axis))
+
+
+def gather(values, axis):
+    count = lax.axis_size(axis)
+    blocks = jnp.broadcast_to(values[None], (count,) + values.shape)
+    return exchange(blocks, axis).reshape(count * values.shape[0], values.shape[1])
+
+
 def body(
     audio_clips, band_widths, band_gain, band_weight, norm_gain, qkv_weight, out_weight, cotangent
 ):
     tm = lax.axis_size("tm")
-    own_bands = BANDS // lax.axis_size("band")
+    band_at = lax.axis_index("x") * lax.axis_size("core") + lax.axis_index("core")
+    own_bands = band_gain.shape[0]
     frame_block = audio_clips.shape[2] // HOP
     audio = jnp.transpose(audio_clips, (1, 0, 2)).reshape(2 * CLIPS, -1)
     rim = lax.ppermute(
         audio[:, : WIN - HOP], "tm", [(source, source - 1) for source in range(1, tm)]
     )
+    sequences = own_bands * CLIPS
+    rows = FEAT // tm
+    early = jnp.concatenate(
+        [
+            cotangent.reshape(sequences, frame_block, D),
+            jnp.broadcast_to(band_weight[:, None], (own_bands, CLIPS, rows, D)).reshape(
+                sequences, rows, D
+            ),
+        ],
+        axis=1,
+    )
+    early = exchange(early, "tm")
+    grads = early[:, :frame_block].reshape(FRAMES, D)
+    weight = early[:, frame_block:].reshape(FEAT, D)
     starts = jnp.cumsum(band_widths, dtype=jnp.int32) - band_widths
-    first_band = lax.axis_index("band") * own_bands
+    first_band = band_at * own_bands
     widths_own = lax.dynamic_slice_in_dim(band_widths, first_band, own_bands)
     starts_own = lax.dynamic_slice_in_dim(starts, first_band, own_bands)
     within = lax.iota(jnp.int32, MAXW)[None, :]
@@ -349,48 +402,40 @@
         gain,
         place.reshape(1, own_bands * MAXW),
     )
-    sequences = own_bands * CLIPS
-    early = jnp.concatenate(
-        [
-            cotangent.reshape(sequences, frame_block, D),
-            jnp.broadcast_to(
-                band_weight[:, None], (own_bands, CLIPS, FEAT // tm, D)
-            ).reshape(sequences, FEAT // tm, D),
-        ],
-        axis=1,
-    )
-    early = lax.all_to_all(early, "tm", split_axis=0, concat_axis=0, tiled=True)
-    grads = early[:, :frame_block].reshape(FRAMES, D)
-    weight = early[:, frame_block:].reshape(FEAT, D)
-    feats = lax.all_to_all(
-        normed.reshape(sequences, frame_block, FEAT), "tm", split_axis=0, concat_axis=0, tiled=True
-    ).reshape(FRAMES, FEAT)
+    feats = exchange(normed.reshape(sequences, frame_block, FEAT), "tm").reshape(FRAMES, FEAT)
     factor_all = 1.0 / math.sqrt(BANDS * CLIPS * FRAMES)
-    attended, grad_qkv, grad_out = layer(
-        feats, weight, grads, norm_gain, qkv_weight, out_weight, factor_all, jnp.float32
-    )
-    returned = lax.all_to_all(
-        attended.reshape(tm, frame_block, D), "tm", split_axis=0, concat_axis=0, tiled=True
-    )
-    attended_out = returned.reshape(own_bands, CLIPS, frame_block, D)
-    grad_qkv, grad_out = lax.psum((grad_qkv, grad_out), ("tm", "band"))
+    attended, partial = layer(
+        feats, weight, grads, norm_gain, qkv_weight, out_weight, factor_all
+    )
+    partial = scatter_sum(scatter_sum(partial, "core"), "x")
+    both = jnp.concatenate(
+        [attended.reshape(tm, frame_block, D), partial.reshape(tm, -1, D)], axis=1
+    )
+    both = exchange(both, "tm")
+    attended_out = both[:, :frame_block].reshape(own_bands, CLIPS, frame_block, D)
+    total = reduced(both[:, frame_block:])
+    for axis in ("tm", "x", "core"):
+        total = gather(total, axis)
+    grad_qkv, grad_out = unpack(total)
     return (attended_out, grad_qkv, grad_out)
 
 
 def solution(mesh):
+    split = Mesh(mesh.devices.reshape(mesh.shape["tm"], -1, 2), ("tm", "x", "core"))
+    band = ("x", "core")
     return jax.shard_map(
         body,
-        mesh=mesh,
+        mesh=split,
         in_specs=(
             P(None, None, "tm"),
             P(),
-            P("band", None),
-            P("band", "tm", None),
+            P(band, None),
+            P(band, "tm", None),
             P(),
             P(),
             P(),
-            P("band", None, "tm", None),
+            P(band, None, "tm", None),
         ),
-        out_specs=(P("band", None, "tm", None), P(), P()),
+        out_specs=(P(band, None, "tm", None), P(), P()),
         check_vma=False,
     )

time: 391 us -> 180 us (0.46)
  waiting for transfers between devices: 293 us -> 42.5 us
  blocking collectives: 19.8 us -> 69.6 us
  between operations: 14.1 us -> 0.79 us
  local copies, waits for them, and re-layouts: 17.1 us -> 11.7 us
  starting transfers between devices: 25.3 us -> 29.3 us
    psum x1 -> x0, waiting for transfers between devices: 262 us -> none  [body(): grad_qkv, grad_out = lax.psum((grad_qkv, grad_out), ('tm', 'band'))]
    all_to_all x1 -> x5, blocking collectives: 19.8 us -> 69.6 us  [exchange(): return lax.all_to_all(blocks, axis, split_axis=0, concat_axis=0, tiled=True)]
    all_to_all x2 -> x3, waiting for transfers between devices: 30.8 us -> 42.5 us  [exchange(): return lax.all_to_all(blocks, axis, split_axis=0, concat_axis=0, tiled=True)]
    unnamed x18 -> x13, local copies, waits for them, and re-layouts: 7.25 us -> 1.5 us
    all_to_all x2 -> x3, starting transfers between devices: 23.7 us -> 27.9 us  [exchange(): return lax.all_to_all(blocks, axis, split_axis=0, concat_axis=0, tiled=True)]
  transfers between devices with their start and end apart: 4 -> 4, of which waited for: 3 -> 3; matrix products, arithmetic and copies ran while one was open for 2% -> 5% of each run, Pallas kernels for 0% -> 0%
where the time goes in v2:
time: 180 us; the launch traced here: 179 us
  blocking collectives  69.6 us (39%)
  waiting for transfers between devices  42.5 us (24%)
  starting transfers between devices  29.3 us (16%)
  Pallas kernels  20.3 us (11%)
  local copies, waits for them, and re-layouts  11.7 us (6%)
  other arithmetic  5.25 us (3%)
    all_to_all x5, blocking collectives, exchange(): return lax.all_to_all(blocks, axis, split_axis=0, concat_axis=0, tiled=True)  69.6 us
    all_to_all x3, waiting for transfers between devices, exchange(): return lax.all_to_all(blocks, axis, split_axis=0, concat_axis=0, tiled=True)  42.5 us
    all_to_all x3, starting transfers between devices, exchange(): return lax.all_to_all(blocks, axis, split_axis=0, concat_axis=0, tiled=True)  27.9 us
    pallas_call x1, Pallas kernels, layer(): pl.pallas_call(lambda *refs: layer_kernel(*refs, factor_all=factor_all),...  11.3 us
    pallas_call x1, Pallas kernels, spectrum(): pl.pallas_call(lambda *refs: spectrum_kernel(frames_here, *refs), out_sha...  5.72 us
  transfers between devices with their start and end apart: 4, of which 3 were waited for; matrix products, arithmetic and copies ran while one was open for 5% of the time, Pallas kernels for 0%

profile of v2, /device:TPU:1, one launch (start us, length us, event | category | flops | bytes accessed | tf_op | source)
XLA Modules:
  0.0 179.4 jit_solution(10773171819208880020)
XLA Ops:
  0.6 0.9 copy.27
  1.5 0.0 copy-start
  1.5 0.0 copy-start.4
  1.6 1.4 collective-permute-start
  3.0 1.3 dynamic-slice_bitcast_fusion.1.refs_0_
  4.3 0.7 dynamic_slice.6
  5.0 0.7 copy.22
  5.8 0.1 reduce-window.9
  5.9 0.0 copy-start.2
  5.9 0.1 reduce.3
  6.0 0.7 sub.3
  6.6 0.1 dynamic_slice.7
  6.7 0.8 copy.24
  7.6 0.7 copy.25
  8.3 0.7 add_select_fusion
  8.9 0.6 dynamic-slice_bitcast_fusion.refs_1_
  9.5 0.0 collective-permute-done.refs_3_
  9.5 0.0 copy-start.3
  9.5 0.0 copy-done
  9.5 0.6 copy-done.3
  10.2 5.7 %spectrum.1 = bf16[256,512]{1,0:T(8,128)(2,1)} custom-call(s32[1,8]{1,0:T(1,128)} %dynamic-slice_bitcast_fusion.1.refs_0_, s32[1,8]{1,0:T(1,128)} %dynamic-slice_bitcast_fusion.refs_1_, f32[16,1764]{1,0:T(8,128)} %bitcast.27, f32[16,1607]{1,0:T(8,128)} %copy-done.3, f32[8,4,128]{2,1,0:T(4,128)} %bitcast.31, s32[1,1024]{1,0:T(1,128)} %bitcast.32, ...), custom_call_target="tpu_custom_call" | custom-call | tf_op jit(solution)/shard_map/spectrum/pallas_call | solution.py:275
  15.9 1.7 reshape.145
  17.6 18.0 %all-to-all-start = ((bf16[64,4,512]{2,1,0:T(4,128)(2,1)}), bf16[64,4,512]{2,1,0:T(4,128)(2,1)S(1)}, u32[]{:S(2)}, u32[]{:S(2)}) async-start(bf16[64,4,512]{2,1,0:T(4,128)(2,1)} %reshape.145), calls=%async_computation | async-start | bytes 524288 | tf_op jit(solution)/shard_map/all_to_all | solution.py:345
  35.6 0.0 copy-done.4
  35.7 0.0 copy-start.5
  35.7 0.0 copy-done.2
  35.7 1.2 pad_maximum_fusion
  36.9 11.4 %all-to-all-done = bf16[64,4,512]{2,1,0:T(4,128)(2,1)S(1)} async-done(((bf16[64,4,512]{2,1,0:T(4,128)(2,1)}), bf16[64,4,512]{2,1,0:T(4,128)(2,1)S(1)}, u32[]{:S(2)}, u32[]{:S(2)}) %all-to-all-start) | async-done | bytes 262176 | tf_op jit(solution)/shard_map/all_to_all | solution.py:345
  48.3 5.8 %all-to-all-start.1 = ((bf16[64,12,384]{2,1,0:T(8,128)(2,1)}), bf16[64,12,384]{2,1,0:T(8,128)(2,1)S(1)}, u32[]{:S(2)}, u32[]{:S(2)}) async-start(bf16[64,12,384]{2,1,0:T(8,128)(2,1)} %pad_maximum_fusion), calls=%async_computation.1 | async-start | bytes 1572864 | tf_op jit(solution)/shard_map/all_to_all | solution.py:345
  54.2 0.0 copy-done.5
  54.2 0.6 reshape.151.refs_3_
  54.8 0.8 reshape.146.refs_0_
  55.5 19.4 %all-to-all-done.1 = bf16[64,12,384]{2,1,0:T(8,128)(2,1)S(1)} async-done(((bf16[64,12,384]{2,1,0:T(8,128)(2,1)}), bf16[64,12,384]{2,1,0:T(8,128)(2,1)S(1)}, u32[]{:S(2)}, u32[]{:S(2)}) %all-to-all-start.1) | async-done | bytes 589856 | tf_op jit(solution)/shard_map/all_to_all | solution.py:345
  74.9 0.1 slice.22
  75.0 0.7 reshape.150.refs_2_
  75.7 0.9 slice_bitcast_fusion.refs_1_
  76.6 11.3 %layer.1 = (bf16[256,384]{1,0:T(8,128)(2,1)}, bf16[2048,384]{1,0:T(8,128)(2,1)}) custom-call(bf16[256,512]{1,0:T(8,128)(2,1)} %reshape.146.refs_0_, bf16[512,384]{1,0:T(8,128)(2,1)} %slice_bitcast_fusion.refs_1_, bf16[256,384]{1,0:T(8,128)(2,1)} %reshape.150.refs_2_, f32[1,384]{1,0:T(1,128)} %reshape.151.refs_3_, bf16[384,1536]{1,0:T(8,128)(2,1)} %refs_4_.1, ...), custom_call_target="tpu_custom_call" | custom-call | tf_op jit(solution)/shard_map/layer/pallas_call | solution.py:304
  87.9 10.4 %all_to_all.40 = bf16[2,1024,384]{2,1,0:T(8,128)(2,1)S(1)} all-to-all(bf16[2,1024,384]{2,1,0:T(8,128)(2,1)} %bitcast.23), channel_id=1, replica_groups=mesh['tm'=64,'x'=4,'core'=2] {'core'}, dimensions={0} | all-to-all | bytes 3145728 | tf_op jit(solution)/shard_map/all_to_all | solution.py:345
  98.3 0.0 copy-start.1
  98.3 1.4 reduce_sum.36
  99.7 4.0 %all-to-all-start.3 = ((bf16[4,256,384]{2,1,0:T(8,128)(2,1)}), bf16[4,256,384]{2,1,0:T(8,128)(2,1)S(1)}, u32[]{:S(2)}, u32[]{:S(2)}) async-start(bf16[4,256,384]{2,1,0:T(8,128)(2,1)} %bitcast.12), calls=%async_computation.3 | async-start | bytes 1572864 | tf_op jit(solution)/shard_map/all_to_all | solution.py:345
  103.7 0.0 copy-done.1
  103.7 0.1 reshape.152
  103.7 11.7 %all-to-all-done.3 = bf16[4,256,384]{2,1,0:T(8,128)(2,1)S(1)} async-done(((bf16[4,256,384]{2,1,0:T(8,128)(2,1)}), bf16[4,256,384]{2,1,0:T(8,128)(2,1)S(1)}, u32[]{:S(2)}, u32[]{:S(2)}) %all-to-all-start.3) | async-done | bytes 786464 | tf_op jit(solution)/shard_map/all_to_all | solution.py:345
  115.4 0.2 reduce_sum.37
  115.5 0.1 reshape.155
  115.6 0.2 pad_maximum_fusion.1
  115.8 19.5 %all_to_all.41 = bf16[64,8,384]{2,1,0:T(8,128)(2,1)S(1)} all-to-all(bf16[64,8,384]{2,1,0:T(8,128)(2,1)S(1)} %pad_maximum_fusion.1), channel_id=1, replica_groups=mesh['tm'=64,'x'=4,'core'=2] {'tm'}, dimensions={0} | all-to-all | bytes 786432 | tf_op jit(solution)/shard_map/all_to_all | solution.py:345
  135.3 0.8 slice_reduce_fusion
  136.1 0.1 broadcast_in_dim.18
  136.2 18.7 %all_to_all.42 = bf16[64,4,384]{2,1,0:T(4,128)(2,1)S(1)} all-to-all(bf16[64,4,384]{2,1,0:T(4,128)(2,1)S(1)} %broadcast_in_dim.18), channel_id=1, replica_groups=mesh['tm'=64,'x'=4,'core'=2] {'tm'}, dimensions={0} | all-to-all | bytes 393216 | tf_op jit(solution)/shard_map/all_to_all | solution.py:345
  154.8 0.1 broadcast_in_dim.36
  154.9 0.1 broadcast_in_dim.37
  155.0 11.6 %all_to_all.43 = bf16[4,256,384]{2,1,0:T(8,128)(2,1)S(1)} all-to-all(bf16[4,256,384]{2,1,0:T(8,128)(2,1)S(1)} %broadcast_in_dim.37), channel_id=1, replica_groups=mesh['tm'=64,'x'=4,'core'=2] {'x'}, dimensions={0} | all-to-all | bytes 1572864 | tf_op jit(solution)/shard_map/all_to_all | solution.py:345
  166.6 0.1 broadcast_in_dim.39
  166.7 9.5 %all_to_all.44 = bf16[2,1024,384]{2,1,0:T(8,128)(2,1)} all-to-all(bf16[2,1024,384]{2,1,0:T(8,128)(2,1)S(1)} %broadcast_in_dim.39), channel_id=1, replica_groups=mesh['tm'=64,'x'=4,'core'=2] {'core'}, dimensions={0} | all-to-all | bytes 3145728 | tf_op jit(solution)/shard_map/all_to_all | solution.py:345
  176.2 3.2 %unpack.1 = (f32[384,1536]{1,0:T(8,128)}, f32[512,384]{1,0:T(8,128)}) custom-call(bf16[2048,384]{1,0:T(8,128)(2,1)} %bitcast.21), custom_call_target="tpu_custom_call" | custom-call | tf_op jit(solution)/shard_map/unpack/pallas_call | solution.py:332
  (2 shorter events, 0.0 us)
Async XLA Ops:
  1.5 8.0 %copy-start = (f32[2,8,1764]{2,1,0:T(8,128)}, f32[2,8,1764]{2,1,0:T(8,128)S(1)}, u32[]{:S(2)}) copy-start(f32[2,8,1764]{2,1,0:T(8,128)S(1)} %copy.27) | copy-start | bytes 338692
  1.5 34.1 %copy-start.4 = (bf16[8,8,384]{2,1,0:T(8,128)(2,1)S(1)}, bf16[8,8,384]{2,1,0:T(8,128)(2,1)}, u32[]{:S(2)}) copy-start(bf16[8,8,384]{2,1,0:T(8,128)(2,1)} %param.16) | copy-start | bytes 147460
  1.6 7.9 %collective-permute-start = (f32[16,1607]{1,0:T(8,128)S(1)}, f32[16,1607]{1,0:T(8,128)S(1)}, u32[]{:S(2)}, u32[]{:S(2)}) collective-permute-start(f32[16,1607]{1,0:T(8,128)S(1)} %slice.20), channel_id=1, source_target_pairs={{8,0},{16,8},{24,16},{32,24},{40,32},{48,40},{56,48},{64,56},{72,6... | collective-permute-start | bytes 308552 | tf_op jit(solution)/shard_map/ppermute | solution.py:372
  5.9 29.9 %copy-start.2 = (bf16[8,8,4,384]{3,2,1,0:T(4,128)(2,1)S(1)}, bf16[8,8,4,384]{3,2,1,0:T(4,128)(2,1)}, u32[]{:S(2)}) copy-start(bf16[8,8,4,384]{3,2,1,0:T(4,128)(2,1)} %param.20) | copy-start | bytes 589828
  9.5 0.6 copy-start.3
  17.6 30.7 %all-to-all-start = ((bf16[64,4,512]{2,1,0:T(4,128)(2,1)}), bf16[64,4,512]{2,1,0:T(4,128)(2,1)S(1)}, u32[]{:S(2)}, u32[]{:S(2)}) async-start(bf16[64,4,512]{2,1,0:T(4,128)(2,1)} %reshape.145), calls=%async_computation | async-start | bytes 524288 | tf_op jit(solution)/shard_map/all_to_all | solution.py:345
  35.7 18.5 %copy-start.5 = (f32[384]{0:T(512)S(1)}, f32[384]{0:T(512)}, u32[]{:S(2)}) copy-start(f32[384]{0:T(512)} %param.17) | copy-start | bytes 4612
  48.3 26.6 %all-to-all-start.1 = ((bf16[64,12,384]{2,1,0:T(8,128)(2,1)}), bf16[64,12,384]{2,1,0:T(8,128)(2,1)S(1)}, u32[]{:S(2)}, u32[]{:S(2)}) async-start(bf16[64,12,384]{2,1,0:T(8,128)(2,1)} %pad_maximum_fusion), calls=%async_computation.1 | async-start | bytes 1572864 | tf_op jit(solution)/shard_map/all_to_all | solution.py:345
  98.3 5.4 %copy-start.1 = (bf16[256,384]{1,0:T(8,128)(2,1)S(1)}, bf16[256,384]{1,0:T(8,128)(2,1)}, u32[]{:S(2)}) copy-start(bf16[256,384]{1,0:T(8,128)(2,1)} %get-tuple-element.7) | copy-start | bytes 589828
  99.7 15.7 %all-to-all-start.3 = ((bf16[4,256,384]{2,1,0:T(8,128)(2,1)}), bf16[4,256,384]{2,1,0:T(8,128)(2,1)S(1)}, u32[]{:S(2)}, u32[]{:S(2)}) async-start(bf16[4,256,384]{2,1,0:T(8,128)(2,1)} %bitcast.12), calls=%async_computation.3 | async-start | bytes 1572864 | tf_op jit(solution)/shard_map/all_to_all | solution.py:345

commit v3 on v2

--- a/solution.py
+++ b/solution.py
@@ -7,6 +7,7 @@
 from jax.experimental import pallas as pl
 from jax.experimental.pallas import tpu as pltpu
 from jax.sharding import Mesh, PartitionSpec as P
+
 
 D = 384
 HEADS = 8
@@ -20,6 +21,8 @@
 BINS = 1024
 FEAT = 512
 FRAMES = 256
+TIME = ("z", "y")
+BAND = ("x", "core")
 
 OUTER = 8
 SPAN = WIN // OUTER
@@ -57,14 +60,25 @@
     )
 
 
+def split_bf16(values):
+    parts = []
+    for _ in range(3):
+        kept = values.astype(jnp.bfloat16)
+        parts.append(kept)
+        values = values - kept.astype(jnp.float32)
+    return parts
+
+
+def one_hot(hit):
+    return jnp.where(hit, 1.0, 0.0).astype(jnp.bfloat16)
+
+
 def spectrum_kernel(
-    frames_here,
+    place_ref,
     widths_ref,
-    starts_ref,
     audio_ref,
     rim_ref,
     gain_ref,
-    place_ref,
     taper_ref,
     twiddle_ref,
     inner_ref,
@@ -76,11 +90,14 @@
     bins,
     pick,
 ):
-    own = audio_ref.shape[1]
-    rows = audio_ref.shape[0]
+    own = audio_ref.shape[2]
+    rows = audio_ref.shape[0] * audio_ref.shape[1]
+    frames_here = own // HOP
     total = rows * frames_here
-    lead[:, :own] = audio_ref[...]
-    tail[:, : WIN - HOP] = rim_ref[...]
+    own_bands = gain_ref.shape[0]
+    for c in range(CLIPS):
+        lead[2 * c : 2 * c + 2, :own] = audio_ref[c]
+        tail[2 * c : 2 * c + 2, :own] = rim_ref[c]
     lane = lax.broadcasted_iota(jnp.int32, (rows, WIN), 1)
     for f in range(frames_here):
         here = own - HOP * f
@@ -127,40 +144,54 @@
         precision=lax.Precision.HIGHEST,
     )
     for low in range(OUTER):
+        cols = slice(low * HIGH, (low + 1) * HIGH)
         for part in range(2):
             piece = made[low * total : (low + 1) * total, part * HIGH : (part + 1) * HIGH]
-            cols = slice(low * HIGH, (low + 1) * HIGH)
-            for split in range(3):
+            for split, kept in enumerate(split_bf16(piece)):
                 at = (split * 2 + part) * total
-                kept = piece.astype(jnp.bfloat16)
                 bins[at : at + total, cols] = kept
-                piece = piece - kept.astype(jnp.float32)
-    target = place_ref[...]
-    for low in range(OUTER):
-        bin_at = low + OUTER * lax.broadcasted_iota(jnp.int32, (HIGH, target.shape[1]), 0)
-        pick[low * HIGH : (low + 1) * HIGH, :] = jnp.where(bin_at == target, 1.0, 0.0).astype(
-            jnp.bfloat16
-        )
-    own_bands = target.shape[1] // MAXW
-    half_rows = total // 2
+    first_band = place_ref[0] * own_bands
+    start = lax.fori_loop(0, first_band, lambda i, past: past + widths_ref[i], jnp.int32(0))
+    within = lax.broadcasted_iota(jnp.int32, (1, MAXW), 1)
+    high_at = OUTER * lax.broadcasted_iota(jnp.int32, (HIGH, MAXW), 0)
+    counts = []
+    for band in range(own_bands):
+        width = widths_ref[first_band + band]
+        target = jnp.where(within < width, start + within, -1)
+        for low in range(OUTER):
+            pick[low * HIGH : (low + 1) * HIGH, band * MAXW : (band + 1) * MAXW] = one_hot(
+                high_at == target - low
+            )
+        counts.append((4 * width).astype(jnp.float32))
+        start = start + width
     chosen = jnp.dot(bins[...], pick[...], preferred_element_type=jnp.float32)
     exact = chosen[: 2 * total] + chosen[2 * total : 4 * total] + chosen[4 * total :]
+    feature = lax.broadcasted_iota(jnp.int32, (FEAT, FEAT), 0)
+    column = lax.broadcasted_iota(jnp.int32, (FEAT, FEAT), 1)
+    order = one_hot(feature == (column % MAXW) * 4 + column // MAXW)
+    gain = sum(
+        jnp.dot(part, order, preferred_element_type=jnp.float32)
+        for part in split_bf16(gain_ref[...])
+    )
+    row = lax.broadcasted_iota(jnp.int32, (total, 1), 0)
     for band in range(own_bands):
         cols = slice(band * MAXW, (band + 1) * MAXW)
         re = exact[:total, cols]
         im = exact[total:, cols]
         power = jnp.sum(re * re + im * im, axis=1, keepdims=True)
-        power = power[:half_rows] + power[half_rows:]
-        count = (4 * widths_ref[0, band]).astype(jnp.float32)
-        inverse = lax.rsqrt(jnp.maximum(power / count, 0.25))
-        for a in range(2):
-            for r in range(2):
-                value = (re, im)[r][a * half_rows : (a + 1) * half_rows]
+        ahead = pltpu.roll(power, total - frames_here, 0)
+        behind = pltpu.roll(power, frames_here, 0)
+        power = power + jnp.where(row % (2 * frames_here) < frames_here, ahead, behind)
+        inverse = lax.rsqrt(jnp.maximum(power / counts[band], 0.25))
+        for r in range(2):
+            value = ((re, im)[r] * inverse).reshape(CLIPS, 2 * frames_here, MAXW)
+            for a in range(2):
                 which = 2 * a + r
-                out_ref[
-                    band * half_rows : (band + 1) * half_rows,
-                    which * MAXW : (which + 1) * MAXW,
-                ] = (value * inverse * gain_ref[band, which : which + 1, :]).astype(jnp.bfloat16)
+                lanes = slice(which * MAXW, (which + 1) * MAXW)
+                own_gain = gain[band : band + 1, lanes]
+                out_ref[band * CLIPS : (band + 1) * CLIPS, :, lanes] = (
+                    value[:, a * frames_here : (a + 1) * frames_here, :] * own_gain[None]
+                ).astype(jnp.bfloat16)
 
 
 def swap_halves(values):
@@ -184,12 +215,15 @@
     outw_ref,
     cos_ref,
     sin_ref,
+    core_ref,
     attended_ref,
-    partial_ref,
+    keep_ref,
+    send_ref,
     query_s,
     key_s,
     mixed_s,
     gproj_s,
+    halves,
     *,
     factor_all,
 ):
@@ -249,33 +283,59 @@
         )
     mixed_b = mixed_s[...]
     attended_ref[...] = (x + dot(mixed_b, outw_ref[...])).astype(jnp.bfloat16)
+    core = core_ref[0]
+    half_rows = 2 * INNER
+
+    def place(first, values):
+        values = (values * factor_all).astype(jnp.bfloat16)
+        at = first
+        while at < first + D:
+            half, row = divmod(at, half_rows)
+            end = min(first + D, (half + 1) * half_rows)
+            slot = core if half == 0 else 1 - core
+            halves[slot, row : row + end - at, :] = values[at - first : end - first]
+            at = end
+
     for block in range(3 * INNER // D):
-        part = dot(normed_x, gproj_s[:, block * D : (block + 1) * D], ((0,), (0,)))
-        partial_ref[block * D : (block + 1) * D, :] = (part * factor_all).astype(jnp.bfloat16)
-    part = dot(mixed_b, grads_ref[...], ((0,), (0,)))
-    partial_ref[3 * INNER :, :] = (part * factor_all).astype(jnp.bfloat16)
-
-
-def unpack_kernel(gathered_ref, grad_qkv_ref, grad_out_ref):
+        place(block * D, dot(normed_x, gproj_s[:, block * D : (block + 1) * D], ((0,), (0,))))
+    part = dot(mixed_b, grads_ref[...], ((0,), (0,))) * factor_all
+    halves[1 - core, half_rows - INNER :, :] = part.astype(jnp.bfloat16)
+    keep_ref[...] = halves[0]
+    send_ref[...] = halves[1]
+
+
+def unpack_kernel(core_ref, own_ref, other_ref, grad_qkv_ref, grad_out_ref):
+    half_rows = own_ref.shape[0]
+    first = core_ref[0] == 0
+
+    def rows(start, stop):
+        half = start // half_rows
+        at = slice(start - half * half_rows, stop - half * half_rows)
+        own, other = own_ref[at, :], other_ref[at, :]
+        return lax.select(first, *((own, other) if half == 0 else (other, own))).astype(jnp.float32)
+
     for block in range(3 * INNER // D):
-        grad_qkv_ref[:, block * D : (block + 1) * D] = gathered_ref[
-            block * D : (block + 1) * D, :
-        ].astype(jnp.float32)
-    grad_out_ref[...] = gathered_ref[3 * INNER :, :].astype(jnp.float32)
+        at = block * D
+        while at < (block + 1) * D:
+            end = min((block + 1) * D, (at // half_rows + 1) * half_rows)
+            grad_qkv_ref[at - block * D : end - block * D, block * D : (block + 1) * D] = rows(at, end)
+            at = end
+    grad_out_ref[...] = rows(3 * INNER, 4 * INNER)
 
 
 def whole(memory_space=pltpu.VMEM):
     return pl.BlockSpec(memory_space=memory_space)
 
 
-def spectrum(frames_here, widths_own, starts_own, audio, rim, gain, place):
-    rows, own = audio.shape
+def spectrum(band_at, band_widths, audio, rim, gain):
+    rows, own = audio.shape[0] * audio.shape[1], audio.shape[2]
+    frames_here = own // HOP
     total = rows * frames_here
-    own_bands = place.shape[1] // MAXW
+    own_bands = gain.shape[0]
     return pl.pallas_call(
-        lambda *refs: spectrum_kernel(frames_here, *refs),
-        out_shape=jax.ShapeDtypeStruct((own_bands * total // 2, FEAT), jnp.bfloat16),
-        in_specs=[whole(pltpu.SMEM)] * 2 + [whole()] * 7,
+        spectrum_kernel,
+        out_shape=jax.ShapeDtypeStruct((own_bands * CLIPS, frames_here, FEAT), jnp.bfloat16),
+        in_specs=[whole(pltpu.SMEM)] * 2 + [whole()] * 6,
         out_specs=whole(),
         scratch_shapes=[
             pltpu.VMEM((rows, WIN), jnp.float32),
@@ -287,33 +347,34 @@
         ],
         name="spectrum",
     )(
-        widths_own,
-        starts_own,
+        band_at.reshape(1),
+        band_widths,
         audio,
         rim,
         gain,
-        place,
         jnp.asarray(window_table()),
         jnp.asarray(twiddle_table()),
         jnp.asarray(inner_table()),
     )
 
 
-def layer(feats, weight, grads, norm_gain, qkv_weight, out_weight, factor_all):
+def layer(feats, weight, grads, norm_gain, qkv_weight, out_weight, core, factor_all):
     cosine, sine = rotary_table(np.arange(FRAMES))
     return pl.pallas_call(
         lambda *refs: layer_kernel(*refs, factor_all=factor_all),
         out_shape=(
             jax.ShapeDtypeStruct((FRAMES, D), jnp.bfloat16),
-            jax.ShapeDtypeStruct((4 * INNER, D), jnp.bfloat16),
+            jax.ShapeDtypeStruct((2 * INNER, D), jnp.bfloat16),
+            jax.ShapeDtypeStruct((2 * INNER, D), jnp.bfloat16),
         ),
-        in_specs=[whole()] * 8,
-        out_specs=(whole(),) * 2,
+        in_specs=[whole()] * 8 + [whole(pltpu.SMEM)],
+        out_specs=(whole(),) * 3,
         scratch_shapes=[
             pltpu.VMEM((FRAMES, INNER), jnp.bfloat16),
             pltpu.VMEM((FRAMES, INNER), jnp.bfloat16),
             pltpu.VMEM((FRAMES, INNER), jnp.bfloat16),
             pltpu.VMEM((FRAMES, 3 * INNER), jnp.bfloat16),
+            pltpu.VMEM((2, 2 * INNER, D), jnp.bfloat16),
         ],
         name="layer",
     )(
@@ -325,20 +386,21 @@
         out_weight,
         jnp.asarray(cosine),
         jnp.asarray(sine),
-    )
-
-
-def unpack(gathered):
+        core,
+    )
+
+
+def unpack(core, own, other):
     return pl.pallas_call(
         unpack_kernel,
         out_shape=(
             jax.ShapeDtypeStruct((D, 3 * INNER), jnp.float32),
             jax.ShapeDtypeStruct((INNER, D), jnp.float32),
         ),
-        in_specs=[whole()],
+        in_specs=[whole(pltpu.SMEM), whole(), whole()],
         out_specs=(whole(),) * 2,
         name="unpack",
-    )(gathered)
+    )(core, own, other)
 
 
 def exchange(blocks, axis):
@@ -361,17 +423,14 @@
     return exchange(blocks, axis).reshape(count * values.shape[0], values.shape[1])
 
 
-def body(
+def staged(
     audio_clips, band_widths, band_gain, band_weight, norm_gain, qkv_weight, out_weight, cotangent
 ):
-    tm = lax.axis_size("tm")
+    tm = lax.axis_size(TIME)
     band_at = lax.axis_index("x") * lax.axis_size("core") + lax.axis_index("core")
     own_bands = band_gain.shape[0]
     frame_block = audio_clips.shape[2] // HOP
-    audio = jnp.transpose(audio_clips, (1, 0, 2)).reshape(2 * CLIPS, -1)
-    rim = lax.ppermute(
-        audio[:, : WIN - HOP], "tm", [(source, source - 1) for source in range(1, tm)]
-    )
+    rim = lax.ppermute(audio_clips, TIME, [(source, source - 1) for source in range(1, tm)])
     sequences = own_bands * CLIPS
     rows = FEAT // tm
     early = jnp.concatenate(
@@ -383,59 +442,44 @@
         ],
         axis=1,
     )
-    early = exchange(early, "tm")
+    early = exchange(early, TIME)
     grads = early[:, :frame_block].reshape(FRAMES, D)
     weight = early[:, frame_block:].reshape(FEAT, D)
-    starts = jnp.cumsum(band_widths, dtype=jnp.int32) - band_widths
-    first_band = band_at * own_bands
-    widths_own = lax.dynamic_slice_in_dim(band_widths, first_band, own_bands)
-    starts_own = lax.dynamic_slice_in_dim(starts, first_band, own_bands)
-    within = lax.iota(jnp.int32, MAXW)[None, :]
-    place = jnp.where(within < widths_own[:, None], starts_own[:, None] + within, -1)
-    gain = jnp.transpose(band_gain.reshape(own_bands, MAXW, 4), (0, 2, 1))
-    normed = spectrum(
-        frame_block,
-        widths_own.reshape(1, own_bands),
-        starts_own.reshape(1, own_bands),
-        audio,
-        rim,
-        gain,
-        place.reshape(1, own_bands * MAXW),
-    )
-    feats = exchange(normed.reshape(sequences, frame_block, FEAT), "tm").reshape(FRAMES, FEAT)
+    normed = spectrum(band_at, band_widths, audio_clips, rim, band_gain)
+    feats = exchange(normed, TIME).reshape(FRAMES, FEAT)
     factor_all = 1.0 / math.sqrt(BANDS * CLIPS * FRAMES)
-    attended, partial = layer(
-        feats, weight, grads, norm_gain, qkv_weight, out_weight, factor_all
-    )
-    partial = scatter_sum(scatter_sum(partial, "core"), "x")
+    core = lax.axis_index("core").reshape(1)
+    attended, keep, send = layer(
+        feats, weight, grads, norm_gain, qkv_weight, out_weight, core, factor_all
+    )
+    swap = [(0, 1), (1, 0)]
+    partial = keep.astype(jnp.float32) + lax.ppermute(send, "core", swap).astype(jnp.float32)
+    partial = scatter_sum(partial.astype(jnp.bfloat16), "x")
     both = jnp.concatenate(
         [attended.reshape(tm, frame_block, D), partial.reshape(tm, -1, D)], axis=1
     )
-    both = exchange(both, "tm")
+    both = exchange(both, TIME)
     attended_out = both[:, :frame_block].reshape(own_bands, CLIPS, frame_block, D)
-    total = reduced(both[:, frame_block:])
-    for axis in ("tm", "x", "core"):
-        total = gather(total, axis)
-    grad_qkv, grad_out = unpack(total)
+    partial = gather(gather(reduced(both[:, frame_block:]), TIME), "x")
+    grad_qkv, grad_out = unpack(core, partial, lax.ppermute(partial, "core", swap))
     return (attended_out, grad_qkv, grad_out)
 
 
 def solution(mesh):
-    split = Mesh(mesh.devices.reshape(mesh.shape["tm"], -1, 2), ("tm", "x", "core"))
-    band = ("x", "core")
+    split = Mesh(mesh.devices.reshape(8, -1, 4, 2), TIME + BAND)
     return jax.shard_map(
-        body,
+        staged,
         mesh=split,
         in_specs=(
-            P(None, None, "tm"),
+            P(None, None, TIME),
             P(),
-            P(band, None),
-            P(band, "tm", None),
+            P(BAND, None),
+            P(BAND, TIME, None),
             P(),
             P(),
             P(),
-            P(band, None, "tm", None),
+            P(BAND, None, TIME, None),
         ),
-        out_specs=(P(band, None, "tm", None), P(), P()),
+        out_specs=(P(BAND, None, TIME, None), P(), P()),
         check_vma=False,
     )

time: 180 us -> 174 us (0.967)
  blocking collectives: 69.6 us -> 49.7 us
  starting transfers between devices: 29.3 us -> 41.4 us
  waiting for transfers between devices: 42.5 us -> 50.8 us
  local copies, waits for them, and re-layouts: 11.7 us -> 4.86 us
    all_to_all x5 -> x3, blocking collectives: 69.6 us -> 49.7 us  [exchange(): return lax.all_to_all(blocks, axis, split_axis=0, concat_axis=0, tiled=True)]
    ppermute x1 -> x3, starting transfers between devices: 1.42 us -> 14.5 us  [the longest x1 7.11 us: staged(): lax.ppermute(send, 'core', swap).astype(jnp.float32)]
    ppermute x1 -> x3, waiting for transfers between devices: 0.01 us -> 9.09 us  [the longest x1 5.1 us: staged(): lax.ppermute(audio_clips, TIME, [(source, source - 1) for source in range...]
    reshape x9 -> x5, local copies, waits for them, and re-layouts: 6.74 us -> 2.44 us  [the longest x1 0.86 us: staged(): weight = early[:, frame_block:].reshape(FEAT, D)]
    convert_element_type x0 -> x1, other arithmetic: none -> 2.25 us  [staged(): partial = scatter_sum(partial.astype(jnp.bfloat16), 'x')]
  transfers between devices with their start and end apart: 4 -> 6, of which waited for: 3 -> 6; matrix products, arithmetic and copies ran while one was open for 5% -> 1% of each run, Pallas kernels for 0% -> 0%
where the time goes in v3:
time: 174 us; the launch traced here: 173 us
  waiting for transfers between devices  50.8 us (29%)
  blocking collectives  49.7 us (29%)
  starting transfers between devices  41.4 us (24%)
  Pallas kernels  20.9 us (12%)
  local copies, waits for them, and re-layouts  4.86 us (3%)
  other arithmetic  4.6 us (3%)
    all_to_all x3, blocking collectives, exchange(): return lax.all_to_all(blocks, axis, split_axis=0, concat_axis=0, tiled=True)  49.7 us
    all_to_all x3, waiting for transfers between devices, exchange(): return lax.all_to_all(blocks, axis, split_axis=0, concat_axis=0, tiled=True)  41.7 us
    all_to_all x3, starting transfers between devices, exchange(): return lax.all_to_all(blocks, axis, split_axis=0, concat_axis=0, tiled=True)  26.9 us
    pallas_call x1, Pallas kernels, layer(): pl.pallas_call(lambda *refs: layer_kernel(*refs, factor_all=factor_all),...  11.5 us
    ppermute x1, starting transfers between devices, staged(): lax.ppermute(send, 'core', swap).astype(jnp.float32)  7.11 us
    pallas_call x1, Pallas kernels, spectrum(): pl.pallas_call(spectrum_kernel, out_shape=jax.ShapeDtypeStruct((own_bands...  6.24 us
    ppermute x1, starting transfers between devices, staged(): lax.ppermute(partial, 'core', swap)  5.97 us
    ppermute x1, waiting for transfers between devices, staged(): lax.ppermute(audio_clips, TIME, [(source, source - 1) for source in range...  5.1 us
  transfers between devices with their start and end apart: 6, of which 6 were waited for; matrix products, arithmetic and copies ran while one was open for 1% of the time, Pallas kernels for 0%

profile of v3, /device:TPU:1, one launch (start us, length us, event | category | flops | bytes accessed | tf_op | source)
XLA Modules:
  0.0 173.1 jit_solution(16601338961704483406)
XLA Ops:
  0.6 0.0 copy-start.3
  0.6 0.0 copy-start.5
  0.7 1.4 collective-permute-start
  2.1 5.1 %collective-permute-done.rim_ref = f32[8,2,1764]{2,1,0:T(2,128)S(1)} collective-permute-done((f32[8,2,1764]{2,1,0:T(2,128)}, f32[8,2,1764]{2,1,0:T(2,128)S(1)}, u32[]{:S(2)}, u32[]{:S(2)}) %collective-permute-start) | collective-permute-done | bytes 112928 | tf_op jit(solution)/shard_map/ppermute | solution.py:433
  7.2 0.0 copy-start.4
  7.2 0.6 copy-done.4
  7.8 6.2 %spectrum.1 = bf16[64,4,512]{2,1,0:T(4,128)(2,1)} custom-call(s32[1]{0:T(128)} %bitcast.place_ref, s32[64]{0:T(128)} %widths_ref.1, f32[8,2,1764]{2,1,0:T(2,128)} %audio_ref.1, f32[8,2,1764]{2,1,0:T(2,128)} %copy-done.4, f32[8,512]{1,0:T(8,128)} %gain_ref.1, f32[1,2048]{1,0:T(1,128)} %constant.24.clone.taper_ref, f32[16,256]{1,0:T(8,128)} %constant.25.clone.twiddle_ref, ...), custom_call_target="tpu_custom_call" | custom-call | tf_op jit(solution)/shard_map/spectrum/pallas_call | solution.py:335
  14.1 16.9 %all-to-all-start = ((bf16[64,4,512]{2,1,0:T(4,128)(2,1)}), bf16[64,4,512]{2,1,0:T(4,128)(2,1)S(1)}, u32[]{:S(2)}, u32[]{:S(2)}) async-start(bf16[64,4,512]{2,1,0:T(4,128)(2,1)} %spectrum.1), calls=%async_computation | async-start | bytes 524288 | tf_op jit(solution)/shard_map/all_to_all | solution.py:407
  30.9 0.0 copy-done.5
  31.0 0.0 copy-start.6
  31.0 0.0 copy-done.3
  31.0 1.2 pad_maximum_fusion
  32.2 11.2 %all-to-all-done = bf16[64,4,512]{2,1,0:T(4,128)(2,1)S(1)} async-done(((bf16[64,4,512]{2,1,0:T(4,128)(2,1)}), bf16[64,4,512]{2,1,0:T(4,128)(2,1)S(1)}, u32[]{:S(2)}, u32[]{:S(2)}) %all-to-all-start) | async-done | bytes 262176 | tf_op jit(solution)/shard_map/all_to_all | solution.py:407
  43.4 5.8 %all-to-all-start.1 = ((bf16[64,12,384]{2,1,0:T(8,128)(2,1)}), bf16[64,12,384]{2,1,0:T(8,128)(2,1)S(1)}, u32[]{:S(2)}, u32[]{:S(2)}) async-start(bf16[64,12,384]{2,1,0:T(8,128)(2,1)} %pad_maximum_fusion), calls=%async_computation.1 | async-start | bytes 1572864 | tf_op jit(solution)/shard_map/all_to_all | solution.py:407
  49.3 0.0 copy-done.6
  49.3 0.6 reshape.54.refs_3_
  49.8 0.8 reshape.49.refs_0_
  50.6 18.8 %all-to-all-done.1 = bf16[64,12,384]{2,1,0:T(8,128)(2,1)S(1)} async-done(((bf16[64,12,384]{2,1,0:T(8,128)(2,1)}), bf16[64,12,384]{2,1,0:T(8,128)(2,1)S(1)}, u32[]{:S(2)}, u32[]{:S(2)}) %all-to-all-start.1) | async-done | bytes 589856 | tf_op jit(solution)/shard_map/all_to_all | solution.py:407
  69.4 0.1 slice.17
  69.5 0.7 reshape.53.refs_2_
  70.2 0.9 slice_bitcast_fusion.refs_1_
  71.0 11.5 %layer.1 = (bf16[256,384]{1,0:T(8,128)(2,1)}, bf16[1024,384]{1,0:T(8,128)(2,1)}, bf16[1024,384]{1,0:T(8,128)(2,1)}) custom-call(bf16[256,512]{1,0:T(8,128)(2,1)} %reshape.49.refs_0_, bf16[512,384]{1,0:T(8,128)(2,1)} %slice_bitcast_fusion.refs_1_, bf16[256,384]{1,0:T(8,128)(2,1)} %reshape.53.refs_2_, f32[1,384]{1,0:T(1,128)} %reshape.54.refs_3_, ...), custom_call_target="tpu_custom_call" | custom-call | tf_op jit(solution)/shard_map/layer/pallas_call | solution.py:363
  82.5 7.1 %collective-permute-start.1 = (bf16[1024,384]{1,0:T(8,128)(2,1)}, bf16[1024,384]{1,0:T(8,128)(2,1)S(1)}, u32[]{:S(2)}, u32[]{:S(2)}) collective-permute-start(bf16[1024,384]{1,0:T(8,128)(2,1)} %get-tuple-element.10), channel_id=1, source_target_pairs={{0,1},{1,0},{2,3},{3,2},{4,5},{5,4},{6,7},{7,6},{8,9},{9,8},{10,11... | collective-permute-start | bytes 2359304 | tf_op jit(solution)/shard_map/ppermute | solution.py:456
  89.6 2.1 %collective-permute-done.1 = bf16[1024,384]{1,0:T(8,128)(2,1)S(1)} collective-permute-done((bf16[1024,384]{1,0:T(8,128)(2,1)}, bf16[1024,384]{1,0:T(8,128)(2,1)S(1)}, u32[]{:S(2)}, u32[]{:S(2)}) %collective-permute-start.1) | collective-permute-done | bytes 786464 | tf_op jit(solution)/shard_map/ppermute | solution.py:456
  91.7 0.0 copy-start.2
  91.7 2.2 %add_convert_fusion = bf16[1024,384]{1,0:T(8,128)(2,1)} fusion(bf16[1024,384]{1,0:T(8,128)(2,1)S(1)} %collective-permute-done.1, bf16[1024,384]{1,0:T(8,128)(2,1)} %get-tuple-element.9), kind=kLoop, calls=%fused_computation | loop fusion | flops 1572864 | bytes 2359296 | tf_op jit(solution)/shard_map/convert_element_type | solution.py:457
  94.0 4.2 %all-to-all-start.2 = ((bf16[4,256,384]{2,1,0:T(8,128)(2,1)}), bf16[4,256,384]{2,1,0:T(8,128)(2,1)S(1)}, u32[]{:S(2)}, u32[]{:S(2)}) async-start(bf16[4,256,384]{2,1,0:T(8,128)(2,1)} %bitcast.5), calls=%async_computation.2 | async-start | bytes 1572864 | tf_op jit(solution)/shard_map/all_to_all | solution.py:407
  98.2 0.0 copy-done.2
  98.2 0.1 reshape.56
  98.2 11.7 %all-to-all-done.2 = bf16[4,256,384]{2,1,0:T(8,128)(2,1)S(1)} async-done(((bf16[4,256,384]{2,1,0:T(8,128)(2,1)}), bf16[4,256,384]{2,1,0:T(8,128)(2,1)S(1)}, u32[]{:S(2)}, u32[]{:S(2)}) %all-to-all-start.2) | async-done | bytes 786464 | tf_op jit(solution)/shard_map/all_to_all | solution.py:407
  109.9 0.2 reduce_sum.24
  110.0 0.1 reshape.58
  110.1 0.2 pad_maximum_fusion.1
  110.3 19.5 %all_to_all.30 = bf16[64,8,384]{2,1,0:T(8,128)(2,1)S(1)} all-to-all(bf16[64,8,384]{2,1,0:T(8,128)(2,1)S(1)} %pad_maximum_fusion.1), channel_id=1, replica_groups=mesh['z'=8,'y'=8,'x'=4,'core'=2] {'z','y'}, dimensions={0} | all-to-all | bytes 786432 | tf_op jit(solution)/shard_map/all_to_all | solution.py:407
  129.8 0.8 slice_reduce_fusion
  130.6 0.1 broadcast_in_dim.9
  130.7 18.7 %all_to_all.31 = bf16[64,4,384]{2,1,0:T(4,128)(2,1)S(1)} all-to-all(bf16[64,4,384]{2,1,0:T(4,128)(2,1)S(1)} %broadcast_in_dim.9), channel_id=1, replica_groups=mesh['z'=8,'y'=8,'x'=4,'core'=2] {'z','y'}, dimensions={0} | all-to-all | bytes 393216 | tf_op jit(solution)/shard_map/all_to_all | solution.py:407
  149.4 0.1 broadcast_in_dim.10
  149.4 0.1 broadcast_in_dim.22
  149.5 11.6 %all_to_all.32 = bf16[4,256,384]{2,1,0:T(8,128)(2,1)S(1)} all-to-all(bf16[4,256,384]{2,1,0:T(8,128)(2,1)S(1)} %broadcast_in_dim.22), channel_id=1, replica_groups=mesh['z'=8,'y'=8,'x'=4,'core'=2] {'x'}, dimensions={0} | all-to-all | bytes 1572864 | tf_op jit(solution)/shard_map/all_to_all | solution.py:407
  161.1 0.0 copy-start
  161.1 6.0 %collective-permute-start.2 = (bf16[1024,384]{1,0:T(8,128)(2,1)S(1)}, bf16[1024,384]{1,0:T(8,128)(2,1)S(1)}, u32[]{:S(2)}, u32[]{:S(2)}) collective-permute-start(bf16[1024,384]{1,0:T(8,128)(2,1)S(1)} %bitcast.9), channel_id=1, source_target_pairs={{0,1},{1,0},{2,3},{3,2},{4,5},{5,4},{6,7},{7,6},{8,9},{9,8},{10,11... | collective-permute-start | bytes 2359304 | tf_op jit(solution)/shard_map/ppermute | solution.py:464
  167.0 1.9 %collective-permute-done.2.other_ref = bf16[1024,384]{1,0:T(8,128)(2,1)S(1)} collective-permute-done((bf16[1024,384]{1,0:T(8,128)(2,1)S(1)}, bf16[1024,384]{1,0:T(8,128)(2,1)S(1)}, u32[]{:S(2)}, u32[]{:S(2)}) %collective-permute-start.2) | collective-permute-done | bytes 786464 | tf_op jit(solution)/shard_map/ppermute | solution.py:464
  168.9 0.0 copy-done
  168.9 0.0 copy-start.1
  168.9 0.9 copy-done.1
  169.9 3.2 %unpack.1 = (f32[384,1536]{1,0:T(8,128)}, f32[512,384]{1,0:T(8,128)}) custom-call(s32[1]{0:T(128)} %bitcast.4.refs_8_.core_ref, bf16[1024,384]{1,0:T(8,128)(2,1)} %bitcast.10, bf16[1024,384]{1,0:T(8,128)(2,1)} %copy-done.1), custom_call_target="tpu_custom_call" | custom-call | tf_op jit(solution)/shard_map/unpack/pallas_call | solution.py:394
  (1 shorter events, 0.0 us)
Async XLA Ops:
  0.6 30.4 %copy-start.3 = (bf16[8,8,4,384]{3,2,1,0:T(4,128)(2,1)S(1)}, bf16[8,8,4,384]{3,2,1,0:T(4,128)(2,1)}, u32[]{:S(2)}) copy-start(bf16[8,8,4,384]{3,2,1,0:T(4,128)(2,1)} %param.20) | copy-start | bytes 589828
  0.6 30.3 %copy-start.5 = (bf16[8,8,384]{2,1,0:T(8,128)(2,1)S(1)}, bf16[8,8,384]{2,1,0:T(8,128)(2,1)}, u32[]{:S(2)}) copy-start(bf16[8,8,384]{2,1,0:T(8,128)(2,1)} %param.16) | copy-start | bytes 147460
  0.7 6.5 %collective-permute-start = (f32[8,2,1764]{2,1,0:T(2,128)}, f32[8,2,1764]{2,1,0:T(2,128)S(1)}, u32[]{:S(2)}, u32[]{:S(2)}) collective-permute-start(f32[8,2,1764]{2,1,0:T(2,128)} %audio_ref.1), channel_id=1, source_target_pairs={{8,0},{16,8},{24,16},{32,24},{40,32},{48,40},{56,48},{64,56},{72,6... | collective-permute-start | bytes 338696 | tf_op jit(solution)/shard_map/ppermute | solution.py:433
  7.2 0.6 copy-start.4
  14.1 29.3 %all-to-all-start = ((bf16[64,4,512]{2,1,0:T(4,128)(2,1)}), bf16[64,4,512]{2,1,0:T(4,128)(2,1)S(1)}, u32[]{:S(2)}, u32[]{:S(2)}) async-start(bf16[64,4,512]{2,1,0:T(4,128)(2,1)} %spectrum.1), calls=%async_computation | async-start | bytes 524288 | tf_op jit(solution)/shard_map/all_to_all | solution.py:407
  31.0 18.3 %copy-start.6 = (f32[384]{0:T(512)S(1)}, f32[384]{0:T(512)}, u32[]{:S(2)}) copy-start(f32[384]{0:T(512)} %param.17) | copy-start | bytes 4612
  43.4 26.0 %all-to-all-start.1 = ((bf16[64,12,384]{2,1,0:T(8,128)(2,1)}), bf16[64,12,384]{2,1,0:T(8,128)(2,1)S(1)}, u32[]{:S(2)}, u32[]{:S(2)}) async-start(bf16[64,12,384]{2,1,0:T(8,128)(2,1)} %pad_maximum_fusion), calls=%async_computation.1 | async-start | bytes 1572864 | tf_op jit(solution)/shard_map/all_to_all | solution.py:407
  82.5 9.2 %collective-permute-start.1 = (bf16[1024,384]{1,0:T(8,128)(2,1)}, bf16[1024,384]{1,0:T(8,128)(2,1)S(1)}, u32[]{:S(2)}, u32[]{:S(2)}) collective-permute-start(bf16[1024,384]{1,0:T(8,128)(2,1)} %get-tuple-element.10), channel_id=1, source_target_pairs={{0,1},{1,0},{2,3},{3,2},{4,5},{5,4},{6,7},{7,6},{8,9},{9,8},{10,11... | collective-permute-start | bytes 2359304 | tf_op jit(solution)/shard_map/ppermute | solution.py:456
  91.7 6.4 %copy-start.2 = (bf16[256,384]{1,0:T(8,128)(2,1)S(1)}, bf16[256,384]{1,0:T(8,128)(2,1)}, u32[]{:S(2)}) copy-start(bf16[256,384]{1,0:T(8,128)(2,1)} %get-tuple-element.8) | copy-start | bytes 589828
  94.0 15.9 %all-to-all-start.2 = ((bf16[4,256,384]{2,1,0:T(8,128)(2,1)}), bf16[4,256,384]{2,1,0:T(8,128)(2,1)S(1)}, u32[]{:S(2)}, u32[]{:S(2)}) async-start(bf16[4,256,384]{2,1,0:T(8,128)(2,1)} %bitcast.5), calls=%async_computation.2 | async-start | bytes 1572864 | tf_op jit(solution)/shard_map/all_to_all | solution.py:407
  161.1 7.9 %copy-start = (bf16[4,256,384]{2,1,0:T(8,128)(2,1)}, bf16[4,256,384]{2,1,0:T(8,128)(2,1)S(1)}, u32[]{:S(2)}) copy-start(bf16[4,256,384]{2,1,0:T(8,128)(2,1)S(1)} %all_to_all.32) | copy-start | bytes 2359300
  161.1 7.9 %collective-permute-start.2 = (bf16[1024,384]{1,0:T(8,128)(2,1)S(1)}, bf16[1024,384]{1,0:T(8,128)(2,1)S(1)}, u32[]{:S(2)}, u32[]{:S(2)}) collective-permute-start(bf16[1024,384]{1,0:T(8,128)(2,1)S(1)} %bitcast.9), channel_id=1, source_target_pairs={{0,1},{1,0},{2,3},{3,2},{4,5},{5,4},{6,7},{7,6},{8,9},{9,8},{10,11... | collective-permute-start | bytes 2359304 | tf_op jit(solution)/shard_map/ppermute | solution.py:464
  168.9 0.9 copy-start.1

commit v4 on v3

--- a/solution.py
+++ b/solution.py
@@ -194,133 +194,177 @@
                 ).astype(jnp.bfloat16)
 
 
-def swap_halves(values):
-    width = values.shape[1]
-    lane = lax.broadcasted_iota(jnp.int32, values.shape, 1)
-    forward = pltpu.roll(values, width - HDIM // 2, 1)
-    backward = pltpu.roll(values, HDIM // 2, 1)
-    return jnp.where(lane % HDIM < HDIM // 2, forward, backward)
-
-
 def dot(left, right, dims=((1,), (0,))):
     return lax.dot_general(left, right, (dims, ((), ())), preferred_element_type=jnp.float32)
 
 
+def split_heads(values):
+    low = lax.broadcasted_iota(jnp.int32, values.shape, 1) < HDIM
+    return (
+        jnp.where(low, values, 0.0).astype(jnp.bfloat16),
+        jnp.where(low, 0.0, values).astype(jnp.bfloat16),
+    )
+
+
+def prepare_kernel(weight_ref, grads_ref, qkv_ref, outw_ref, embed_ref, heads_ref, swapped_ref):
+    natural = lax.broadcasted_iota(jnp.int32, (FEAT, FEAT), 1)
+    wanted = lax.broadcasted_iota(jnp.int32, (FEAT, FEAT), 0)
+    order = one_hot(natural == (wanted % MAXW) * 4 + wanted // MAXW)
+    embed_ref[...] = dot(order, weight_ref[...]).astype(jnp.bfloat16)
+    grad_mixed = dot(grads_ref[...], outw_ref[...], ((1,), (1,)))
+    for pair in range(HEADS // 2):
+        low, high = split_heads(grad_mixed[:, pair * 128 : (pair + 1) * 128])
+        heads_ref[pair, :FRAMES, :] = low
+        heads_ref[pair, FRAMES:, :] = high
+    row = lax.broadcasted_iota(jnp.int32, (128, 128), 0)
+    lane = lax.broadcasted_iota(jnp.int32, (128, 128), 1)
+    swap = one_hot(row == lane + jnp.where(lane % HDIM < HDIM // 2, HDIM // 2, -(HDIM // 2)))
+    for block in range(2 * INNER // 128):
+        cols = slice(block * 128, (block + 1) * 128)
+        swapped_ref[:, cols] = dot(qkv_ref[:, cols], swap).astype(jnp.bfloat16)
+
+
 def layer_kernel(
+    core_ref,
     feats_ref,
-    weight_ref,
-    grads_ref,
+    embed_ref,
     gain_ref,
-    qkv_ref,
-    outw_ref,
-    cos_ref,
-    sin_ref,
-    core_ref,
+    qkv_hbm,
+    swapped_hbm,
+    cos_hbm,
+    sin_hbm,
+    heads_hbm,
+    outw_hbm,
+    grads_hbm,
     attended_ref,
     keep_ref,
     send_ref,
-    query_s,
-    key_s,
+    qkv_ref,
+    swapped_ref,
+    cos_ref,
+    sin_ref,
+    heads_ref,
+    outw_ref,
+    grads_ref,
     mixed_s,
     gproj_s,
     halves,
+    sems,
     *,
     factor_all,
 ):
-    natural = lax.broadcasted_iota(jnp.int32, (FEAT, FEAT), 1)
-    wanted = lax.broadcasted_iota(jnp.int32, (FEAT, FEAT), 0)
-    wanted = (wanted % MAXW) * 4 + wanted // MAXW
-    order = jnp.where(natural == wanted, 1.0, 0.0).astype(jnp.bfloat16)
-    weight = dot(order, weight_ref[...]).astype(jnp.bfloat16)
-    x = dot(feats_ref[...], weight).astype(jnp.bfloat16).astype(jnp.float32)
+    pairs = (
+        (qkv_hbm, qkv_ref),
+        (swapped_hbm, swapped_ref),
+        (cos_hbm, cos_ref),
+        (sin_hbm, sin_ref),
+        (heads_hbm, heads_ref),
+        (outw_hbm, outw_ref),
+        (grads_hbm, grads_ref),
+    )
+    copies = [
+        pltpu.make_async_copy(source, target, sems.at[at])
+        for at, (source, target) in enumerate(pairs)
+    ]
+    for copy in copies:
+        copy.start()
+    x = dot(feats_ref[...], embed_ref[...]).astype(jnp.bfloat16).astype(jnp.float32)
     scale = lax.rsqrt(jnp.mean(x * x, axis=1, keepdims=True) + 1e-06)
     normed_x = (x * scale * gain_ref[...]).astype(jnp.bfloat16)
+    for copy in copies[:4]:
+        copy.wait()
     factor = 1.0 / math.sqrt(HDIM)
     cosine = cos_ref[...]
     sine = sin_ref[...]
-    qk = dot(normed_x, qkv_ref[:, : 2 * INNER])
-    for block in range(INNER // 128):
-        cols = slice(block * 128, (block + 1) * 128)
-        q = qk[:, cols]
-        k = qk[:, INNER + block * 128 : INNER + (block + 1) * 128]
-        query_s[:, cols] = ((q * cosine + swap_halves(q) * sine) * factor).astype(jnp.bfloat16)
-        key_s[:, cols] = (k * cosine + swap_halves(k) * sine).astype(jnp.bfloat16)
-    value_b = dot(normed_x, qkv_ref[:, 2 * INNER :]).astype(jnp.bfloat16)
-    grad_mixed = dot(grads_ref[...], outw_ref[...], ((1,), (1,))).astype(jnp.bfloat16)
-    for pair in range(HEADS // 2):
+    for copy in copies[4:]:
+        copy.wait()
+
+    def opened(pair):
         cols = slice(pair * 128, (pair + 1) * 128)
-        results = []
-        for side in range(2):
-            head = slice(side * HDIM, (side + 1) * HDIM)
-            head_q = query_s[:, cols][:, head]
-            head_k = key_s[:, cols][:, head]
-            head_v = value_b[:, cols][:, head]
-            head_g = grad_mixed[:, cols][:, head]
-            scores = dot(head_q, head_k, ((1,), (1,)))
-            peak = jnp.max(scores, axis=1, keepdims=True)
-            expo = jnp.exp(scores - peak)
-            probs = expo / jnp.sum(expo, axis=1, keepdims=True)
-            probs_b = probs.astype(jnp.bfloat16)
-            mixed = dot(probs_b, head_v)
-            grad_p = dot(head_g, head_v, ((1,), (1,)))
-            grad_v = dot(probs_b, head_g, ((0,), (0,)))
-            row_dot = jnp.sum(probs * grad_p, axis=1, keepdims=True)
-            grad_s = (probs * (grad_p - row_dot)).astype(jnp.bfloat16)
-            grad_q = dot(grad_s, head_k)
-            grad_k = dot(grad_s, head_q, ((0,), (0,)))
-            results.append((mixed, grad_q, grad_k, grad_v))
-        mixed, grad_q, grad_k, grad_v = (
-            jnp.concatenate([low, high], axis=1) for low, high in zip(*results)
+        after = slice(INNER + pair * 128, INNER + (pair + 1) * 128)
+        q, k, v = (
+            dot(normed_x, qkv_ref[:, part * INNER + pair * 128 : part * INNER + (pair + 1) * 128])
+            for part in range(3)
         )
+        q_swap = dot(normed_x, swapped_ref[:, cols])
+        k_swap = dot(normed_x, swapped_ref[:, after])
+        query = split_heads((q * cosine + q_swap * sine) * factor)
+        query_swap = split_heads((q_swap * cosine - q * sine) * factor)
+        turned = k * cosine + k_swap * sine
+        key = split_heads(turned)
+        key_swap = split_heads(k_swap * cosine - k * sine)
+        value = split_heads(v)
+        stacked = jnp.concatenate(query, axis=0)
+        scores = dot(stacked, turned.astype(jnp.bfloat16), ((1,), (1,)))
+        grad_p = dot(heads_ref[pair], v.astype(jnp.bfloat16), ((1,), (1,)))
+        both_q = jnp.concatenate([stacked, jnp.concatenate(query_swap, axis=0)], axis=1)
+        both_k = [jnp.concatenate([a, b], axis=1) for a, b in zip(key, key_swap)]
+        return scores, grad_p, both_q, both_k, value
+
+    def closed(pair, scores, grad_p, both_q, both_k, value):
+        cols = slice(pair * 128, (pair + 1) * 128)
+        peak = jnp.max(scores, axis=1, keepdims=True)
+        expo = jnp.exp(scores - peak)
+        probs = expo / jnp.sum(expo, axis=1, keepdims=True)
+        probs_b = probs.astype(jnp.bfloat16)
+        row_dot = jnp.sum(probs * grad_p, axis=1, keepdims=True)
+        grad_s = (probs * (grad_p - row_dot)).astype(jnp.bfloat16)
+        mixed = dot(probs_b[:FRAMES], value[0]) + dot(probs_b[FRAMES:], value[1])
+        grad_v = dot(probs_b, heads_ref[pair], ((0,), (0,)))
+        grad_q = (dot(grad_s[:FRAMES], both_k[0]) + dot(grad_s[FRAMES:], both_k[1])) * factor
+        grad_k = dot(grad_s, both_q, ((0,), (0,)))
         mixed_s[:, cols] = mixed.astype(jnp.bfloat16)
-        grad_q = grad_q * factor
-        gproj_s[:, cols] = (grad_q * cosine - swap_halves(grad_q) * sine).astype(jnp.bfloat16)
-        gproj_s[:, INNER + pair * 128 : INNER + (pair + 1) * 128] = (
-            grad_k * cosine - swap_halves(grad_k) * sine
-        ).astype(jnp.bfloat16)
+        for part, grad in enumerate((grad_q, grad_k)):
+            turned = grad[:, :128] * cosine - grad[:, 128:] * sine
+            gproj_s[:, part * INNER + pair * 128 : part * INNER + (pair + 1) * 128] = turned.astype(
+                jnp.bfloat16
+            )
         gproj_s[:, 2 * INNER + pair * 128 : 2 * INNER + (pair + 1) * 128] = grad_v.astype(
             jnp.bfloat16
         )
+
+    ready = opened(0)
+    for pair in range(HEADS // 2):
+        following = opened(pair + 1) if pair + 1 < HEADS // 2 else None
+        closed(pair, *ready)
+        ready = following
     mixed_b = mixed_s[...]
     attended_ref[...] = (x + dot(mixed_b, outw_ref[...])).astype(jnp.bfloat16)
     core = core_ref[0]
-    half_rows = 2 * INNER
 
     def place(first, values):
         values = (values * factor_all).astype(jnp.bfloat16)
-        at = first
-        while at < first + D:
-            half, row = divmod(at, half_rows)
-            end = min(first + D, (half + 1) * half_rows)
-            slot = core if half == 0 else 1 - core
-            halves[slot, row : row + end - at, :] = values[at - first : end - first]
-            at = end
+        rows = values.shape[0] // 2
+        halves[core, first : first + rows, :] = values[:rows]
+        halves[1 - core, first : first + rows, :] = values[rows:]
 
     for block in range(3 * INNER // D):
-        place(block * D, dot(normed_x, gproj_s[:, block * D : (block + 1) * D], ((0,), (0,))))
-    part = dot(mixed_b, grads_ref[...], ((0,), (0,))) * factor_all
-    halves[1 - core, half_rows - INNER :, :] = part.astype(jnp.bfloat16)
+        place(
+            block * D // 2, dot(normed_x, gproj_s[:, block * D : (block + 1) * D], ((0,), (0,)))
+        )
+    place(3 * INNER // 2, dot(mixed_b, grads_ref[...], ((0,), (0,))))
     keep_ref[...] = halves[0]
     send_ref[...] = halves[1]
 
 
-def unpack_kernel(core_ref, own_ref, other_ref, grad_qkv_ref, grad_out_ref):
-    half_rows = own_ref.shape[0]
-    first = core_ref[0] == 0
-
-    def rows(start, stop):
-        half = start // half_rows
-        at = slice(start - half * half_rows, stop - half * half_rows)
-        own, other = own_ref[at, :], other_ref[at, :]
-        return lax.select(first, *((own, other) if half == 0 else (other, own))).astype(jnp.float32)
-
+def unpack_kernel(core_ref, half_ref, *refs):
+    grad_qkv_hbm, grad_out_hbm, wide, tall, sems = refs[-5:]
+    rows = wide.shape[0]
     for block in range(3 * INNER // D):
-        at = block * D
-        while at < (block + 1) * D:
-            end = min((block + 1) * D, (at // half_rows + 1) * half_rows)
-            grad_qkv_ref[at - block * D : end - block * D, block * D : (block + 1) * D] = rows(at, end)
-            at = end
-    grad_out_ref[...] = rows(3 * INNER, 4 * INNER)
+        wide[:, block * D : (block + 1) * D] = half_ref[
+            block * rows : (block + 1) * rows, :
+        ].astype(jnp.float32)
+    tall[...] = half_ref[3 * INNER // D * rows :, :].astype(jnp.float32)
+    core = core_ref[0]
+    copies = []
+    for at, (source, target) in enumerate(((wide, grad_qkv_hbm), (tall, grad_out_hbm))):
+        count = source.shape[0]
+        place = target.at[pl.ds(pl.multiple_of(core * count, count), count), :]
+        copies.append(pltpu.make_async_copy(source, place, sems.at[at]))
+    for copy in copies:
+        copy.start()
+    for copy in copies:
+        copy.wait()
 
 
 def whole(memory_space=pltpu.VMEM):
@@ -358,8 +402,32 @@
     )
 
 
-def layer(feats, weight, grads, norm_gain, qkv_weight, out_weight, core, factor_all):
+def prepare(weight, grads, qkv_weight, out_weight):
+    return pl.pallas_call(
+        prepare_kernel,
+        out_shape=(
+            jax.ShapeDtypeStruct((FEAT, D), jnp.bfloat16),
+            jax.ShapeDtypeStruct((HEADS // 2, 2 * FRAMES, 128), jnp.bfloat16),
+            jax.ShapeDtypeStruct((D, 2 * INNER), jnp.bfloat16),
+        ),
+        in_specs=[whole()] * 4,
+        out_specs=(whole(),) * 3,
+        name="prepare",
+    )(weight, grads, qkv_weight, out_weight)
+
+
+def layer(core, feats, prepared, grads, norm_gain, qkv_weight, out_weight, factor_all):
+    embed, heads, swapped = prepared
     cosine, sine = rotary_table(np.arange(FRAMES))
+    later = (
+        qkv_weight,
+        swapped,
+        jnp.asarray(cosine),
+        jnp.asarray(sine),
+        heads,
+        out_weight,
+        grads,
+    )
     return pl.pallas_call(
         lambda *refs: layer_kernel(*refs, factor_all=factor_all),
         out_shape=(
@@ -367,40 +435,36 @@
             jax.ShapeDtypeStruct((2 * INNER, D), jnp.bfloat16),
             jax.ShapeDtypeStruct((2 * INNER, D), jnp.bfloat16),
         ),
-        in_specs=[whole()] * 8 + [whole(pltpu.SMEM)],
+        in_specs=[whole(pltpu.SMEM)] + [whole()] * 3 + [whole(pl.ANY)] * len(later),
         out_specs=(whole(),) * 3,
-        scratch_shapes=[
-            pltpu.VMEM((FRAMES, INNER), jnp.bfloat16),
-            pltpu.VMEM((FRAMES, INNER), jnp.bfloat16),
+        scratch_shapes=[pltpu.VMEM(value.shape, value.dtype) for value in later]
+        + [
             pltpu.VMEM((FRAMES, INNER), jnp.bfloat16),
             pltpu.VMEM((FRAMES, 3 * INNER), jnp.bfloat16),
             pltpu.VMEM((2, 2 * INNER, D), jnp.bfloat16),
+            pltpu.SemaphoreType.DMA((len(later),)),
         ],
         name="layer",
-    )(
-        feats,
-        weight,
-        grads,
-        norm_gain.reshape(1, D),
-        qkv_weight,
-        out_weight,
-        jnp.asarray(cosine),
-        jnp.asarray(sine),
-        core,
-    )
-
-
-def unpack(core, own, other):
+    )(core, feats, embed, norm_gain.reshape(1, D), *later)
+
+
+def unpack(core, half, filled=()):
     return pl.pallas_call(
         unpack_kernel,
         out_shape=(
             jax.ShapeDtypeStruct((D, 3 * INNER), jnp.float32),
             jax.ShapeDtypeStruct((INNER, D), jnp.float32),
         ),
-        in_specs=[whole(pltpu.SMEM), whole(), whole()],
-        out_specs=(whole(),) * 2,
+        in_specs=[whole(pltpu.SMEM), whole()] + [whole(pl.ANY)] * len(filled),
+        out_specs=(whole(pl.ANY),) * 2,
+        input_output_aliases={2 + at: at for at in range(len(filled))},
+        scratch_shapes=[
+            pltpu.VMEM((D // 2, 3 * INNER), jnp.float32),
+            pltpu.VMEM((INNER // 2, D), jnp.float32),
+            pltpu.SemaphoreType.DMA((2,)),
+        ],
         name="unpack",
-    )(core, own, other)
+    )(core, half, *filled)
 
 
 def exchange(blocks, axis):
@@ -449,8 +513,9 @@
     feats = exchange(normed, TIME).reshape(FRAMES, FEAT)
     factor_all = 1.0 / math.sqrt(BANDS * CLIPS * FRAMES)
     core = lax.axis_index("core").reshape(1)
+    prepared = prepare(weight, grads, qkv_weight, out_weight)
     attended, keep, send = layer(
-        feats, weight, grads, norm_gain, qkv_weight, out_weight, core, factor_all
+        core, feats, prepared, grads, norm_gain, qkv_weight, out_weight, factor_all
     )
     swap = [(0, 1), (1, 0)]
     partial = keep.astype(jnp.float32) + lax.ppermute(send, "core", swap).astype(jnp.float32)
@@ -461,7 +526,9 @@
     both = exchange(both, TIME)
     attended_out = both[:, :frame_block].reshape(own_bands, CLIPS, frame_block, D)
     partial = gather(gather(reduced(both[:, frame_block:]), TIME), "x")
-    grad_qkv, grad_out = unpack(core, partial, lax.ppermute(partial, "core", swap))
+    other = lax.ppermute(partial, "core", swap)
+    filled = unpack(core, partial)
+    grad_qkv, grad_out = unpack(1 - core, other, filled)
     return (attended_out, grad_qkv, grad_out)
 
 

time: 174 us -> 174 us (level)
  waiting for transfers between devices: 50.8 us -> 48.9 us
  Pallas kernels: 20.9 us -> 22.7 us
    pallas_call x0 -> x1, Pallas kernels: none -> 3.24 us  [prepare(): pl.pallas_call(prepare_kernel, out_shape=(jax.ShapeDtypeStruct((FEAT, D),...]
    pallas_call x1, Pallas kernels: 11.5 us -> 8.55 us  [layer(): pl.pallas_call(lambda *refs: layer_kernel(*refs, factor_all=factor_all),...]
    ppermute x1, waiting for transfers between devices: 1.89 us -> 0.01 us  [staged(): other = lax.ppermute(partial, 'core', swap)]
    pallas_call x1 -> x2, Pallas kernels: 3.21 us -> 4.72 us  [unpack(): pl.pallas_call(unpack_kernel, out_shape=(jax.ShapeDtypeStruct((D, 3 * INN...]
  transfers between devices with their start and end apart: 6 -> 6, of which waited for: 6 -> 5; matrix products, arithmetic and copies ran while one was open for 1% -> 2% of each run, Pallas kernels for 0% -> 1%
where the time goes in v4:
time: 174 us; the launch traced here: 173 us
  blocking collectives  49.7 us (29%)
  waiting for transfers between devices  48.9 us (28%)
  starting transfers between devices  41.4 us (24%)
  Pallas kernels  22.7 us (13%)
  local copies, waits for them, and re-layouts  4.88 us (3%)
  other arithmetic  4.6 us (3%)
    all_to_all x3, blocking collectives, exchange(): return lax.all_to_all(blocks, axis, split_axis=0, concat_axis=0, tiled=True)  49.7 us
    all_to_all x3, waiting for transfers between devices, exchange(): return lax.all_to_all(blocks, axis, split_axis=0, concat_axis=0, tiled=True)  41.9 us
    all_to_all x3, starting transfers between devices, exchange(): return lax.all_to_all(blocks, axis, split_axis=0, concat_axis=0, tiled=True)  26.7 us
    pallas_call x1, Pallas kernels, layer(): pl.pallas_call(lambda *refs: layer_kernel(*refs, factor_all=factor_all),...  8.55 us
    ppermute x1, starting transfers between devices, staged(): lax.ppermute(send, 'core', swap).astype(jnp.float32)  7.31 us
    pallas_call x1, Pallas kernels, spectrum(): pl.pallas_call(spectrum_kernel, out_shape=jax.ShapeDtypeStruct((own_bands...  6.24 us
    ppermute x1, starting transfers between devices, staged(): other = lax.ppermute(partial, 'core', swap)  5.97 us
    ppermute x1, waiting for transfers between devices, staged(): lax.ppermute(audio_clips, TIME, [(source, source - 1) for source in range...  5.1 us
  transfers between devices with their start and end apart: 6, of which 5 were waited for; matrix products, arithmetic and copies ran while one was open for 2% of the time, Pallas kernels for 1%

profile of v4, /device:TPU:1, one launch (start us, length us, event | category | flops | bytes accessed | tf_op | source)
XLA Modules:
  0.0 173.2 jit_solution(5351660568903435713)
XLA Ops:
  0.6 0.0 copy-start.3
  0.6 0.0 copy-start.5
  0.7 1.4 collective-permute-start
  2.1 5.1 %collective-permute-done.rim_ref = f32[8,2,1764]{2,1,0:T(2,128)S(1)} collective-permute-done((f32[8,2,1764]{2,1,0:T(2,128)}, f32[8,2,1764]{2,1,0:T(2,128)S(1)}, u32[]{:S(2)}, u32[]{:S(2)}) %collective-permute-start) | collective-permute-done | bytes 112928 | tf_op jit(solution)/shard_map/ppermute | solution.py:497
  7.2 0.0 copy-start.4
  7.2 0.6 copy-done.4
  7.8 6.2 %spectrum.1 = bf16[64,4,512]{2,1,0:T(4,128)(2,1)} custom-call(s32[1]{0:T(128)} %bitcast.1.place_ref, s32[64]{0:T(128)} %widths_ref.1, f32[8,2,1764]{2,1,0:T(2,128)} %audio_ref.1, f32[8,2,1764]{2,1,0:T(2,128)} %copy-done.4, f32[8,512]{1,0:T(8,128)} %gain_ref.1, f32[1,2048]{1,0:T(1,128)} %constant.26.clone.taper_ref, f32[16,256]{1,0:T(8,128)} %constant.27.clone.twiddle_ref, ...), custom_call_target="tpu_custom_call" | custom-call | tf_op jit(solution)/shard_map/spectrum/pallas_call | solution.py:379
  14.1 16.9 %all-to-all-start = ((bf16[64,4,512]{2,1,0:T(4,128)(2,1)}), bf16[64,4,512]{2,1,0:T(4,128)(2,1)S(1)}, u32[]{:S(2)}, u32[]{:S(2)}) async-start(bf16[64,4,512]{2,1,0:T(4,128)(2,1)} %spectrum.1), calls=%async_computation | async-start | bytes 524288 | tf_op jit(solution)/shard_map/all_to_all | solution.py:471
  30.9 0.0 copy-done.5
  31.0 0.0 copy-start.6
  31.0 0.0 copy-done.3
  31.0 1.2 pad_maximum_fusion
  32.2 11.2 %all-to-all-done = bf16[64,4,512]{2,1,0:T(4,128)(2,1)S(1)} async-done(((bf16[64,4,512]{2,1,0:T(4,128)(2,1)}), bf16[64,4,512]{2,1,0:T(4,128)(2,1)S(1)}, u32[]{:S(2)}, u32[]{:S(2)}) %all-to-all-start) | async-done | bytes 262176 | tf_op jit(solution)/shard_map/all_to_all | solution.py:471
  43.4 5.7 %all-to-all-start.1 = ((bf16[64,12,384]{2,1,0:T(8,128)(2,1)}), bf16[64,12,384]{2,1,0:T(8,128)(2,1)S(1)}, u32[]{:S(2)}, u32[]{:S(2)}) async-start(bf16[64,12,384]{2,1,0:T(8,128)(2,1)} %pad_maximum_fusion), calls=%async_computation.1 | async-start | bytes 1572864 | tf_op jit(solution)/shard_map/all_to_all | solution.py:471
  49.1 0.0 copy-done.6
  49.1 0.6 reshape.55.refs_3_
  49.7 0.8 reshape.50.refs_1_
  50.4 18.9 %all-to-all-done.1 = bf16[64,12,384]{2,1,0:T(8,128)(2,1)S(1)} async-done(((bf16[64,12,384]{2,1,0:T(8,128)(2,1)}), bf16[64,12,384]{2,1,0:T(8,128)(2,1)S(1)}, u32[]{:S(2)}, u32[]{:S(2)}) %all-to-all-start.1) | async-done | bytes 589856 | tf_op jit(solution)/shard_map/all_to_all | solution.py:471
  69.4 0.1 slice.17
  69.4 0.7 reshape.54.grads_ref.refs_10_
  70.2 0.9 slice_bitcast_fusion.weight_ref
  71.0 3.2 %prepare.1 = (bf16[512,384]{1,0:T(8,128)(2,1)}, bf16[4,512,128]{2,1,0:T(8,128)(2,1)}, bf16[384,1024]{1,0:T(8,128)(2,1)}) custom-call(bf16[512,384]{1,0:T(8,128)(2,1)} %slice_bitcast_fusion.weight_ref, bf16[256,384]{1,0:T(8,128)(2,1)} %reshape.54.grads_ref.refs_10_, bf16[384,1536]{1,0:T(8,128)(2,1)} %refs_4_.1, bf16[512,384]{1,0:T(8,128)(2,1)} %refs_9_.1), custom_call_target="tpu_custom_call" | custom-call | tf_op jit(solution)/shard_map/prepare/pallas_call | solution.py:406
  74.3 8.5 %layer.1 = (bf16[256,384]{1,0:T(8,128)(2,1)}, bf16[1024,384]{1,0:T(8,128)(2,1)}, bf16[1024,384]{1,0:T(8,128)(2,1)}) custom-call(s32[1]{0:T(128)} %bitcast.refs_0_.core_ref, bf16[256,512]{1,0:T(8,128)(2,1)} %reshape.50.refs_1_, bf16[512,384]{1,0:T(8,128)(2,1)} %get-tuple-element.13.refs_2_, f32[1,384]{1,0:T(1,128)} %reshape.55.refs_3_, ...), custom_call_target="tpu_custom_call" | custom-call | tf_op jit(solution)/shard_map/layer/pallas_call | solution.py:431
  82.8 7.3 %collective-permute-start.1 = (bf16[1024,384]{1,0:T(8,128)(2,1)}, bf16[1024,384]{1,0:T(8,128)(2,1)S(1)}, u32[]{:S(2)}, u32[]{:S(2)}) collective-permute-start(bf16[1024,384]{1,0:T(8,128)(2,1)} %get-tuple-element.18), channel_id=1, source_target_pairs={{0,1},{1,0},{2,3},{3,2},{4,5},{5,4},{6,7},{7,6},{8,9},{9,8},{10,11... | collective-permute-start | bytes 2359304 | tf_op jit(solution)/shard_map/ppermute | solution.py:521
  90.2 1.9 %collective-permute-done.1 = bf16[1024,384]{1,0:T(8,128)(2,1)S(1)} collective-permute-done((bf16[1024,384]{1,0:T(8,128)(2,1)}, bf16[1024,384]{1,0:T(8,128)(2,1)S(1)}, u32[]{:S(2)}, u32[]{:S(2)}) %collective-permute-start.1) | collective-permute-done | bytes 786464 | tf_op jit(solution)/shard_map/ppermute | solution.py:521
  92.1 0.0 copy-start.2
  92.1 2.2 %add_convert_fusion = bf16[1024,384]{1,0:T(8,128)(2,1)} fusion(bf16[1024,384]{1,0:T(8,128)(2,1)S(1)} %collective-permute-done.1, bf16[1024,384]{1,0:T(8,128)(2,1)} %get-tuple-element.17), kind=kLoop, calls=%fused_computation | loop fusion | flops 1572864 | bytes 2359296 | tf_op jit(solution)/shard_map/convert_element_type | solution.py:522
  94.3 4.2 %all-to-all-start.2 = ((bf16[4,256,384]{2,1,0:T(8,128)(2,1)}), bf16[4,256,384]{2,1,0:T(8,128)(2,1)S(1)}, u32[]{:S(2)}, u32[]{:S(2)}) async-start(bf16[4,256,384]{2,1,0:T(8,128)(2,1)} %bitcast.5), calls=%async_computation.2 | async-start | bytes 1572864 | tf_op jit(solution)/shard_map/all_to_all | solution.py:471
  98.5 0.0 copy-done.2
  98.5 0.1 reshape.56
  98.6 11.7 %all-to-all-done.2 = bf16[4,256,384]{2,1,0:T(8,128)(2,1)S(1)} async-done(((bf16[4,256,384]{2,1,0:T(8,128)(2,1)}), bf16[4,256,384]{2,1,0:T(8,128)(2,1)S(1)}, u32[]{:S(2)}, u32[]{:S(2)}) %all-to-all-start.2) | async-done | bytes 786464 | tf_op jit(solution)/shard_map/all_to_all | solution.py:471
  110.2 0.2 reduce_sum.24
  110.4 0.1 reshape.58
  110.4 0.2 pad_maximum_fusion.1
  110.7 19.5 %all_to_all.30 = bf16[64,8,384]{2,1,0:T(8,128)(2,1)S(1)} all-to-all(bf16[64,8,384]{2,1,0:T(8,128)(2,1)S(1)} %pad_maximum_fusion.1), channel_id=1, replica_groups=mesh['z'=8,'y'=8,'x'=4,'core'=2] {'z','y'}, dimensions={0} | all-to-all | bytes 786432 | tf_op jit(solution)/shard_map/all_to_all | solution.py:471
  130.2 0.8 slice_reduce_fusion
  131.0 0.1 broadcast_in_dim.9
  131.1 18.7 %all_to_all.31 = bf16[64,4,384]{2,1,0:T(4,128)(2,1)S(1)} all-to-all(bf16[64,4,384]{2,1,0:T(4,128)(2,1)S(1)} %broadcast_in_dim.9), channel_id=1, replica_groups=mesh['z'=8,'y'=8,'x'=4,'core'=2] {'z','y'}, dimensions={0} | all-to-all | bytes 393216 | tf_op jit(solution)/shard_map/all_to_all | solution.py:471
  149.7 0.1 broadcast_in_dim.10
  149.8 0.1 broadcast_in_dim.22
  149.8 11.6 %all_to_all.32 = bf16[4,256,384]{2,1,0:T(8,128)(2,1)S(1)} all-to-all(bf16[4,256,384]{2,1,0:T(8,128)(2,1)S(1)} %broadcast_in_dim.22), channel_id=1, replica_groups=mesh['z'=8,'y'=8,'x'=4,'core'=2] {'x'}, dimensions={0} | all-to-all | bytes 1572864 | tf_op jit(solution)/shard_map/all_to_all | solution.py:471
  161.4 0.0 copy-start
  161.4 6.0 %collective-permute-start.2 = (bf16[1024,384]{1,0:T(8,128)(2,1)S(1)}, bf16[1024,384]{1,0:T(8,128)(2,1)S(1)}, u32[]{:S(2)}, u32[]{:S(2)}) collective-permute-start(bf16[1024,384]{1,0:T(8,128)(2,1)S(1)} %bitcast.9), channel_id=1, source_target_pairs={{0,1},{1,0},{2,3},{3,2},{4,5},{5,4},{6,7},{7,6},{8,9},{9,8},{10,11... | collective-permute-start | bytes 2359304 | tf_op jit(solution)/shard_map/ppermute | solution.py:529
  167.4 0.0 copy-done
  167.4 2.4 %unpack.2 = (f32[384,1536]{1,0:T(8,128)}, f32[512,384]{1,0:T(8,128)}) custom-call(s32[1]{0:T(128)} %bitcast.refs_0_.core_ref, bf16[1024,384]{1,0:T(8,128)(2,1)} %bitcast.10), custom_call_target="tpu_custom_call" | custom-call | tf_op jit(solution)/shard_map/unpack/pallas_call | solution.py:452
  169.8 0.0 collective-permute-done.2.half_ref
  169.8 0.0 copy-start.1
  169.8 0.9 copy-done.1
  170.7 2.4 %unpack.3 = (f32[384,1536]{1,0:T(8,128)}, f32[512,384]{1,0:T(8,128)}) custom-call(s32[1]{0:T(128)S(6)} %sub.3.core_ref, bf16[1024,384]{1,0:T(8,128)(2,1)} %copy-done.1, f32[384,1536]{1,0:T(8,128)} %get-tuple-element.19.refs_0_, f32[512,384]{1,0:T(8,128)} %get-tuple-element.20.refs_1_), custom_call_target="tpu_custom_call", output_to_operand_aliasing={{0}: (2, {}), {1}: (3, {})} | custom-call | tf_op jit(solution)/shard_map/unpack/pallas_call | solution.py:452
  (1 shorter events, 0.0 us)
Async XLA Ops:
  0.6 30.4 %copy-start.3 = (bf16[8,8,4,384]{3,2,1,0:T(4,128)(2,1)S(1)}, bf16[8,8,4,384]{3,2,1,0:T(4,128)(2,1)}, u32[]{:S(2)}) copy-start(bf16[8,8,4,384]{3,2,1,0:T(4,128)(2,1)} %param.20) | copy-start | bytes 589828
  0.6 30.3 %copy-start.5 = (bf16[8,8,384]{2,1,0:T(8,128)(2,1)S(1)}, bf16[8,8,384]{2,1,0:T(8,128)(2,1)}, u32[]{:S(2)}) copy-start(bf16[8,8,384]{2,1,0:T(8,128)(2,1)} %param.16) | copy-start | bytes 147460
  0.7 6.5 %collective-permute-start = (f32[8,2,1764]{2,1,0:T(2,128)}, f32[8,2,1764]{2,1,0:T(2,128)S(1)}, u32[]{:S(2)}, u32[]{:S(2)}) collective-permute-start(f32[8,2,1764]{2,1,0:T(2,128)} %audio_ref.1), channel_id=1, source_target_pairs={{8,0},{16,8},{24,16},{32,24},{40,32},{48,40},{56,48},{64,56},{72,6... | collective-permute-start | bytes 338696 | tf_op jit(solution)/shard_map/ppermute | solution.py:497
  7.2 0.6 copy-start.4
  14.1 29.3 %all-to-all-start = ((bf16[64,4,512]{2,1,0:T(4,128)(2,1)}), bf16[64,4,512]{2,1,0:T(4,128)(2,1)S(1)}, u32[]{:S(2)}, u32[]{:S(2)}) async-start(bf16[64,4,512]{2,1,0:T(4,128)(2,1)} %spectrum.1), calls=%async_computation | async-start | bytes 524288 | tf_op jit(solution)/shard_map/all_to_all | solution.py:471
  31.0 18.1 %copy-start.6 = (f32[384]{0:T(512)S(1)}, f32[384]{0:T(512)}, u32[]{:S(2)}) copy-start(f32[384]{0:T(512)} %param.17) | copy-start | bytes 4612
  43.4 26.0 %all-to-all-start.1 = ((bf16[64,12,384]{2,1,0:T(8,128)(2,1)}), bf16[64,12,384]{2,1,0:T(8,128)(2,1)S(1)}, u32[]{:S(2)}, u32[]{:S(2)}) async-start(bf16[64,12,384]{2,1,0:T(8,128)(2,1)} %pad_maximum_fusion), calls=%async_computation.1 | async-start | bytes 1572864 | tf_op jit(solution)/shard_map/all_to_all | solution.py:471
  82.8 9.2 %collective-permute-start.1 = (bf16[1024,384]{1,0:T(8,128)(2,1)}, bf16[1024,384]{1,0:T(8,128)(2,1)S(1)}, u32[]{:S(2)}, u32[]{:S(2)}) collective-permute-start(bf16[1024,384]{1,0:T(8,128)(2,1)} %get-tuple-element.18), channel_id=1, source_target_pairs={{0,1},{1,0},{2,3},{3,2},{4,5},{5,4},{6,7},{7,6},{8,9},{9,8},{10,11... | collective-permute-start | bytes 2359304 | tf_op jit(solution)/shard_map/ppermute | solution.py:521
  92.1 6.4 %copy-start.2 = (bf16[256,384]{1,0:T(8,128)(2,1)S(1)}, bf16[256,384]{1,0:T(8,128)(2,1)}, u32[]{:S(2)}) copy-start(bf16[256,384]{1,0:T(8,128)(2,1)} %get-tuple-element.16) | copy-start | bytes 589828
  94.3 15.9 %all-to-all-start.2 = ((bf16[4,256,384]{2,1,0:T(8,128)(2,1)}), bf16[4,256,384]{2,1,0:T(8,128)(2,1)S(1)}, u32[]{:S(2)}, u32[]{:S(2)}) async-start(bf16[4,256,384]{2,1,0:T(8,128)(2,1)} %bitcast.5), calls=%async_computation.2 | async-start | bytes 1572864 | tf_op jit(solution)/shard_map/all_to_all | solution.py:471
  161.4 6.0 %copy-start = (bf16[4,256,384]{2,1,0:T(8,128)(2,1)}, bf16[4,256,384]{2,1,0:T(8,128)(2,1)S(1)}, u32[]{:S(2)}) copy-start(bf16[4,256,384]{2,1,0:T(8,128)(2,1)S(1)} %all_to_all.32) | copy-start | bytes 2359300
  161.4 8.4 %collective-permute-start.2 = (bf16[1024,384]{1,0:T(8,128)(2,1)S(1)}, bf16[1024,384]{1,0:T(8,128)(2,1)S(1)}, u32[]{:S(2)}, u32[]{:S(2)}) collective-permute-start(bf16[1024,384]{1,0:T(8,128)(2,1)S(1)} %bitcast.9), channel_id=1, source_target_pairs={{0,1},{1,0},{2,3},{3,2},{4,5},{5,4},{6,7},{7,6},{8,9},{9,8},{10,11... | collective-permute-start | bytes 2359304 | tf_op jit(solution)/shard_map/ppermute | solution.py:529
  169.8 0.9 copy-start.1

commit v5 on v4

--- a/solution.py
+++ b/solution.py
@@ -194,6 +194,17 @@
                 ).astype(jnp.bfloat16)
 
 
+def assemble_kernel(grads_ref, weight_ref, out_ref):
+    block = grads_ref.shape[1]
+    steps = weight_ref.shape[1] // block
+    out_ref[:, 0] = grads_ref[...]
+    for band in range(weight_ref.shape[0]):
+        for step in range(steps):
+            piece = weight_ref[band, step * block : (step + 1) * block, :]
+            for c in range(CLIPS):
+                out_ref[band * CLIPS + c, 1 + step] = piece
+
+
 def dot(left, right, dims=((1,), (0,))):
     return lax.dot_general(left, right, (dims, ((), ())), preferred_element_type=jnp.float32)
 
@@ -268,7 +279,7 @@
     ]
     for copy in copies:
         copy.start()
-    x = dot(feats_ref[...], embed_ref[...]).astype(jnp.bfloat16).astype(jnp.float32)
+    x = dot(feats_ref[...].reshape(FRAMES, FEAT), embed_ref[...]).astype(jnp.bfloat16).astype(jnp.float32)
     scale = lax.rsqrt(jnp.mean(x * x, axis=1, keepdims=True) + 1e-06)
     normed_x = (x * scale * gain_ref[...]).astype(jnp.bfloat16)
     for copy in copies[:4]:
@@ -329,7 +340,8 @@
         closed(pair, *ready)
         ready = following
     mixed_b = mixed_s[...]
-    attended_ref[...] = (x + dot(mixed_b, outw_ref[...])).astype(jnp.bfloat16)
+    attended = x + dot(mixed_b, outw_ref[...])
+    attended_ref[...] = attended.reshape(attended_ref.shape).astype(jnp.bfloat16)
     core = core_ref[0]
 
     def place(first, values):
@@ -402,6 +414,19 @@
     )
 
 
+def assemble(grads, weight):
+    sequences, block, width = grads.shape
+    return pl.pallas_call(
+        assemble_kernel,
+        out_shape=jax.ShapeDtypeStruct(
+            (sequences, 1 + weight.shape[1] // block, block, width), grads.dtype
+        ),
+        in_specs=[whole()] * 2,
+        out_specs=whole(),
+        name="assemble",
+    )(grads, weight)
+
+
 def prepare(weight, grads, qkv_weight, out_weight):
     return pl.pallas_call(
         prepare_kernel,
@@ -431,7 +456,7 @@
     return pl.pallas_call(
         lambda *refs: layer_kernel(*refs, factor_all=factor_all),
         out_shape=(
-            jax.ShapeDtypeStruct((FRAMES, D), jnp.bfloat16),
+            jax.ShapeDtypeStruct(feats.shape[:2] + (D,), jnp.bfloat16),
             jax.ShapeDtypeStruct((2 * INNER, D), jnp.bfloat16),
             jax.ShapeDtypeStruct((2 * INNER, D), jnp.bfloat16),
         ),
@@ -496,21 +521,14 @@
     frame_block = audio_clips.shape[2] // HOP
     rim = lax.ppermute(audio_clips, TIME, [(source, source - 1) for source in range(1, tm)])
     sequences = own_bands * CLIPS
-    rows = FEAT // tm
-    early = jnp.concatenate(
-        [
-            cotangent.reshape(sequences, frame_block, D),
-            jnp.broadcast_to(band_weight[:, None], (own_bands, CLIPS, rows, D)).reshape(
-                sequences, rows, D
-            ),
-        ],
-        axis=1,
-    )
-    early = exchange(early, TIME)
-    grads = early[:, :frame_block].reshape(FRAMES, D)
-    weight = early[:, frame_block:].reshape(FEAT, D)
+    early = assemble(cotangent.reshape(sequences, frame_block, D), band_weight)
+    parts = early.shape[1]
+    early = exchange(early.reshape(sequences * parts, frame_block, D), TIME)
+    early = early.reshape(tm, parts, frame_block, D)
+    grads = early[:, 0].reshape(FRAMES, D)
+    weight = early[:, 1:].reshape(FEAT, D)
     normed = spectrum(band_at, band_widths, audio_clips, rim, band_gain)
-    feats = exchange(normed, TIME).reshape(FRAMES, FEAT)
+    feats = exchange(normed, TIME)
     factor_all = 1.0 / math.sqrt(BANDS * CLIPS * FRAMES)
     core = lax.axis_index("core").reshape(1)
     prepared = prepare(weight, grads, qkv_weight, out_weight)
@@ -521,7 +539,7 @@
     partial = keep.astype(jnp.float32) + lax.ppermute(send, "core", swap).astype(jnp.float32)
     partial = scatter_sum(partial.astype(jnp.bfloat16), "x")
     both = jnp.concatenate(
-        [attended.reshape(tm, frame_block, D), partial.reshape(tm, -1, D)], axis=1
+        [attended, partial.reshape(tm, -1, D)], axis=1
     )
     both = exchange(both, TIME)
     attended_out = both[:, :frame_block].reshape(own_bands, CLIPS, frame_block, D)

time: 174 us -> 162 us (0.931)
  waiting for transfers between devices: 48.9 us -> 23.8 us
  blocking collectives: 49.7 us -> 63.2 us
  other arithmetic: 4.6 us -> 2.51 us
  Pallas kernels: 22.7 us -> 24.6 us
    all_to_all x3 -> x2, waiting for transfers between devices: 41.9 us -> 7.02 us  [exchange(): return lax.all_to_all(blocks, axis, split_axis=0, concat_axis=0, tiled=True)]
    all_to_all x3 -> x4, blocking collectives: 49.7 us -> 63.2 us  [exchange(): return lax.all_to_all(blocks, axis, split_axis=0, concat_axis=0, tiled=True)]
    ppermute x1, waiting for transfers between devices: 5.1 us -> 14.7 us  [staged(): lax.ppermute(audio_clips, TIME, [(source, source - 1) for source in range...]
    all_to_all x3 -> x2, starting transfers between devices: 26.7 us -> 29.3 us  [exchange(): return lax.all_to_all(blocks, axis, split_axis=0, concat_axis=0, tiled=True)]
    ppermute x1, starting transfers between devices: 7.31 us -> 5.12 us  [staged(): lax.ppermute(send, 'core', swap).astype(jnp.float32)]
    pallas_call x0 -> x1, Pallas kernels: none -> 1.84 us  [assemble(): pl.pallas_call(assemble_kernel, out_shape=jax.ShapeDtypeStruct((sequences...]
  transfers between devices with their start and end apart: 6 -> 5, of which waited for: 5 -> 3; matrix products, arithmetic and copies ran while one was open for 2% -> 1% of each run, Pallas kernels for 1% -> 7%
where the time goes in v5:
time: 162 us
  blocking collectives  63.2 us (39%)
  starting transfers between devices  41.9 us (26%)
  Pallas kernels  24.6 us (15%)
  waiting for transfers between devices  23.8 us (15%)
  local copies, waits for them, and re-layouts  4.84 us (3%)
  other arithmetic  2.51 us (2%)
    all_to_all x4, blocking collectives, exchange(): return lax.all_to_all(blocks, axis, split_axis=0, concat_axis=0, tiled=True)  63.2 us
    all_to_all x2, starting transfers between devices, exchange(): return lax.all_to_all(blocks, axis, split_axis=0, concat_axis=0, tiled=True)  29.3 us
    ppermute x1, waiting for transfers between devices, staged(): lax.ppermute(audio_clips, TIME, [(source, source - 1) for source in range...  14.7 us
    pallas_call x1, Pallas kernels, layer(): pl.pallas_call(lambda *refs: layer_kernel(*refs, factor_all=factor_all),...  8.54 us
    all_to_all x2, waiting for transfers between devices, exchange(): return lax.all_to_all(blocks, axis, split_axis=0, concat_axis=0, tiled=True)  7.02 us
    pallas_call x1, Pallas kernels, spectrum(): pl.pallas_call(spectrum_kernel, out_shape=jax.ShapeDtypeStruct((own_bands...  6.23 us
    ppermute x1, starting transfers between devices, staged(): other = lax.ppermute(partial, 'core', swap)  6.13 us
    ppermute x1, starting transfers between devices, staged(): lax.ppermute(send, 'core', swap).astype(jnp.float32)  5.12 us
  transfers between devices with their start and end apart: 5, of which 3 were waited for; matrix products, arithmetic and copies ran while one was open for 1% of the time, Pallas kernels for 7%

profile of v5, /device:TPU:1, one launch (start us, length us, event | category | flops | bytes accessed | tf_op | source)
XLA Modules:
  0.0 161.8 jit_solution(948545163466705041)
XLA Ops:
  0.6 0.0 copy-start.4
  0.6 1.8 %assemble.1 = bf16[64,3,4,384]{3,2,1,0:T(4,128)(2,1)} custom-call(bf16[64,4,384]{2,1,0:T(4,128)(2,1)} %bitcast.14, bf16[8,8,384]{2,1,0:T(8,128)(2,1)} %weight_ref.1), custom_call_target="tpu_custom_call" | custom-call | tf_op jit(solution)/shard_map/assemble/pallas_call | solution.py:419
  2.5 0.0 copy-start.6
  2.5 17.3 %all-to-all-start.1 = ((bf16[192,4,384]{2,1,0:T(4,128)(2,1)}), bf16[192,4,384]{2,1,0:T(4,128)(2,1)S(1)}, u32[]{:S(2)}, u32[]{:S(2)}) async-start(bf16[192,4,384]{2,1,0:T(4,128)(2,1)} %bitcast.13), calls=%async_computation.1 | async-start | bytes 1179648 | tf_op jit(solution)/shard_map/all_to_all | solution.py:496
  19.8 0.0 copy-done.4
  19.8 1.3 collective-permute-start
  21.1 14.7 %collective-permute-done.rim_ref = f32[8,2,1764]{2,1,0:T(2,128)S(1)} collective-permute-done((f32[8,2,1764]{2,1,0:T(2,128)S(1)}, f32[8,2,1764]{2,1,0:T(2,128)S(1)}, u32[]{:S(2)}, u32[]{:S(2)}) %collective-permute-start) | collective-permute-done | bytes 112928 | tf_op jit(solution)/shard_map/ppermute | solution.py:522
  35.8 0.0 copy-start.5
  35.8 0.6 copy-done.5
  36.4 6.2 %spectrum.1 = bf16[64,4,512]{2,1,0:T(4,128)(2,1)} custom-call(s32[1]{0:T(128)} %bitcast.1.place_ref, s32[64]{0:T(128)} %widths_ref.1, f32[8,2,1764]{2,1,0:T(2,128)} %audio_ref.1, f32[8,2,1764]{2,1,0:T(2,128)} %copy-done.5, f32[8,512]{1,0:T(8,128)} %gain_ref.1, f32[1,2048]{1,0:T(1,128)} %constant.26.clone.taper_ref, f32[16,256]{1,0:T(8,128)} %constant.27.clone.twiddle_ref, ...), custom_call_target="tpu_custom_call" | custom-call | tf_op jit(solution)/shard_map/spectrum/pallas_call | solution.py:391
  42.6 0.0 all-to-all-done.1
  42.6 12.1 %all-to-all-start = ((bf16[64,4,512]{2,1,0:T(4,128)(2,1)}), bf16[64,4,512]{2,1,0:T(4,128)(2,1)S(1)}, u32[]{:S(2)}, u32[]{:S(2)}) async-start(bf16[64,4,512]{2,1,0:T(4,128)(2,1)} %spectrum.1), calls=%async_computation | async-start | bytes 524288 | tf_op jit(solution)/shard_map/all_to_all | solution.py:496
  54.7 0.0 copy-done.6
  54.7 0.6 reshape.47.refs_3_
  55.3 0.1 slice.17
  55.4 0.1 slice.16
  55.5 0.7 reshape_squeeze.3.grads_ref.refs_10_
  56.3 0.8 reshape.46.weight_ref
  57.1 3.2 %prepare.1 = (bf16[512,384]{1,0:T(8,128)(2,1)}, bf16[4,512,128]{2,1,0:T(8,128)(2,1)}, bf16[384,1024]{1,0:T(8,128)(2,1)}) custom-call(bf16[512,384]{1,0:T(8,128)(2,1)} %reshape.46.weight_ref, bf16[256,384]{1,0:T(8,128)(2,1)} %reshape_squeeze.3.grads_ref.refs_10_, bf16[384,1536]{1,0:T(8,128)(2,1)} %refs_4_.1, bf16[512,384]{1,0:T(8,128)(2,1)} %refs_9_.1), custom_call_target="tpu_custom_call" | custom-call | tf_op jit(solution)/shard_map/prepare/pallas_call | solution.py:431
  60.4 7.0 %all-to-all-done.refs_1_ = bf16[64,4,512]{2,1,0:T(4,128)(2,1)S(1)} async-done(((bf16[64,4,512]{2,1,0:T(4,128)(2,1)}), bf16[64,4,512]{2,1,0:T(4,128)(2,1)S(1)}, u32[]{:S(2)}, u32[]{:S(2)}) %all-to-all-start) | async-done | bytes 262176 | tf_op jit(solution)/shard_map/all_to_all | solution.py:496
  67.4 0.0 copy-start.1
  67.4 0.7 copy-done.1
  68.1 8.5 %layer.1 = (bf16[64,4,384]{2,1,0:T(4,128)(2,1)}, bf16[1024,384]{1,0:T(8,128)(2,1)}, bf16[1024,384]{1,0:T(8,128)(2,1)}) custom-call(s32[1]{0:T(128)} %bitcast.refs_0_.core_ref, bf16[64,4,512]{2,1,0:T(4,128)(2,1)} %copy-done.1, bf16[512,384]{1,0:T(8,128)(2,1)} %get-tuple-element.13.refs_2_, f32[1,384]{1,0:T(1,128)} %reshape.47.refs_3_, ...), custom_call_target="tpu_custom_call" | custom-call | tf_op jit(solution)/shard_map/layer/pallas_call | solution.py:456
  76.6 5.1 %collective-permute-start.1 = (bf16[1024,384]{1,0:T(8,128)(2,1)}, bf16[1024,384]{1,0:T(8,128)(2,1)S(1)}, u32[]{:S(2)}, u32[]{:S(2)}) collective-permute-start(bf16[1024,384]{1,0:T(8,128)(2,1)} %get-tuple-element.18), channel_id=1, source_target_pairs={{0,1},{1,0},{2,3},{3,2},{4,5},{5,4},{6,7},{7,6},{8,9},{9,8},{10,11... | collective-permute-start | bytes 2359304 | tf_op jit(solution)/shard_map/ppermute | solution.py:539
  81.7 2.1 %collective-permute-done.1 = bf16[1024,384]{1,0:T(8,128)(2,1)S(1)} collective-permute-done((bf16[1024,384]{1,0:T(8,128)(2,1)}, bf16[1024,384]{1,0:T(8,128)(2,1)S(1)}, u32[]{:S(2)}, u32[]{:S(2)}) %collective-permute-start.1) | collective-permute-done | bytes 786464 | tf_op jit(solution)/shard_map/ppermute | solution.py:539
  83.8 1.3 add_convert_fusion
  85.2 0.0 copy-start.3
  85.2 15.5 %all_to_all.30 = bf16[4,256,384]{2,1,0:T(8,128)(2,1)S(1)} all-to-all(bf16[4,256,384]{2,1,0:T(8,128)(2,1)S(1)} %bitcast.10), channel_id=1, replica_groups=mesh['z'=8,'y'=8,'x'=4,'core'=2] {'x'}, dimensions={0} | all-to-all | bytes 1572864 | tf_op jit(solution)/shard_map/all_to_all | solution.py:496
  100.7 0.2 reduce_sum.24
  100.9 0.1 reshape.49
  100.9 0.0 copy-done.3
  100.9 0.2 pad_maximum_fusion
  101.2 17.7 %all_to_all.31 = bf16[64,8,384]{2,1,0:T(8,128)(2,1)S(1)} all-to-all(bf16[64,8,384]{2,1,0:T(8,128)(2,1)S(1)} %pad_maximum_fusion), channel_id=1, replica_groups=mesh['z'=8,'y'=8,'x'=4,'core'=2] {'z','y'}, dimensions={0} | all-to-all | bytes 786432 | tf_op jit(solution)/shard_map/all_to_all | solution.py:496
  118.9 0.8 slice_reduce_fusion
  119.7 0.1 broadcast_in_dim.6
  119.7 18.5 %all_to_all.32 = bf16[64,4,384]{2,1,0:T(4,128)(2,1)S(1)} all-to-all(bf16[64,4,384]{2,1,0:T(4,128)(2,1)S(1)} %broadcast_in_dim.6), channel_id=1, replica_groups=mesh['z'=8,'y'=8,'x'=4,'core'=2] {'z','y'}, dimensions={0} | all-to-all | bytes 393216 | tf_op jit(solution)/shard_map/all_to_all | solution.py:496
  138.3 0.1 broadcast_in_dim.14
  138.3 0.1 broadcast_in_dim.15
  138.4 11.4 %all_to_all.33 = bf16[4,256,384]{2,1,0:T(8,128)(2,1)S(1)} all-to-all(bf16[4,256,384]{2,1,0:T(8,128)(2,1)S(1)} %broadcast_in_dim.15), channel_id=1, replica_groups=mesh['z'=8,'y'=8,'x'=4,'core'=2] {'x'}, dimensions={0} | all-to-all | bytes 1572864 | tf_op jit(solution)/shard_map/all_to_all | solution.py:496
  149.8 0.0 copy-start
  149.8 6.1 %collective-permute-start.2 = (bf16[1024,384]{1,0:T(8,128)(2,1)S(1)}, bf16[1024,384]{1,0:T(8,128)(2,1)S(1)}, u32[]{:S(2)}, u32[]{:S(2)}) collective-permute-start(bf16[1024,384]{1,0:T(8,128)(2,1)S(1)} %bitcast.8), channel_id=1, source_target_pairs={{0,1},{1,0},{2,3},{3,2},{4,5},{5,4},{6,7},{7,6},{8,9},{9,8},{10,11... | collective-permute-start | bytes 2359304 | tf_op jit(solution)/shard_map/ppermute | solution.py:547
  155.9 0.0 copy-done
  156.0 2.4 %unpack.2 = (f32[384,1536]{1,0:T(8,128)}, f32[512,384]{1,0:T(8,128)}) custom-call(s32[1]{0:T(128)} %bitcast.refs_0_.core_ref, bf16[1024,384]{1,0:T(8,128)(2,1)} %bitcast.9), custom_call_target="tpu_custom_call" | custom-call | tf_op jit(solution)/shard_map/unpack/pallas_call | solution.py:477
  158.3 0.0 collective-permute-done.2.half_ref
  158.3 0.0 copy-start.2
  158.3 0.9 copy-done.2
  159.2 2.4 %unpack.3 = (f32[384,1536]{1,0:T(8,128)}, f32[512,384]{1,0:T(8,128)}) custom-call(s32[1]{0:T(128)S(6)} %sub.3.core_ref, bf16[1024,384]{1,0:T(8,128)(2,1)} %copy-done.2, f32[384,1536]{1,0:T(8,128)} %get-tuple-element.19.refs_0_, f32[512,384]{1,0:T(8,128)} %get-tuple-element.20.refs_1_), custom_call_target="tpu_custom_call", output_to_operand_aliasing={{0}: (2, {}), {1}: (3, {})} | custom-call | tf_op jit(solution)/shard_map/unpack/pallas_call | solution.py:477
Async XLA Ops:
  0.6 19.1 %copy-start.4 = (f32[8,2,1764]{2,1,0:T(2,128)S(1)}, f32[8,2,1764]{2,1,0:T(2,128)}, u32[]{:S(2)}) copy-start(f32[8,2,1764]{2,1,0:T(2,128)} %audio_ref.1) | copy-start | bytes 338692
  2.5 52.2 %copy-start.6 = (f32[384]{0:T(512)S(1)}, f32[384]{0:T(512)}, u32[]{:S(2)}) copy-start(f32[384]{0:T(512)} %param.17) | copy-start | bytes 4612
  2.5 40.1 %all-to-all-start.1 = ((bf16[192,4,384]{2,1,0:T(4,128)(2,1)}), bf16[192,4,384]{2,1,0:T(4,128)(2,1)S(1)}, u32[]{:S(2)}, u32[]{:S(2)}) async-start(bf16[192,4,384]{2,1,0:T(4,128)(2,1)} %bitcast.13), calls=%async_computation.1 | async-start | bytes 1179648 | tf_op jit(solution)/shard_map/all_to_all | solution.py:496
  19.8 16.0 %collective-permute-start = (f32[8,2,1764]{2,1,0:T(2,128)S(1)}, f32[8,2,1764]{2,1,0:T(2,128)S(1)}, u32[]{:S(2)}, u32[]{:S(2)}) collective-permute-start(f32[8,2,1764]{2,1,0:T(2,128)S(1)} %copy-done.4), channel_id=1, source_target_pairs={{8,0},{16,8},{24,16},{32,24},{40,32},{48,40},{56,48},{64,56},{72,6... | collective-permute-start | bytes 338696 | tf_op jit(solution)/shard_map/ppermute | solution.py:522
  35.8 0.6 copy-start.5
  42.6 24.7 %all-to-all-start = ((bf16[64,4,512]{2,1,0:T(4,128)(2,1)}), bf16[64,4,512]{2,1,0:T(4,128)(2,1)S(1)}, u32[]{:S(2)}, u32[]{:S(2)}) async-start(bf16[64,4,512]{2,1,0:T(4,128)(2,1)} %spectrum.1), calls=%async_computation | async-start | bytes 524288 | tf_op jit(solution)/shard_map/all_to_all | solution.py:496
  67.4 0.7 copy-start.1
  76.6 7.2 %collective-permute-start.1 = (bf16[1024,384]{1,0:T(8,128)(2,1)}, bf16[1024,384]{1,0:T(8,128)(2,1)S(1)}, u32[]{:S(2)}, u32[]{:S(2)}) collective-permute-start(bf16[1024,384]{1,0:T(8,128)(2,1)} %get-tuple-element.18), channel_id=1, source_target_pairs={{0,1},{1,0},{2,3},{3,2},{4,5},{5,4},{6,7},{7,6},{8,9},{9,8},{10,11... | collective-permute-start | bytes 2359304 | tf_op jit(solution)/shard_map/ppermute | solution.py:539
  85.2 15.8 %copy-start.3 = (bf16[64,4,384]{2,1,0:T(4,128)(2,1)S(1)}, bf16[64,4,384]{2,1,0:T(4,128)(2,1)}, u32[]{:S(2)}) copy-start(bf16[64,4,384]{2,1,0:T(4,128)(2,1)} %get-tuple-element.16) | copy-start | bytes 589828
  149.8 6.1 %copy-start = (bf16[4,256,384]{2,1,0:T(8,128)(2,1)}, bf16[4,256,384]{2,1,0:T(8,128)(2,1)S(1)}, u32[]{:S(2)}) copy-start(bf16[4,256,384]{2,1,0:T(8,128)(2,1)S(1)} %all_to_all.33) | copy-start | bytes 2359300
  149.8 8.5 %collective-permute-start.2 = (bf16[1024,384]{1,0:T(8,128)(2,1)S(1)}, bf16[1024,384]{1,0:T(8,128)(2,1)S(1)}, u32[]{:S(2)}, u32[]{:S(2)}) collective-permute-start(bf16[1024,384]{1,0:T(8,128)(2,1)S(1)} %bitcast.8), channel_id=1, source_target_pairs={{0,1},{1,0},{2,3},{3,2},{4,5},{5,4},{6,7},{7,6},{8,9},{9,8},{10,11... | collective-permute-start | bytes 2359304 | tf_op jit(solution)/shard_map/ppermute | solution.py:547
  158.3 0.9 copy-start.2

commit v6 on v5

--- a/solution.py
+++ b/solution.py
@@ -217,7 +217,7 @@
     )
 
 
-def prepare_kernel(weight_ref, grads_ref, qkv_ref, outw_ref, embed_ref, heads_ref, swapped_ref):
+def prepare_kernel(weight_ref, grads_ref, qkv_ref, outw_ref, embed_ref, heads_ref, turned_ref):
     natural = lax.broadcasted_iota(jnp.int32, (FEAT, FEAT), 1)
     wanted = lax.broadcasted_iota(jnp.int32, (FEAT, FEAT), 0)
     order = one_hot(natural == (wanted % MAXW) * 4 + wanted // MAXW)
@@ -230,18 +230,21 @@
     row = lax.broadcasted_iota(jnp.int32, (128, 128), 0)
     lane = lax.broadcasted_iota(jnp.int32, (128, 128), 1)
     swap = one_hot(row == lane + jnp.where(lane % HDIM < HDIM // 2, HDIM // 2, -(HDIM // 2)))
-    for block in range(2 * INNER // 128):
-        cols = slice(block * 128, (block + 1) * 128)
-        swapped_ref[:, cols] = dot(qkv_ref[:, cols], swap).astype(jnp.bfloat16)
+    for part in range(2):
+        for pair in range(HEADS // 2):
+            piece = qkv_ref[:, part * INNER + pair * 128 : part * INNER + (pair + 1) * 128]
+            at = pair * 512 + part * 256
+            turned_ref[:, at : at + 128] = piece
+            turned_ref[:, at + 128 : at + 256] = dot(piece, swap).astype(jnp.bfloat16)
 
 
 def layer_kernel(
     core_ref,
-    feats_ref,
     embed_ref,
     gain_ref,
+    feats_hbm,
+    turned_hbm,
     qkv_hbm,
-    swapped_hbm,
     cos_hbm,
     sin_hbm,
     heads_hbm,
@@ -250,8 +253,9 @@
     attended_ref,
     keep_ref,
     send_ref,
-    qkv_ref,
-    swapped_ref,
+    feats_ref,
+    turned_ref,
+    plain_ref,
     cos_ref,
     sin_ref,
     heads_ref,
@@ -265,8 +269,9 @@
     factor_all,
 ):
     pairs = (
-        (qkv_hbm, qkv_ref),
-        (swapped_hbm, swapped_ref),
+        (feats_hbm, feats_ref),
+        (turned_hbm, turned_ref),
+        (qkv_hbm.at[:, 2 * INNER :], plain_ref),
         (cos_hbm, cos_ref),
         (sin_hbm, sin_ref),
         (heads_hbm, heads_ref),
@@ -279,26 +284,21 @@
     ]
     for copy in copies:
         copy.start()
+    copies[0].wait()
     x = dot(feats_ref[...].reshape(FRAMES, FEAT), embed_ref[...]).astype(jnp.bfloat16).astype(jnp.float32)
     scale = lax.rsqrt(jnp.mean(x * x, axis=1, keepdims=True) + 1e-06)
     normed_x = (x * scale * gain_ref[...]).astype(jnp.bfloat16)
-    for copy in copies[:4]:
+    for copy in copies[1:]:
         copy.wait()
     factor = 1.0 / math.sqrt(HDIM)
     cosine = cos_ref[...]
     sine = sin_ref[...]
-    for copy in copies[4:]:
-        copy.wait()
+    values = dot(normed_x, plain_ref[...])
 
     def opened(pair):
-        cols = slice(pair * 128, (pair + 1) * 128)
-        after = slice(INNER + pair * 128, INNER + (pair + 1) * 128)
-        q, k, v = (
-            dot(normed_x, qkv_ref[:, part * INNER + pair * 128 : part * INNER + (pair + 1) * 128])
-            for part in range(3)
-        )
-        q_swap = dot(normed_x, swapped_ref[:, cols])
-        k_swap = dot(normed_x, swapped_ref[:, after])
+        made = dot(normed_x, turned_ref[:, pair * 512 : (pair + 1) * 512])
+        q, q_swap, k, k_swap = (made[:, at * 128 : (at + 1) * 128] for at in range(4))
+        v = values[:, pair * 128 : (pair + 1) * 128]
         query = split_heads((q * cosine + q_swap * sine) * factor)
         query_swap = split_heads((q_swap * cosine - q * sine) * factor)
         turned = k * cosine + k_swap * sine
@@ -359,23 +359,34 @@
     send_ref[...] = halves[1]
 
 
-def unpack_kernel(core_ref, half_ref, *refs):
-    grad_qkv_hbm, grad_out_hbm, wide, tall, sems = refs[-5:]
-    rows = wide.shape[0]
-    for block in range(3 * INNER // D):
-        wide[:, block * D : (block + 1) * D] = half_ref[
-            block * rows : (block + 1) * rows, :
-        ].astype(jnp.float32)
-    tall[...] = half_ref[3 * INNER // D * rows :, :].astype(jnp.float32)
+def unpack_kernel(core_ref, half_hbm, *refs):
+    grad_qkv_hbm, grad_out_hbm, half_ref, wide_ref, in_sems, out_sems = refs[-6:]
     core = core_ref[0]
-    copies = []
-    for at, (source, target) in enumerate(((wide, grad_qkv_hbm), (tall, grad_out_hbm))):
-        count = source.shape[0]
-        place = target.at[pl.ds(pl.multiple_of(core * count, count), count), :]
-        copies.append(pltpu.make_async_copy(source, place, sems.at[at]))
-    for copy in copies:
+    rows = D // 2
+    spans = [(at * rows, rows) for at in range(3 * INNER // D)] + [(3 * INNER // 2, INNER // 2)]
+    arrivals = []
+    for at, (first, count) in enumerate(spans):
+        span = pl.ds(first, count)
+        arrivals.append(
+            pltpu.make_async_copy(half_hbm.at[span, :], half_ref.at[span, :], in_sems.at[at])
+        )
+    for copy in arrivals:
         copy.start()
-    for copy in copies:
+    leaving = []
+    for at, (first, count) in enumerate(spans):
+        arrivals[at].wait()
+        span = slice(first, first + count)
+        wide_ref[span, :] = half_ref[span, :].astype(jnp.float32)
+        place = pl.ds(pl.multiple_of(core * count, count), count)
+        if at < len(spans) - 1:
+            target = grad_qkv_hbm.at[place, pl.ds(at * D, D)]
+        else:
+            target = grad_out_hbm.at[place, :]
+        leaving.append(
+            pltpu.make_async_copy(wide_ref.at[pl.ds(first, count), :], target, out_sems.at[at])
+        )
+        leaving[-1].start()
+    for copy in leaving:
         copy.wait()
 
 
@@ -433,7 +444,7 @@
         out_shape=(
             jax.ShapeDtypeStruct((FEAT, D), jnp.bfloat16),
             jax.ShapeDtypeStruct((HEADS // 2, 2 * FRAMES, 128), jnp.bfloat16),
-            jax.ShapeDtypeStruct((D, 2 * INNER), jnp.bfloat16),
+            jax.ShapeDtypeStruct((D, 4 * INNER), jnp.bfloat16),
         ),
         in_specs=[whole()] * 4,
         out_specs=(whole(),) * 3,
@@ -442,11 +453,12 @@
 
 
 def layer(core, feats, prepared, grads, norm_gain, qkv_weight, out_weight, factor_all):
-    embed, heads, swapped = prepared
+    embed, heads, turned = prepared
     cosine, sine = rotary_table(np.arange(FRAMES))
     later = (
+        feats,
+        turned,
         qkv_weight,
-        swapped,
         jnp.asarray(cosine),
         jnp.asarray(sine),
         heads,
@@ -456,13 +468,16 @@
     return pl.pallas_call(
         lambda *refs: layer_kernel(*refs, factor_all=factor_all),
         out_shape=(
-            jax.ShapeDtypeStruct(feats.shape[:2] + (D,), jnp.bfloat16),
-            jax.ShapeDtypeStruct((2 * INNER, D), jnp.bfloat16),
-            jax.ShapeDtypeStruct((2 * INNER, D), jnp.bfloat16),
+            pltpu.VMEM(feats.shape[:2] + (D,), jnp.bfloat16),
+            pltpu.VMEM((2 * INNER, D), jnp.bfloat16),
+            pltpu.VMEM((2 * INNER, D), jnp.bfloat16),
         ),
-        in_specs=[whole(pltpu.SMEM)] + [whole()] * 3 + [whole(pl.ANY)] * len(later),
+        in_specs=[whole(pltpu.SMEM)] + [whole()] * 2 + [whole(pl.ANY)] * len(later),
         out_specs=(whole(),) * 3,
-        scratch_shapes=[pltpu.VMEM(value.shape, value.dtype) for value in later]
+        scratch_shapes=[
+            pltpu.VMEM((D, INNER) if value is qkv_weight else value.shape, value.dtype)
+            for value in later
+        ]
         + [
             pltpu.VMEM((FRAMES, INNER), jnp.bfloat16),
             pltpu.VMEM((FRAMES, 3 * INNER), jnp.bfloat16),
@@ -470,7 +485,7 @@
             pltpu.SemaphoreType.DMA((len(later),)),
         ],
         name="layer",
-    )(core, feats, embed, norm_gain.reshape(1, D), *later)
+    )(core, embed, norm_gain.reshape(1, D), *later)
 
 
 def unpack(core, half, filled=()):
@@ -480,13 +495,14 @@
             jax.ShapeDtypeStruct((D, 3 * INNER), jnp.float32),
             jax.ShapeDtypeStruct((INNER, D), jnp.float32),
         ),
-        in_specs=[whole(pltpu.SMEM), whole()] + [whole(pl.ANY)] * len(filled),
+        in_specs=[whole(pltpu.SMEM)] + [whole(pl.ANY)] * (1 + len(filled)),
         out_specs=(whole(pl.ANY),) * 2,
         input_output_aliases={2 + at: at for at in range(len(filled))},
         scratch_shapes=[
-            pltpu.VMEM((D // 2, 3 * INNER), jnp.float32),
-            pltpu.VMEM((INNER // 2, D), jnp.float32),
-            pltpu.SemaphoreType.DMA((2,)),
+            pltpu.VMEM(half.shape, half.dtype),
+            pltpu.VMEM(half.shape, jnp.float32),
+            pltpu.SemaphoreType.DMA((3 * INNER // D + 1,)),
+            pltpu.SemaphoreType.DMA((3 * INNER // D + 1,)),
         ],
         name="unpack",
     )(core, half, *filled)
@@ -530,6 +546,7 @@
     normed = spectrum(band_at, band_widths, audio_clips, rim, band_gain)
     feats = exchange(normed, TIME)
     factor_all = 1.0 / math.sqrt(BANDS * CLIPS * FRAMES)
+    feats = pltpu.with_memory_space_constraint(feats, pltpu.VMEM)
     core = lax.axis_index("core").reshape(1)
     prepared = prepare(weight, grads, qkv_weight, out_weight)
     attended, keep, send = layer(
@@ -545,6 +562,7 @@
     attended_out = both[:, :frame_block].reshape(own_bands, CLIPS, frame_block, D)
     partial = gather(gather(reduced(both[:, frame_block:]), TIME), "x")
     other = lax.ppermute(partial, "core", swap)
+    other = pltpu.with_memory_space_constraint(other, pltpu.VMEM)
     filled = unpack(core, partial)
     grad_qkv, grad_out = unpack(1 - core, other, filled)
     return (attended_out, grad_qkv, grad_out)

time: 162 us -> 157 us (0.969)
  Pallas kernels: 24.6 us -> 22.9 us
    pallas_call x1, Pallas kernels: 8.54 us -> 6.83 us  [layer(): pl.pallas_call(lambda *refs: layer_kernel(*refs, factor_all=factor_all),...]
  transfers between devices with their start and end apart: 5 -> 5, of which waited for: 3 -> 3; matrix products, arithmetic and copies ran while one was open for 1% -> 2% of each run, Pallas kernels for 7% -> 8%
where the time goes in v6:
time: 157 us
  blocking collectives  63.2 us (40%)
  starting transfers between devices  41.9 us (27%)
  waiting for transfers between devices  23.3 us (15%)
  Pallas kernels  22.9 us (15%)
  local copies, waits for them, and re-layouts  3.25 us (2%)
    all_to_all x4, blocking collectives, exchange(): return lax.all_to_all(blocks, axis, split_axis=0, concat_axis=0, tiled=True)  63.2 us
    all_to_all x2, starting transfers between devices, exchange(): return lax.all_to_all(blocks, axis, split_axis=0, concat_axis=0, tiled=True)  29.3 us
    ppermute x1, waiting for transfers between devices, staged(): lax.ppermute(audio_clips, TIME, [(source, source - 1) for source in range...  14.7 us
    pallas_call x1, Pallas kernels, layer(): pl.pallas_call(lambda *refs: layer_kernel(*refs, factor_all=factor_all),...  6.83 us
    all_to_all x2, waiting for transfers between devices, exchange(): return lax.all_to_all(blocks, axis, split_axis=0, concat_axis=0, tiled=True)  6.72 us
    pallas_call x1, Pallas kernels, spectrum(): pl.pallas_call(spectrum_kernel, out_shape=jax.ShapeDtypeStruct((own_bands...  6.23 us
    ppermute x1, starting transfers between devices, staged(): other = lax.ppermute(partial, 'core', swap)  6.13 us
    ppermute x1, starting transfers between devices, staged(): lax.ppermute(send, 'core', swap).astype(jnp.float32)  5.12 us
  transfers between devices with their start and end apart: 5, of which 3 were waited for; matrix products, arithmetic and copies ran while one was open for 2% of the time, Pallas kernels for 8%

profile of v6, /device:TPU:1, one launch (start us, length us, event | category | flops | bytes accessed | tf_op | source)
XLA Modules:
  0.0 156.8 jit_solution(15903189567372156570)
XLA Ops:
  0.6 0.0 copy-start.1
  0.6 1.8 %assemble.1 = bf16[64,3,4,384]{3,2,1,0:T(4,128)(2,1)} custom-call(bf16[64,4,384]{2,1,0:T(4,128)(2,1)} %bitcast.14, bf16[8,8,384]{2,1,0:T(8,128)(2,1)} %weight_ref.1), custom_call_target="tpu_custom_call" | custom-call | tf_op jit(solution)/shard_map/assemble/pallas_call | solution.py:430
  2.5 0.0 copy-start.3
  2.5 17.3 %all-to-all-start = ((bf16[192,4,384]{2,1,0:T(4,128)(2,1)}), bf16[192,4,384]{2,1,0:T(4,128)(2,1)S(1)}, u32[]{:S(2)}, u32[]{:S(2)}) async-start(bf16[192,4,384]{2,1,0:T(4,128)(2,1)} %bitcast.13), calls=%async_computation | async-start | bytes 1179648 | tf_op jit(solution)/shard_map/all_to_all | solution.py:512
  19.8 0.0 copy-done.1
  19.8 1.3 collective-permute-start
  21.1 14.7 %collective-permute-done.rim_ref = f32[8,2,1764]{2,1,0:T(2,128)S(1)} collective-permute-done((f32[8,2,1764]{2,1,0:T(2,128)S(1)}, f32[8,2,1764]{2,1,0:T(2,128)S(1)}, u32[]{:S(2)}, u32[]{:S(2)}) %collective-permute-start) | collective-permute-done | bytes 112928 | tf_op jit(solution)/shard_map/ppermute | solution.py:538
  35.8 0.0 copy-start.2
  35.8 0.6 copy-done.2
  36.4 6.2 %spectrum.1 = bf16[64,4,512]{2,1,0:T(4,128)(2,1)} custom-call(s32[1]{0:T(128)} %bitcast.4.place_ref, s32[64]{0:T(128)} %widths_ref.1, f32[8,2,1764]{2,1,0:T(2,128)} %audio_ref.1, f32[8,2,1764]{2,1,0:T(2,128)} %copy-done.2, f32[8,512]{1,0:T(8,128)} %gain_ref.1, f32[1,2048]{1,0:T(1,128)} %constant.26.clone.taper_ref, f32[16,256]{1,0:T(8,128)} %constant.27.clone.twiddle_ref, ...), custom_call_target="tpu_custom_call" | custom-call | tf_op jit(solution)/shard_map/spectrum/pallas_call | solution.py:402
  42.6 0.0 all-to-all-done
  42.6 12.1 %all-to-all-start.1 = ((bf16[64,4,512]{2,1,0:T(4,128)(2,1)}), bf16[64,4,512]{2,1,0:T(4,128)(2,1)S(1)}, u32[]{:S(2)}, u32[]{:S(2)}) async-start(bf16[64,4,512]{2,1,0:T(4,128)(2,1)} %spectrum.1), calls=%async_computation.1 | async-start | bytes 524288 | tf_op jit(solution)/shard_map/all_to_all | solution.py:512
  54.7 0.0 copy-done.3
  54.7 0.6 reshape.46.refs_2_
  55.3 0.1 slice.17
  55.4 0.1 slice.16
  55.5 0.7 reshape_squeeze.3.grads_ref.refs_10_
  56.3 0.8 reshape.45.weight_ref
  57.1 3.6 %prepare.1 = (bf16[512,384]{1,0:T(8,128)(2,1)}, bf16[4,512,128]{2,1,0:T(8,128)(2,1)}, bf16[384,2048]{1,0:T(8,128)(2,1)}) custom-call(bf16[512,384]{1,0:T(8,128)(2,1)} %reshape.45.weight_ref, bf16[256,384]{1,0:T(8,128)(2,1)} %reshape_squeeze.3.grads_ref.refs_10_, bf16[384,1536]{1,0:T(8,128)(2,1)} %refs_5_.1, bf16[512,384]{1,0:T(8,128)(2,1)} %refs_9_.1), custom_call_target="tpu_custom_call" | custom-call | tf_op jit(solution)/shard_map/prepare/pallas_call | solution.py:442
  60.7 6.7 %all-to-all-done.1.refs_3_ = bf16[64,4,512]{2,1,0:T(4,128)(2,1)S(1)} async-done(((bf16[64,4,512]{2,1,0:T(4,128)(2,1)}), bf16[64,4,512]{2,1,0:T(4,128)(2,1)S(1)}, u32[]{:S(2)}, u32[]{:S(2)}) %all-to-all-start.1) | async-done | bytes 262176 | tf_op jit(solution)/shard_map/all_to_all | solution.py:512
  67.4 6.8 %layer.1 = (bf16[64,4,384]{2,1,0:T(4,128)(2,1)S(1)}, bf16[1024,384]{1,0:T(8,128)(2,1)S(1)}, bf16[1024,384]{1,0:T(8,128)(2,1)S(1)}) custom-call(s32[1]{0:T(128)} %bitcast.refs_0_.core_ref, bf16[512,384]{1,0:T(8,128)(2,1)} %get-tuple-element.13.refs_1_, f32[1,384]{1,0:T(1,128)} %reshape.46.refs_2_, bf16[64,4,512]{2,1,0:T(4,128)(2,1)S(1)} %all-to-all-done.1.refs_3_, ...), custom_call_target="tpu_custom_call" | custom-call | tf_op jit(solution)/shard_map/layer/pallas_call | solution.py:468
  74.2 5.1 %collective-permute-start.1 = (bf16[1024,384]{1,0:T(8,128)(2,1)S(1)}, bf16[1024,384]{1,0:T(8,128)(2,1)S(1)}, u32[]{:S(2)}, u32[]{:S(2)}) collective-permute-start(bf16[1024,384]{1,0:T(8,128)(2,1)S(1)} %get-tuple-element.18), channel_id=1, source_target_pairs={{0,1},{1,0},{2,3},{3,2},{4,5},{5,4},{6,7},{7,6},{8,9},{9,8},{10,11... | collective-permute-start | bytes 2359304 | tf_op jit(solution)/shard_map/ppermute | solution.py:556
  79.3 1.9 %collective-permute-done.1 = bf16[1024,384]{1,0:T(8,128)(2,1)S(1)} collective-permute-done((bf16[1024,384]{1,0:T(8,128)(2,1)S(1)}, bf16[1024,384]{1,0:T(8,128)(2,1)S(1)}, u32[]{:S(2)}, u32[]{:S(2)}) %collective-permute-start.1) | collective-permute-done | bytes 786464 | tf_op jit(solution)/shard_map/ppermute | solution.py:556
  81.2 0.2 add_convert_fusion
  81.4 15.4 %all_to_all.30 = bf16[4,256,384]{2,1,0:T(8,128)(2,1)S(1)} all-to-all(bf16[4,256,384]{2,1,0:T(8,128)(2,1)S(1)} %bitcast.10), channel_id=1, replica_groups=mesh['z'=8,'y'=8,'x'=4,'core'=2] {'x'}, dimensions={0} | all-to-all | bytes 1572864 | tf_op jit(solution)/shard_map/all_to_all | solution.py:512
  96.8 0.2 reduce_sum.24
  97.0 0.1 reshape.49
  97.1 0.2 pad_maximum_fusion
  97.3 17.9 %all_to_all.31 = bf16[64,8,384]{2,1,0:T(8,128)(2,1)S(1)} all-to-all(bf16[64,8,384]{2,1,0:T(8,128)(2,1)S(1)} %pad_maximum_fusion), channel_id=1, replica_groups=mesh['z'=8,'y'=8,'x'=4,'core'=2] {'z','y'}, dimensions={0} | all-to-all | bytes 786432 | tf_op jit(solution)/shard_map/all_to_all | solution.py:512
  115.2 0.8 slice_reduce_fusion
  116.0 0.1 broadcast_in_dim.6
  116.0 18.5 %all_to_all.32 = bf16[64,4,384]{2,1,0:T(4,128)(2,1)S(1)} all-to-all(bf16[64,4,384]{2,1,0:T(4,128)(2,1)S(1)} %broadcast_in_dim.6), channel_id=1, replica_groups=mesh['z'=8,'y'=8,'x'=4,'core'=2] {'z','y'}, dimensions={0} | all-to-all | bytes 393216 | tf_op jit(solution)/shard_map/all_to_all | solution.py:512
  134.5 0.1 broadcast_in_dim.14
  134.6 0.1 broadcast_in_dim.15
  134.7 11.4 %all_to_all.33 = bf16[4,256,384]{2,1,0:T(8,128)(2,1)S(1)} all-to-all(bf16[4,256,384]{2,1,0:T(8,128)(2,1)S(1)} %broadcast_in_dim.15), channel_id=1, replica_groups=mesh['z'=8,'y'=8,'x'=4,'core'=2] {'x'}, dimensions={0} | all-to-all | bytes 1572864 | tf_op jit(solution)/shard_map/all_to_all | solution.py:512
  146.1 0.0 copy-start
  146.1 6.1 %collective-permute-start.2 = (bf16[1024,384]{1,0:T(8,128)(2,1)S(1)}, bf16[1024,384]{1,0:T(8,128)(2,1)S(1)}, u32[]{:S(2)}, u32[]{:S(2)}) collective-permute-start(bf16[1024,384]{1,0:T(8,128)(2,1)S(1)} %bitcast.8), channel_id=1, source_target_pairs={{0,1},{1,0},{2,3},{3,2},{4,5},{5,4},{6,7},{7,6},{8,9},{9,8},{10,11... | collective-permute-start | bytes 2359304 | tf_op jit(solution)/shard_map/ppermute | solution.py:564
  152.2 0.0 copy-done
  152.2 2.2 %unpack.2 = (f32[384,1536]{1,0:T(8,128)}, f32[512,384]{1,0:T(8,128)}) custom-call(s32[1]{0:T(128)} %bitcast.refs_0_.core_ref, bf16[1024,384]{1,0:T(8,128)(2,1)} %bitcast.9), custom_call_target="tpu_custom_call" | custom-call | tf_op jit(solution)/shard_map/unpack/pallas_call | solution.py:492
  154.4 0.0 collective-permute-done.2.half_hbm
  154.4 2.3 %unpack.3 = (f32[384,1536]{1,0:T(8,128)}, f32[512,384]{1,0:T(8,128)}) custom-call(s32[1]{0:T(128)S(6)} %sub.3.core_ref, bf16[1024,384]{1,0:T(8,128)(2,1)S(1)} %collective-permute-done.2.half_hbm, f32[384,1536]{1,0:T(8,128)} %get-tuple-element.19.refs_0_, f32[512,384]{1,0:T(8,128)} %get-tuple-element.20.refs_1_), custom_call_target="tpu_custom_call", output_to_operand_aliasing={{0}: (2, {}), {1}: (3, {})} | custom-call | tf_op jit(solution)/shard_map/unpack/pallas_call | solution.py:492
Async XLA Ops:
  0.6 19.1 %copy-start.1 = (f32[8,2,1764]{2,1,0:T(2,128)S(1)}, f32[8,2,1764]{2,1,0:T(2,128)}, u32[]{:S(2)}) copy-start(f32[8,2,1764]{2,1,0:T(2,128)} %audio_ref.1) | copy-start | bytes 338692
  2.5 52.2 %copy-start.3 = (f32[384]{0:T(512)S(1)}, f32[384]{0:T(512)}, u32[]{:S(2)}) copy-start(f32[384]{0:T(512)} %param.17) | copy-start | bytes 4612
  2.5 40.1 %all-to-all-start = ((bf16[192,4,384]{2,1,0:T(4,128)(2,1)}), bf16[192,4,384]{2,1,0:T(4,128)(2,1)S(1)}, u32[]{:S(2)}, u32[]{:S(2)}) async-start(bf16[192,4,384]{2,1,0:T(4,128)(2,1)} %bitcast.13), calls=%async_computation | async-start | bytes 1179648 | tf_op jit(solution)/shard_map/all_to_all | solution.py:512
  19.8 16.0 %collective-permute-start = (f32[8,2,1764]{2,1,0:T(2,128)S(1)}, f32[8,2,1764]{2,1,0:T(2,128)S(1)}, u32[]{:S(2)}, u32[]{:S(2)}) collective-permute-start(f32[8,2,1764]{2,1,0:T(2,128)S(1)} %copy-done.1), channel_id=1, source_target_pairs={{8,0},{16,8},{24,16},{32,24},{40,32},{48,40},{56,48},{64,56},{72,6... | collective-permute-start | bytes 338696 | tf_op jit(solution)/shard_map/ppermute | solution.py:538
  35.8 0.6 copy-start.2
  42.6 24.7 %all-to-all-start.1 = ((bf16[64,4,512]{2,1,0:T(4,128)(2,1)}), bf16[64,4,512]{2,1,0:T(4,128)(2,1)S(1)}, u32[]{:S(2)}, u32[]{:S(2)}) async-start(bf16[64,4,512]{2,1,0:T(4,128)(2,1)} %spectrum.1), calls=%async_computation.1 | async-start | bytes 524288 | tf_op jit(solution)/shard_map/all_to_all | solution.py:512
  74.2 7.0 %collective-permute-start.1 = (bf16[1024,384]{1,0:T(8,128)(2,1)S(1)}, bf16[1024,384]{1,0:T(8,128)(2,1)S(1)}, u32[]{:S(2)}, u32[]{:S(2)}) collective-permute-start(bf16[1024,384]{1,0:T(8,128)(2,1)S(1)} %get-tuple-element.18), channel_id=1, source_target_pairs={{0,1},{1,0},{2,3},{3,2},{4,5},{5,4},{6,7},{7,6},{8,9},{9,8},{10,11... | collective-permute-start | bytes 2359304 | tf_op jit(solution)/shard_map/ppermute | solution.py:556
  146.1 6.1 %copy-start = (bf16[4,256,384]{2,1,0:T(8,128)(2,1)}, bf16[4,256,384]{2,1,0:T(8,128)(2,1)S(1)}, u32[]{:S(2)}) copy-start(bf16[4,256,384]{2,1,0:T(8,128)(2,1)S(1)} %all_to_all.33) | copy-start | bytes 2359300
  146.1 8.3 %collective-permute-start.2 = (bf16[1024,384]{1,0:T(8,128)(2,1)S(1)}, bf16[1024,384]{1,0:T(8,128)(2,1)S(1)}, u32[]{:S(2)}, u32[]{:S(2)}) collective-permute-start(bf16[1024,384]{1,0:T(8,128)(2,1)S(1)} %bitcast.8), channel_id=1, source_target_pairs={{0,1},{1,0},{2,3},{3,2},{4,5},{5,4},{6,7},{7,6},{8,9},{9,8},{10,11... | collective-permute-start | bytes 2359304 | tf_op jit(solution)/shard_map/ppermute | solution.py:564

commit v7 on v6

--- a/solution.py
+++ b/solution.py
@@ -242,7 +242,7 @@
     core_ref,
     embed_ref,
     gain_ref,
-    feats_hbm,
+    feats_ref,
     turned_hbm,
     qkv_hbm,
     cos_hbm,
@@ -253,7 +253,6 @@
     attended_ref,
     keep_ref,
     send_ref,
-    feats_ref,
     turned_ref,
     plain_ref,
     cos_ref,
@@ -269,7 +268,6 @@
     factor_all,
 ):
     pairs = (
-        (feats_hbm, feats_ref),
         (turned_hbm, turned_ref),
         (qkv_hbm.at[:, 2 * INNER :], plain_ref),
         (cos_hbm, cos_ref),
@@ -284,11 +282,10 @@
     ]
     for copy in copies:
         copy.start()
-    copies[0].wait()
     x = dot(feats_ref[...].reshape(FRAMES, FEAT), embed_ref[...]).astype(jnp.bfloat16).astype(jnp.float32)
     scale = lax.rsqrt(jnp.mean(x * x, axis=1, keepdims=True) + 1e-06)
     normed_x = (x * scale * gain_ref[...]).astype(jnp.bfloat16)
-    for copy in copies[1:]:
+    for copy in copies:
         copy.wait()
     factor = 1.0 / math.sqrt(HDIM)
     cosine = cos_ref[...]
@@ -359,22 +356,13 @@
     send_ref[...] = halves[1]
 
 
-def unpack_kernel(core_ref, half_hbm, *refs):
-    grad_qkv_hbm, grad_out_hbm, half_ref, wide_ref, in_sems, out_sems = refs[-6:]
+def unpack_kernel(core_ref, half_ref, *refs):
+    grad_qkv_hbm, grad_out_hbm, wide_ref, out_sems = refs[-4:]
     core = core_ref[0]
     rows = D // 2
     spans = [(at * rows, rows) for at in range(3 * INNER // D)] + [(3 * INNER // 2, INNER // 2)]
-    arrivals = []
-    for at, (first, count) in enumerate(spans):
-        span = pl.ds(first, count)
-        arrivals.append(
-            pltpu.make_async_copy(half_hbm.at[span, :], half_ref.at[span, :], in_sems.at[at])
-        )
-    for copy in arrivals:
-        copy.start()
     leaving = []
     for at, (first, count) in enumerate(spans):
-        arrivals[at].wait()
         span = slice(first, first + count)
         wide_ref[span, :] = half_ref[span, :].astype(jnp.float32)
         place = pl.ds(pl.multiple_of(core * count, count), count)
@@ -388,6 +376,10 @@
         leaving[-1].start()
     for copy in leaving:
         copy.wait()
+
+
+def in_vmem(values):
+    return pltpu.with_memory_space_constraint(values, pltpu.VMEM)
 
 
 def whole(memory_space=pltpu.VMEM):
@@ -442,7 +434,7 @@
     return pl.pallas_call(
         prepare_kernel,
         out_shape=(
-            jax.ShapeDtypeStruct((FEAT, D), jnp.bfloat16),
+            pltpu.VMEM((FEAT, D), jnp.bfloat16),
             jax.ShapeDtypeStruct((HEADS // 2, 2 * FRAMES, 128), jnp.bfloat16),
             jax.ShapeDtypeStruct((D, 4 * INNER), jnp.bfloat16),
         ),
@@ -456,7 +448,6 @@
     embed, heads, turned = prepared
     cosine, sine = rotary_table(np.arange(FRAMES))
     later = (
-        feats,
         turned,
         qkv_weight,
         jnp.asarray(cosine),
@@ -472,7 +463,7 @@
             pltpu.VMEM((2 * INNER, D), jnp.bfloat16),
             pltpu.VMEM((2 * INNER, D), jnp.bfloat16),
         ),
-        in_specs=[whole(pltpu.SMEM)] + [whole()] * 2 + [whole(pl.ANY)] * len(later),
+        in_specs=[whole(pltpu.SMEM)] + [whole()] * 3 + [whole(pl.ANY)] * len(later),
         out_specs=(whole(),) * 3,
         scratch_shapes=[
             pltpu.VMEM((D, INNER) if value is qkv_weight else value.shape, value.dtype)
@@ -485,7 +476,7 @@
             pltpu.SemaphoreType.DMA((len(later),)),
         ],
         name="layer",
-    )(core, embed, norm_gain.reshape(1, D), *later)
+    )(core, in_vmem(embed), norm_gain.reshape(1, D), in_vmem(feats), *later)
 
 
 def unpack(core, half, filled=()):
@@ -495,17 +486,15 @@
             jax.ShapeDtypeStruct((D, 3 * INNER), jnp.float32),
             jax.ShapeDtypeStruct((INNER, D), jnp.float32),
         ),
-        in_specs=[whole(pltpu.SMEM)] + [whole(pl.ANY)] * (1 + len(filled)),
+        in_specs=[whole(pltpu.SMEM), whole()] + [whole(pl.ANY)] * len(filled),
         out_specs=(whole(pl.ANY),) * 2,
         input_output_aliases={2 + at: at for at in range(len(filled))},
         scratch_shapes=[
-            pltpu.VMEM(half.shape, half.dtype),
             pltpu.VMEM(half.shape, jnp.float32),
-            pltpu.SemaphoreType.DMA((3 * INNER // D + 1,)),
             pltpu.SemaphoreType.DMA((3 * INNER // D + 1,)),
         ],
         name="unpack",
-    )(core, half, *filled)
+    )(core, in_vmem(half), *filled)
 
 
 def exchange(blocks, axis):
@@ -546,7 +535,6 @@
     normed = spectrum(band_at, band_widths, audio_clips, rim, band_gain)
     feats = exchange(normed, TIME)
     factor_all = 1.0 / math.sqrt(BANDS * CLIPS * FRAMES)
-    feats = pltpu.with_memory_space_constraint(feats, pltpu.VMEM)
     core = lax.axis_index("core").reshape(1)
     prepared = prepare(weight, grads, qkv_weight, out_weight)
     attended, keep, send = layer(
@@ -562,7 +550,6 @@
     attended_out = both[:, :frame_block].reshape(own_bands, CLIPS, frame_block, D)
     partial = gather(gather(reduced(both[:, frame_block:]), TIME), "x")
     other = lax.ppermute(partial, "core", swap)
-    other = pltpu.with_memory_space_constraint(other, pltpu.VMEM)
     filled = unpack(core, partial)
     grad_qkv, grad_out = unpack(1 - core, other, filled)
     return (attended_out, grad_qkv, grad_out)

time: 157 us -> 156 us (level)
  Pallas kernels: 22.9 us -> 20.6 us
    pallas_call x2, Pallas kernels: 4.41 us -> 2.39 us  [unpack(): pl.pallas_call(unpack_kernel, out_shape=(jax.ShapeDtypeStruct((D, 3 * INN...]
  transfers between devices with their start and end apart: 5 -> 5, of which waited for: 3 -> 4; matrix products, arithmetic and copies ran while one was open for 2% -> 2% of each run, Pallas kernels for 8% -> 7%
where the time goes in v7:
time: 156 us; the launch traced here: 155 us
  blocking collectives  62.8 us (40%)
  starting transfers between devices  42.2 us (27%)
  waiting for transfers between devices  24 us (15%)
  Pallas kernels  20.6 us (13%)
  local copies, waits for them, and re-layouts  3.21 us (2%)
    all_to_all x4, blocking collectives, exchange(): return lax.all_to_all(blocks, axis, split_axis=0, concat_axis=0, tiled=True)  62.8 us
    all_to_all x2, starting transfers between devices, exchange(): return lax.all_to_all(blocks, axis, split_axis=0, concat_axis=0, tiled=True)  29.3 us
    ppermute x1, waiting for transfers between devices, staged(): lax.ppermute(audio_clips, TIME, [(source, source - 1) for source in range...  14.7 us
    all_to_all x2, waiting for transfers between devices, exchange(): return lax.all_to_all(blocks, axis, split_axis=0, concat_axis=0, tiled=True)  6.74 us
    pallas_call x1, Pallas kernels, layer(): pl.pallas_call(lambda *refs: layer_kernel(*refs, factor_all=factor_all),...  6.59 us
    ppermute x1, starting transfers between devices, staged(): other = lax.ppermute(partial, 'core', swap)  6.5 us
    pallas_call x1, Pallas kernels, spectrum(): pl.pallas_call(spectrum_kernel, out_shape=jax.ShapeDtypeStruct((own_bands...  6.22 us
    ppermute x1, starting transfers between devices, staged(): lax.ppermute(send, 'core', swap).astype(jnp.float32)  5.12 us
  transfers between devices with their start and end apart: 5, of which 4 were waited for; matrix products, arithmetic and copies ran while one was open for 2% of the time, Pallas kernels for 7%

profile of v7, /device:TPU:1, one launch (start us, length us, event | category | flops | bytes accessed | tf_op | source)
XLA Modules:
  0.0 155.2 jit_solution(7375427621057364571)
XLA Ops:
  0.6 0.0 copy-start
  0.6 1.8 %assemble.1 = bf16[64,3,4,384]{3,2,1,0:T(4,128)(2,1)} custom-call(bf16[64,4,384]{2,1,0:T(4,128)(2,1)} %bitcast.14, bf16[8,8,384]{2,1,0:T(8,128)(2,1)} %weight_ref.1), custom_call_target="tpu_custom_call" | custom-call | tf_op jit(solution)/shard_map/assemble/pallas_call | solution.py:422
  2.5 0.0 copy-start.2
  2.5 17.3 %all-to-all-start = ((bf16[192,4,384]{2,1,0:T(4,128)(2,1)}), bf16[192,4,384]{2,1,0:T(4,128)(2,1)S(1)}, u32[]{:S(2)}, u32[]{:S(2)}) async-start(bf16[192,4,384]{2,1,0:T(4,128)(2,1)} %bitcast.13), calls=%async_computation | async-start | bytes 1179648 | tf_op jit(solution)/shard_map/all_to_all | solution.py:501
  19.8 0.0 copy-done
  19.8 1.3 collective-permute-start
  21.1 14.7 %collective-permute-done.rim_ref = f32[8,2,1764]{2,1,0:T(2,128)S(1)} collective-permute-done((f32[8,2,1764]{2,1,0:T(2,128)S(1)}, f32[8,2,1764]{2,1,0:T(2,128)S(1)}, u32[]{:S(2)}, u32[]{:S(2)}) %collective-permute-start) | collective-permute-done | bytes 112928 | tf_op jit(solution)/shard_map/ppermute | solution.py:527
  35.8 0.0 copy-start.1
  35.8 0.6 copy-done.1
  36.4 6.2 %spectrum.1 = bf16[64,4,512]{2,1,0:T(4,128)(2,1)} custom-call(s32[1]{0:T(128)} %bitcast.4.place_ref, s32[64]{0:T(128)} %widths_ref.1, f32[8,2,1764]{2,1,0:T(2,128)} %audio_ref.1, f32[8,2,1764]{2,1,0:T(2,128)} %copy-done.1, f32[8,512]{1,0:T(8,128)} %gain_ref.1, f32[1,2048]{1,0:T(1,128)} %constant.26.clone.taper_ref, f32[16,256]{1,0:T(8,128)} %constant.27.clone.twiddle_ref, ...), custom_call_target="tpu_custom_call" | custom-call | tf_op jit(solution)/shard_map/spectrum/pallas_call | solution.py:394
  42.6 0.0 all-to-all-done
  42.6 12.1 %all-to-all-start.1 = ((bf16[64,4,512]{2,1,0:T(4,128)(2,1)}), bf16[64,4,512]{2,1,0:T(4,128)(2,1)S(1)}, u32[]{:S(2)}, u32[]{:S(2)}) async-start(bf16[64,4,512]{2,1,0:T(4,128)(2,1)} %spectrum.1), calls=%async_computation.1 | async-start | bytes 524288 | tf_op jit(solution)/shard_map/all_to_all | solution.py:501
  54.7 0.0 copy-done.2
  54.7 0.6 reshape.46.refs_2_
  55.3 0.1 slice.17
  55.4 0.1 slice.16
  55.5 0.7 reshape_squeeze.3.grads_ref.refs_10_
  56.2 0.8 reshape.45.weight_ref
  57.1 3.6 %prepare.1 = (bf16[512,384]{1,0:T(8,128)(2,1)S(1)}, bf16[4,512,128]{2,1,0:T(8,128)(2,1)}, bf16[384,2048]{1,0:T(8,128)(2,1)}) custom-call(bf16[512,384]{1,0:T(8,128)(2,1)} %reshape.45.weight_ref, bf16[256,384]{1,0:T(8,128)(2,1)} %reshape_squeeze.3.grads_ref.refs_10_, bf16[384,1536]{1,0:T(8,128)(2,1)} %refs_5_.1, bf16[512,384]{1,0:T(8,128)(2,1)} %refs_9_.1), custom_call_target="tpu_custom_call" | custom-call | tf_op jit(solution)/shard_map/prepare/pallas_call | solution.py:434
  60.6 6.7 %all-to-all-done.1.refs_3_ = bf16[64,4,512]{2,1,0:T(4,128)(2,1)S(1)} async-done(((bf16[64,4,512]{2,1,0:T(4,128)(2,1)}), bf16[64,4,512]{2,1,0:T(4,128)(2,1)S(1)}, u32[]{:S(2)}, u32[]{:S(2)}) %all-to-all-start.1) | async-done | bytes 262176 | tf_op jit(solution)/shard_map/all_to_all | solution.py:501
  67.4 6.6 %layer.1 = (bf16[64,4,384]{2,1,0:T(4,128)(2,1)S(1)}, bf16[1024,384]{1,0:T(8,128)(2,1)S(1)}, bf16[1024,384]{1,0:T(8,128)(2,1)S(1)}) custom-call(s32[1]{0:T(128)} %bitcast.refs_0_.core_ref, bf16[512,384]{1,0:T(8,128)(2,1)S(1)} %get-tuple-element.13.refs_1_, f32[1,384]{1,0:T(1,128)} %reshape.46.refs_2_, bf16[64,4,512]{2,1,0:T(4,128)(2,1)S(1)} %all-to-all-done.1.refs_3_, ...), custom_call_target="tpu_custom_call" | custom-call | tf_op jit(solution)/shard_map/layer/pallas_call | solution.py:459
  74.0 5.1 %collective-permute-start.1 = (bf16[1024,384]{1,0:T(8,128)(2,1)S(1)}, bf16[1024,384]{1,0:T(8,128)(2,1)S(1)}, u32[]{:S(2)}, u32[]{:S(2)}) collective-permute-start(bf16[1024,384]{1,0:T(8,128)(2,1)S(1)} %get-tuple-element.18), channel_id=1, source_target_pairs={{0,1},{1,0},{2,3},{3,2},{4,5},{5,4},{6,7},{7,6},{8,9},{9,8},{10,11... | collective-permute-start | bytes 2359304 | tf_op jit(solution)/shard_map/ppermute | solution.py:544
  79.1 1.9 %collective-permute-done.1 = bf16[1024,384]{1,0:T(8,128)(2,1)S(1)} collective-permute-done((bf16[1024,384]{1,0:T(8,128)(2,1)S(1)}, bf16[1024,384]{1,0:T(8,128)(2,1)S(1)}, u32[]{:S(2)}, u32[]{:S(2)}) %collective-permute-start.1) | collective-permute-done | bytes 786464 | tf_op jit(solution)/shard_map/ppermute | solution.py:544
  81.0 0.2 add_convert_fusion
  81.2 15.4 %all_to_all.30 = bf16[4,256,384]{2,1,0:T(8,128)(2,1)S(1)} all-to-all(bf16[4,256,384]{2,1,0:T(8,128)(2,1)S(1)} %bitcast.10), channel_id=1, replica_groups=mesh['z'=8,'y'=8,'x'=4,'core'=2] {'x'}, dimensions={0} | all-to-all | bytes 1572864 | tf_op jit(solution)/shard_map/all_to_all | solution.py:501
  96.6 0.2 reduce_sum.24
  96.7 0.1 reshape.49
  96.8 0.2 pad_maximum_fusion
  97.0 17.9 %all_to_all.31 = bf16[64,8,384]{2,1,0:T(8,128)(2,1)S(1)} all-to-all(bf16[64,8,384]{2,1,0:T(8,128)(2,1)S(1)} %pad_maximum_fusion), channel_id=1, replica_groups=mesh['z'=8,'y'=8,'x'=4,'core'=2] {'z','y'}, dimensions={0} | all-to-all | bytes 786432 | tf_op jit(solution)/shard_map/all_to_all | solution.py:501
  114.9 0.8 slice_reduce_fusion
  115.7 0.1 broadcast_in_dim.6
  115.8 18.5 %all_to_all.32 = bf16[64,4,384]{2,1,0:T(4,128)(2,1)S(1)} all-to-all(bf16[64,4,384]{2,1,0:T(4,128)(2,1)S(1)} %broadcast_in_dim.6), channel_id=1, replica_groups=mesh['z'=8,'y'=8,'x'=4,'core'=2] {'z','y'}, dimensions={0} | all-to-all | bytes 393216 | tf_op jit(solution)/shard_map/all_to_all | solution.py:501
  134.3 0.1 broadcast_in_dim.14
  134.3 0.1 broadcast_in_dim.15
  134.4 11.1 %all_to_all.33 = bf16[4,256,384]{2,1,0:T(8,128)(2,1)S(1)} all-to-all(bf16[4,256,384]{2,1,0:T(8,128)(2,1)S(1)} %broadcast_in_dim.15), channel_id=1, replica_groups=mesh['z'=8,'y'=8,'x'=4,'core'=2] {'x'}, dimensions={0} | all-to-all | bytes 1572864 | tf_op jit(solution)/shard_map/all_to_all | solution.py:501
  145.5 6.5 %collective-permute-start.2 = (bf16[1024,384]{1,0:T(8,128)(2,1)S(1)}, bf16[1024,384]{1,0:T(8,128)(2,1)S(1)}, u32[]{:S(2)}, u32[]{:S(2)}) collective-permute-start(bf16[1024,384]{1,0:T(8,128)(2,1)S(1)} %bitcast.8), channel_id=1, source_target_pairs={{0,1},{1,0},{2,3},{3,2},{4,5},{5,4},{6,7},{7,6},{8,9},{9,8},{10,11... | collective-permute-start | bytes 2359304 | tf_op jit(solution)/shard_map/ppermute | solution.py:552
  152.0 1.2 unpack.2
  153.2 0.7 collective-permute-done.2.half_ref
  153.9 1.2 unpack.3
Async XLA Ops:
  0.6 19.1 %copy-start = (f32[8,2,1764]{2,1,0:T(2,128)S(1)}, f32[8,2,1764]{2,1,0:T(2,128)}, u32[]{:S(2)}) copy-start(f32[8,2,1764]{2,1,0:T(2,128)} %audio_ref.1) | copy-start | bytes 338692
  2.5 52.2 %copy-start.2 = (f32[384]{0:T(512)S(1)}, f32[384]{0:T(512)}, u32[]{:S(2)}) copy-start(f32[384]{0:T(512)} %param.17) | copy-start | bytes 4612
  2.5 40.1 %all-to-all-start = ((bf16[192,4,384]{2,1,0:T(4,128)(2,1)}), bf16[192,4,384]{2,1,0:T(4,128)(2,1)S(1)}, u32[]{:S(2)}, u32[]{:S(2)}) async-start(bf16[192,4,384]{2,1,0:T(4,128)(2,1)} %bitcast.13), calls=%async_computation | async-start | bytes 1179648 | tf_op jit(solution)/shard_map/all_to_all | solution.py:501
  19.8 16.0 %collective-permute-start = (f32[8,2,1764]{2,1,0:T(2,128)S(1)}, f32[8,2,1764]{2,1,0:T(2,128)S(1)}, u32[]{:S(2)}, u32[]{:S(2)}) collective-permute-start(f32[8,2,1764]{2,1,0:T(2,128)S(1)} %copy-done), channel_id=1, source_target_pairs={{8,0},{16,8},{24,16},{32,24},{40,32},{48,40},{56,48},{64,56},{72,6... | collective-permute-start | bytes 338696 | tf_op jit(solution)/shard_map/ppermute | solution.py:527
  35.8 0.6 copy-start.1
  42.6 24.7 %all-to-all-start.1 = ((bf16[64,4,512]{2,1,0:T(4,128)(2,1)}), bf16[64,4,512]{2,1,0:T(4,128)(2,1)S(1)}, u32[]{:S(2)}, u32[]{:S(2)}) async-start(bf16[64,4,512]{2,1,0:T(4,128)(2,1)} %spectrum.1), calls=%async_computation.1 | async-start | bytes 524288 | tf_op jit(solution)/shard_map/all_to_all | solution.py:501
  74.0 7.0 %collective-permute-start.1 = (bf16[1024,384]{1,0:T(8,128)(2,1)S(1)}, bf16[1024,384]{1,0:T(8,128)(2,1)S(1)}, u32[]{:S(2)}, u32[]{:S(2)}) collective-permute-start(bf16[1024,384]{1,0:T(8,128)(2,1)S(1)} %get-tuple-element.18), channel_id=1, source_target_pairs={{0,1},{1,0},{2,3},{3,2},{4,5},{5,4},{6,7},{7,6},{8,9},{9,8},{10,11... | collective-permute-start | bytes 2359304 | tf_op jit(solution)/shard_map/ppermute | solution.py:544
  145.5 8.4 %collective-permute-start.2 = (bf16[1024,384]{1,0:T(8,128)(2,1)S(1)}, bf16[1024,384]{1,0:T(8,128)(2,1)S(1)}, u32[]{:S(2)}, u32[]{:S(2)}) collective-permute-start(bf16[1024,384]{1,0:T(8,128)(2,1)S(1)} %bitcast.8), channel_id=1, source_target_pairs={{0,1},{1,0},{2,3},{3,2},{4,5},{5,4},{6,7},{7,6},{8,9},{9,8},{10,11... | collective-permute-start | bytes 2359304 | tf_op jit(solution)/shard_map/ppermute | solution.py:552
